TPU v7x, 32 devices: a whole 2x2x4 slice. The times are simulated.
32 devices in a mesh: dp: 8 (over z, y), fsdp: 4 (over x, core).
Axes of the slice: x: 2, y: 2, z: 4, core: 2. Of those that a mesh axis runs over, the one named last changes fastest.
Arguments:
- tokens: bfloat16 [32768, 768], P(('dp', 'fsdp')), may hold values from -6 to 6
- cotangent: bfloat16 [32768, 768], P(('dp', 'fsdp')), may hold values from -6 to 6
- page_id: int32 [32768], P(('dp', 'fsdp')), may hold values from -1 to 4, as said below
- pos_row: int32 [32768], P(('dp', 'fsdp')), may hold values from 0 to 31, as said below
- pos_col: int32 [32768], P(('dp', 'fsdp')), may hold values from 0 to 31, as said below
- ln1_gain: bfloat16 [768], P('fsdp'), may hold values from 0.5 to 1.5
- ln1_shift: bfloat16 [768], P('fsdp'), may hold values from -3 to 3
- w_qkv: bfloat16 [768, 2304], P('fsdp'), may hold values from -0.21875 to 0.21875
- rel_table: bfloat16 [12, 2, 63], P('fsdp'), may hold values from -4 to 4
- w_out: bfloat16 [768, 768], P('fsdp'), may hold values from -0.625 to 0.625
- scale_attn: bfloat16 [768], P('fsdp'), may hold values from 0.5 to 2
- ln2_gain: bfloat16 [768], P('fsdp'), may hold values from 0.5 to 1.5
- ln2_shift: bfloat16 [768], P('fsdp'), may hold values from -3 to 3
- w_up: bfloat16 [768, 3072], P('fsdp'), may hold values from -0.21875 to 0.21875
- b_up: bfloat16 [3072], P('fsdp'), may hold values from -3 to 3
- w_down: bfloat16 [3072, 768], P('fsdp'), may hold values from -0.109375 to 0.109375
- b_down: bfloat16 [768], P('fsdp'), may hold values from -2 to 2
- scale_mlp: bfloat16 [768], P('fsdp'), may hold values from 0.5 to 2
Outputs:
- layer_out: bfloat16 [32768, 768], P(('dp', 'fsdp'))
- grad_tokens: bfloat16 [32768, 768], P(('dp', 'fsdp'))
- grad_ln1_gain: float32 [768], P('fsdp')
- grad_ln1_shift: float32 [768], P('fsdp')
- grad_w_qkv: float32 [768, 2304], P('fsdp')
- grad_rel_table: float32 [12, 2, 63], P('fsdp')
- grad_w_out: float32 [768, 768], P('fsdp')
- grad_scale_attn: float32 [768], P('fsdp')
- grad_ln2_gain: float32 [768], P('fsdp')
- grad_ln2_shift: float32 [768], P('fsdp')
- grad_w_up: float32 [768, 3072], P('fsdp')
- grad_b_up: float32 [3072], P('fsdp')
- grad_w_down: float32 [3072, 768], P('fsdp')
- grad_b_down: float32 [768], P('fsdp')
- grad_scale_mlp: float32 [768], P('fsdp')
Inputs may be any that keep to these rules, and one draw needn't show every extreme that they name: `page_id`: each device's 1024 slots hold whole pages one after another, square grids of side 14, 24 or 32 in row-major order, numbered 0, 1, 2, ... in order within the device; empty slots follow them. Some device is full in every draw. `pos_row`: row of the patch in its page's grid; 0 on empty slots. `pos_col`: column of the patch in its page's grid; 0 on empty slots.
All inputs are finite; a program needn't handle non-finite values.
Results may differ from a plain program's by a relative error of at most 0.012.
Values may be sent and summed in bfloat16 or wider, within the bound.
A program may use at most 256 MiB of HBM per device.

v0:
```python
import jax
import jax.numpy as jnp
from jax import lax
from jax.sharding import PartitionSpec as P

highest = lax.Precision.HIGHEST


def normalize(rows, gain, shift):
    center = rows - jnp.mean(rows, axis=-1, keepdims=True)
    spread = jnp.mean(center * center, axis=-1, keepdims=True)
    return center * lax.rsqrt(spread + 1e-06) * gain + shift


def key_side(keys, table, rows_pos, cols_pos):
    span = (table.shape[2] + 1) // 2
    grid = jnp.arange(span, dtype=jnp.int32)
    index_row = grid[None, :] - rows_pos[:, None] + span - 1
    index_col = grid[None, :] - cols_pos[:, None] + span - 1
    bias_row = jnp.take(table[:, 0, :], index_row, axis=1)
    bias_col = jnp.take(table[:, 1, :], index_col, axis=1)
    return jnp.concatenate([keys, bias_row, bias_col], axis=2)


def attend(q_aug, k_aug, values, match):
    scores = jnp.einsum("hqa,hka->hqk", q_aug, k_aug, preferred_element_type=jnp.float32)
    scores = jnp.where(match[None], scores, -1e30)
    top = jnp.max(scores, axis=2, keepdims=True)
    expo = jnp.exp(scores - top)
    total = jnp.sum(expo, axis=2, keepdims=True)
    prob = (expo / total).astype(jnp.bfloat16)
    result = jnp.einsum("hqk,hke->hqe", prob, values, preferred_element_type=jnp.float32)
    return (result.astype(jnp.bfloat16), (top + jnp.log(total))[..., 0])


def attend_back(q_aug, k_aug, values, match, lse, d_out):
    size_h = values.shape[2]
    scores = jnp.einsum("hqa,hka->hqk", q_aug, k_aug, preferred_element_type=jnp.float32)
    scores = jnp.where(match[None], scores, -1e30)
    prob = jnp.exp(scores - lse[..., None])
    d_prob = jnp.einsum("hqe,hke->hqk", d_out, values, preferred_element_type=jnp.float32)
    d_scores = prob * (d_prob - jnp.sum(prob * d_prob, axis=2, keepdims=True))
    d_low = d_scores.astype(jnp.bfloat16)
    d_query = jnp.einsum(
        "hqk,hke->hqe", d_low, k_aug[..., :size_h], preferred_element_type=jnp.float32
    )
    d_key = jnp.einsum("hqk,hqa->hka", d_low, q_aug, preferred_element_type=jnp.float32)
    d_value = jnp.einsum(
        "hqk,hqe->hke", prob.astype(jnp.bfloat16), d_out, preferred_element_type=jnp.float32
    )
    return (d_query, d_key, d_value)


def table_grad(part, positions, span):
    grid = jnp.arange(span, dtype=jnp.int32)
    onehot = (positions[:, None] == grid[None, :]).astype(jnp.float32)
    square = jnp.einsum("hka,kb->hab", part, onehot, precision=highest)
    offsets = jnp.arange(2 * span - 1, dtype=jnp.int32)
    diagonal = (
        (grid[:, None] - grid[None, :] + span - 1)[:, :, None] == offsets[None, None, :]
    ).astype(jnp.float32)
    return jnp.einsum("hab,abd->hd", square, diagonal, precision=highest)


def local(
    tokens,
    cotangent,
    page_id,
    pos_row,
    pos_col,
    ln1_gain,
    ln1_shift,
    w_qkv,
    rel_table,
    w_out,
    scale_attn,
    ln2_gain,
    ln2_shift,
    w_up,
    b_up,
    w_down,
    b_down,
    scale_mlp,
):
    f32 = jnp.float32
    bf16 = jnp.bfloat16
    full = (
        lax.all_gather(ln1_gain, "fsdp", axis=0, tiled=True),
        lax.all_gather(ln1_shift, "fsdp", axis=0, tiled=True),
        lax.all_gather(w_qkv, "fsdp", axis=0, tiled=True),
        lax.all_gather(rel_table, "fsdp", axis=0, tiled=True),
        lax.all_gather(w_out, "fsdp", axis=0, tiled=True),
        lax.all_gather(scale_attn, "fsdp", axis=0, tiled=True),
        lax.all_gather(ln2_gain, "fsdp", axis=0, tiled=True),
        lax.all_gather(ln2_shift, "fsdp", axis=0, tiled=True),
        lax.all_gather(w_up, "fsdp", axis=0, tiled=True),
        lax.all_gather(b_up, "fsdp", axis=0, tiled=True),
        lax.all_gather(w_down, "fsdp", axis=0, tiled=True),
        lax.all_gather(b_down, "fsdp", axis=0, tiled=True),
        lax.all_gather(scale_mlp, "fsdp", axis=0, tiled=True),
    )
    g_one, s_one, wqkv, table, wout, scale_a, g_two, s_two, wup, bup, wdown, bdown, scale_m = full
    rows = tokens.astype(f32)
    count = rows.shape[0]
    width_d = rows.shape[1]
    heads = table.shape[0]
    size_h = width_d // heads
    span = (table.shape[2] + 1) // 2
    aug = size_h + 2 * span
    block = min(512, count)
    nblocks = count // block
    gain_one = g_one.astype(f32)
    shift_one = s_one.astype(f32)
    norm_one = normalize(rows, gain_one, shift_one).astype(bf16)
    qkv = jnp.dot(norm_one, wqkv, preferred_element_type=f32).astype(bf16)
    split = jnp.transpose(qkv.reshape(count, 3, heads, size_h), (1, 2, 0, 3))
    queries, keys, values = (split[0], split[1], split[2])
    grid = jnp.arange(span, dtype=jnp.int32)
    row_hot = jnp.broadcast_to(
        (pos_row[:, None] == grid[None, :]).astype(bf16)[None], (heads, count, span)
    )
    col_hot = jnp.broadcast_to(
        (pos_col[:, None] == grid[None, :]).astype(bf16)[None], (heads, count, span)
    )
    q_aug = jnp.concatenate([queries * 0.125, row_hot, col_hot], axis=2)
    k_aug = key_side(keys, table, pos_row, pos_col)
    match = page_id[:, None] == page_id[None, :]
    q_blocks = jnp.transpose(q_aug.reshape(heads, nblocks, block, aug), (1, 0, 2, 3))
    match_blocks = match.reshape(nblocks, block, count)
    att_blocks, lse_blocks = lax.map(
        lambda item: attend(item[0], k_aug, values, item[1]), (q_blocks, match_blocks)
    )
    att = jnp.transpose(att_blocks, (0, 2, 1, 3)).reshape(count, width_d)
    proj = jnp.dot(att, wout, preferred_element_type=f32)
    mid = rows + scale_a.astype(f32) * proj
    gain_two = g_two.astype(f32)
    shift_two = s_two.astype(f32)
    norm_two = normalize(mid, gain_two, shift_two).astype(bf16)
    upper = jnp.dot(norm_two, wup, preferred_element_type=f32) + bup.astype(f32)
    act = jax.nn.gelu(upper, approximate=True).astype(bf16)
    down = jnp.dot(act, wdown, preferred_element_type=f32) + bdown.astype(f32)
    layer_out = (mid + scale_m.astype(f32) * down).astype(bf16)
    again = (
        lax.all_gather(ln1_gain, "fsdp", axis=0, tiled=True),
        lax.all_gather(ln1_shift, "fsdp", axis=0, tiled=True),
        lax.all_gather(w_qkv, "fsdp", axis=0, tiled=True),
        lax.all_gather(rel_table, "fsdp", axis=0, tiled=True),
        lax.all_gather(w_out, "fsdp", axis=0, tiled=True),
        lax.all_gather(scale_attn, "fsdp", axis=0, tiled=True),
        lax.all_gather(ln2_gain, "fsdp", axis=0, tiled=True),
        lax.all_gather(ln2_shift, "fsdp", axis=0, tiled=True),
        lax.all_gather(w_up, "fsdp", axis=0, tiled=True),
        lax.all_gather(b_up, "fsdp", axis=0, tiled=True),
        lax.all_gather(w_down, "fsdp", axis=0, tiled=True),
        lax.all_gather(b_down, "fsdp", axis=0, tiled=True),
        lax.all_gather(scale_mlp, "fsdp", axis=0, tiled=True),
    )
    g_one, s_one, wqkv, table, wout, scale_a, g_two, s_two, wup, bup, wdown, bdown, scale_m = again
    grad = cotangent.astype(f32) * (page_id >= 0).astype(f32)[:, None]
    d_scale_m = jnp.sum(grad * down, axis=0)
    d_down = (grad * scale_m.astype(f32)).astype(bf16)
    d_bdown = jnp.sum(d_down.astype(f32), axis=0)
    d_wdown = jnp.einsum("nf,nd->fd", act, d_down, preferred_element_type=f32)
    d_act = jnp.einsum("nd,fd->nf", d_down, wdown, preferred_element_type=f32)
    _, gelu_back = jax.vjp(lambda v: jax.nn.gelu(v, approximate=True), upper)
    d_upper = gelu_back(d_act)[0].astype(bf16)
    d_bup = jnp.sum(d_upper.astype(f32), axis=0)
    d_wup = jnp.einsum("nd,nf->df", norm_two, d_upper, preferred_element_type=f32)
    d_norm_two = jnp.einsum("nf,df->nd", d_upper, wup, preferred_element_type=f32)
    _, norm_two_back = jax.vjp(normalize, mid, g_two.astype(f32), s_two.astype(f32))
    d_mid_norm, d_gain_two, d_shift_two = norm_two_back(d_norm_two)
    d_mid = grad + d_mid_norm
    d_scale_a = jnp.sum(d_mid * proj, axis=0)
    d_proj = (d_mid * scale_a.astype(f32)).astype(bf16)
    d_wout = jnp.einsum("nd,ne->de", att, d_proj, preferred_element_type=f32)
    d_att = jnp.einsum("ne,de->nd", d_proj, wout, preferred_element_type=f32).astype(bf16)
    d_att_blocks = jnp.transpose(d_att.reshape(nblocks, block, heads, size_h), (0, 2, 1, 3))

    def back_block(carry, item):
        q_part, match_part, lse_part, d_part = item
        d_query, d_key, d_value = attend_back(q_part, k_aug, values, match_part, lse_part, d_part)
        return ((carry[0] + d_key, carry[1] + d_value), d_query)

    start = (jnp.zeros((heads, count, aug), f32), jnp.zeros((heads, count, size_h), f32))
    (d_k_aug, d_values), d_q_blocks = lax.scan(
        back_block, start, (q_blocks, match_blocks, lse_blocks, d_att_blocks)
    )
    d_queries = jnp.transpose(d_q_blocks, (0, 2, 1, 3)).reshape(count, width_d) * 0.125
    d_keys = jnp.transpose(d_k_aug[..., :size_h], (1, 0, 2)).reshape(count, width_d)
    d_vals = jnp.transpose(d_values, (1, 0, 2)).reshape(count, width_d)
    d_table = jnp.stack(
        [
            table_grad(d_k_aug[..., size_h : size_h + span], pos_row, span),
            table_grad(d_k_aug[..., size_h + span :], pos_col, span),
        ],
        axis=1,
    )
    d_qkv = jnp.concatenate([d_queries, d_keys, d_vals], axis=1).astype(bf16)
    d_wqkv = jnp.einsum("nd,nc->dc", norm_one, d_qkv, preferred_element_type=f32)
    d_norm_one = jnp.einsum("nc,dc->nd", d_qkv, wqkv, preferred_element_type=f32)
    _, norm_one_back = jax.vjp(normalize, rows, g_one.astype(f32), s_one.astype(f32))
    d_rows_norm, d_gain_one, d_shift_one = norm_one_back(d_norm_one)
    grad_tokens = (d_mid + d_rows_norm).astype(bf16)
    (
        r_gain_one,
        r_shift_one,
        r_wqkv,
        r_table,
        r_wout,
        r_scale_a,
        r_gain_two,
        r_shift_two,
        r_wup,
        r_bup,
        r_wdown,
        r_bdown,
        r_scale_m,
    ) = (
        lax.psum_scatter(d_gain_one, "fsdp", scatter_dimension=0, tiled=True),
        lax.psum_scatter(d_shift_one, "fsdp", scatter_dimension=0, tiled=True),
        lax.psum_scatter(d_wqkv, "fsdp", scatter_dimension=0, tiled=True),
        lax.psum_scatter(d_table, "fsdp", scatter_dimension=0, tiled=True),
        lax.psum_scatter(d_wout, "fsdp", scatter_dimension=0, tiled=True),
        lax.psum_scatter(d_scale_a, "fsdp", scatter_dimension=0, tiled=True),
        lax.psum_scatter(d_gain_two, "fsdp", scatter_dimension=0, tiled=True),
        lax.psum_scatter(d_shift_two, "fsdp", scatter_dimension=0, tiled=True),
        lax.psum_scatter(d_wup, "fsdp", scatter_dimension=0, tiled=True),
        lax.psum_scatter(d_bup, "fsdp", scatter_dimension=0, tiled=True),
        lax.psum_scatter(d_wdown, "fsdp", scatter_dimension=0, tiled=True),
        lax.psum_scatter(d_bdown, "fsdp", scatter_dimension=0, tiled=True),
        lax.psum_scatter(d_scale_m, "fsdp", scatter_dimension=0, tiled=True),
    )
    (
        t_gain_one,
        t_shift_one,
        t_wqkv,
        t_table,
        t_wout,
        t_scale_a,
        t_gain_two,
        t_shift_two,
        t_wup,
        t_bup,
        t_wdown,
        t_bdown,
        t_scale_m,
    ) = lax.psum(
        (
            r_gain_one,
            r_shift_one,
            r_wqkv,
            r_table,
            r_wout,
            r_scale_a,
            r_gain_two,
            r_shift_two,
            r_wup,
            r_bup,
            r_wdown,
            r_bdown,
            r_scale_m,
        ),
        "dp",
    )
    return (
        layer_out,
        grad_tokens,
        t_gain_one,
        t_shift_one,
        t_wqkv,
        t_table,
        t_wout,
        t_scale_a,
        t_gain_two,
        t_shift_two,
        t_wup,
        t_bup,
        t_wdown,
        t_bdown,
        t_scale_m,
    )


def solution(mesh):
    in_specs = (
        P(("dp", "fsdp"), None),
        P(("dp", "fsdp"), None),
        P(("dp", "fsdp")),
        P(("dp", "fsdp")),
        P(("dp", "fsdp")),
        P("fsdp"),
        P("fsdp"),
        P("fsdp", None),
        P("fsdp", None, None),
        P("fsdp", None),
        P("fsdp"),
        P("fsdp"),
        P("fsdp"),
        P("fsdp", None),
        P("fsdp"),
        P("fsdp", None),
        P("fsdp"),
        P("fsdp"),
    )
    out_specs = (
        P(("dp", "fsdp"), None),
        P(("dp", "fsdp"), None),
        P("fsdp"),
        P("fsdp"),
        P("fsdp", None),
        P("fsdp", None, None),
        P("fsdp", None),
        P("fsdp"),
        P("fsdp"),
        P("fsdp"),
        P("fsdp", None),
        P("fsdp"),
        P("fsdp", None),
        P("fsdp"),
        P("fsdp"),
    )
    return jax.shard_map(local, mesh=mesh, in_specs=in_specs, out_specs=out_specs, check_vma=False)
```

profile of v0, /device:TPU:0, one launch (start us, length us, event | category | flops | bytes accessed | tf_op | source)
XLA Modules:
  0.0 1174.8 jit_solution(14659820310803307517)
XLA Ops:
  16.9 14.0 %all-reduce.19 = (bf16[768]{0:T(1024)(128)(2,1)S(1)}, bf16[768]{0:T(1024)(128)(2,1)S(1)}, bf16[768]{0:T(1024)(128)(2,1)}, bf16[768]{0:T(1024)(128)(2,1)}, bf16[7...) all-reduce(bf16[768]{0:T(1024)(128)(2,1)S(1)} %dynamic-update-slice, ...), channel_id=1, replica_groups=mesh['dp'=8,'fsdp'=4] {'fsdp'}, use_global_device_ids=true, to_apply=%add.2 | all-reduce | flops 5376 | bytes 21504
  34.7 5.1 all_gather.51
  40.4 115.0 %gather_fusion = bf16[32768,12]{1,0:T(8,128)(2,1)} fusion(bf16[12,63]{0,1:T(8,128)(2,1)S(1)} %bitcast.148, s32[32768]{0:T(1024)S(1)} %broadcast_clamp_fusion.1), kind=kCustom, calls=%fused_computation.clone | custom fusion | bytes 1703936 | tf_op jit(solution)/shard_map/jit(_take)/gather | solution.py:20
  155.5 9.0 copy.115
  165.0 115.0 %gather_fusion.1 = bf16[32768,12]{1,0:T(8,128)(2,1)} fusion(bf16[12,63]{0,1:T(8,128)(2,1)S(1)} %bitcast.149, s32[32768]{0:T(1024)S(1)} %broadcast_clamp_fusion), kind=kCustom, calls=%fused_computation.1.clone | custom fusion | bytes 1703936 | tf_op jit(solution)/shard_map/jit(_take)/gather | solution.py:21
  280.1 9.1 copy.118
  293.8 5.5 all-gather
  304.4 8.0 convolution_convert_fusion
  312.4 6.7 copy.111
  319.0 4.4 slice_bitcast_fusion
  333.8 5.4 copy.112
  345.3 74.0 %while.27 = (s32[]{:T(128)}, bf16[2,12,512,64]{2,3,1,0:T(8,128)(2,1)}, f32[2,12,512]{2,1,0:T(8,128)S(1)}, pred[2,512,1024]{2,1,0:T(8,128)(4,1)}, bf16[2,12,512,1...) while((s32[]{:T(128)}, ...), condition=%wide.region_5.7_spmd, body=%wide.region_2.6_spmd.sunk | while | flops 2472929280 | bytes 91710584 | solution.py:130
  346.9 11.6 select_reduce_fusion.2
  358.5 11.6 fusion.126
  370.1 12.4 %fusion.127 = bf16[2,12,512,64]{2,3,1,0:T(8,128)(2,1)} fusion(bf16[2,12,512,64]{2,3,1,0:T(8,128)(2,1)} %get-tuple-element.513, s32[]{:T(128)} %get-tuple-element.512, bf16[12,1024,64]{1,2,0:T(8,128)(2,1)S(1)} %copy-done.7, f32[12,512,1024]{2,1,0:T(8,128)} %get-tuple-element.489, f32[12,512]{1,0:T(8,128)S(1)} %fusion.126, ...), kind=kOutput, calls=%fused_computation.13.clone.1 | convolution fusion | flops 830865408 | bytes 28099072 | tf_op jit(solution)/shard_map/while/body/eval_jaxpr/hqk,hke->hqe/dot_general | solution.py:32
  383.6 11.6 select_reduce_fusion.2
  395.2 11.6 fusion.126
  406.9 12.4 %fusion.127 = bf16[2,12,512,64]{2,3,1,0:T(8,128)(2,1)} fusion(bf16[2,12,512,64]{2,3,1,0:T(8,128)(2,1)} %get-tuple-element.513, s32[]{:T(128)} %get-tuple-element.512, bf16[12,1024,64]{1,2,0:T(8,128)(2,1)S(1)} %copy-done.7, f32[12,512,1024]{2,1,0:T(8,128)} %get-tuple-element.489, f32[12,512]{1,0:T(8,128)S(1)} %fusion.126, ...), kind=kOutput, calls=%fused_computation.13.clone.1 | convolution fusion | flops 830865408 | bytes 28099072 | tf_op jit(solution)/shard_map/while/body/eval_jaxpr/hqk,hke->hqe/dot_general | solution.py:32
  423.9 5.6 fusion.81
  431.7 15.5 %multiply_convert_fusion.1 = (bf16[1024,3072]{1,0:T(8,128)(2,1)}, f32[1024,3072]{1,0:T(8,128)}) fusion(f32[3072]{0:T(1024)S(1)} %bitcast.164, bf16[768,3072]{1,0:T(8,128)(2,1)} %all-gather.10.cloned.1.call-done, f32[1024,768]{0,1:T(8,128)} %copy-done.4, f32[768]{0:T(1024)S(1)} %copy-done.70, f32[768]{0:T(1024)S(1)} %copy-done.50, f32[1024]{0:T(1024)S(1)} %fusion.72, ...), kind=kOutput, calls=%fused_computation.55 | convolution fusion | flops 4867227648 | bytes 26765312 | tf_op jit(solution)/shard_map/dot_general | solution.py:139
  447.3 17.8 %convert_reduce_fusion = (f32[3072]{0:T(1024)}, bf16[1024,3072]{1,0:T(8,128)(2,1)S(1)}) fusion(f32[1024,3072]{1,0:T(8,128)} %get-tuple-element.377, f32[3072]{0:T(1024)S(1)} %bitcast.165, bf16[3072,768]{1,0:T(8,128)(2,1)} %all-gather.12.cloned.1.call-done, bf16[1024,768]{0,1:T(8,128)(2,1)} %copy.122, f32[1024]{0:T(1024)S(1)} %copy-done.59, ...), kind=kOutput, calls=%fused_computation.54 | convolution fusion | flops 4907332608 | bytes 25197568 | tf_op jit(solution)/shard_map/nd,fd->nf/dot_general | solution.py:164
  465.1 7.3 fusion.85
  475.9 4.5 multiply_reduce_fusion.2
  500.8 171.7 %while.28 = (s32[]{:T(128)}, f32[12,1024,128]{2,1,0:T(8,128)}, f32[12,1024,64]{1,2,0:T(8,128)}, f32[2,12,512,64]{2,3,1,0:T(8,128)}, pred[2,512,1024]{2,1,0:T(8,1...) while((s32[]{:T(128)}, f32[12,1024,128]{2,1,0:T(8,128)}, ...), condition=%wide.region_12.14_spmd.clone, body=%wide.region_10.13_spmd.clone.sunk | while | flops 5717354496 | bytes 227191472 | solution.py:185
  501.2 11.7 fusion.137
  513.8 17.7 %multiply_reduce_fusion.7 = (f32[12,512]{1,0:T(8,128)S(1)}, f32[12,512,1024]{2,1,0:T(8,128)}) fusion(f32[12,512,1024]{2,1,0:T(8,128)} %fusion.137, f32[12,512]{1,0:T(8,128)S(1)} %dynamic-slice_bitcast_fusion.7, pred[512,1024]{1,0:T(8,128)(4,1)} %dynamic-slice_bitcast_fusion.8, bf16[12,1024,64]{1,2,0:T(8,128)(2,1)} %get-tuple-element.563, ...), kind=kOutput, calls=%fused_computation.18.clone.1 | convolution fusion | flops 830466048 | bytes 53264896 | tf_op jit(solution)/shard_map/while/body/eval_jaxpr/hqe,hke->hqk/dot_general | solution.py:41
  531.4 22.0 %multiply_convert_fusion.8 = bf16[12,512,1024]{2,1,0:T(8,128)(2,1)} fusion(f32[12,512,1024]{2,1,0:T(8,128)} %get-tuple-element.502, f32[12,512,1024]{2,1,0:T(8,128)} %fusion.137, f32[12,512]{1,0:T(8,128)S(1)} %get-tuple-element.503, f32[12,512]{1,0:T(8,128)S(1)} %dynamic-slice_bitcast_fusion.7, pred[512,1024]{1,0:T(8,128)(4,1)} %dynamic-slice_bitcast_fusion.8), kind=kLoop, calls=%fused_computation.17.clone.1 | loop fusion | flops 31457280 | bytes 63488000 | tf_op jit(solution)/shard_map/while/body/eval_jaxpr/convert_element_type | solution.py:43
  553.4 8.9 select_add_fusion.4
  562.3 10.1 bitcast_dynamic-update-slice_fusion.5
  572.3 13.3 %select_add_fusion.5 = f32[12,1024,64]{1,2,0:T(8,128)} fusion(f32[12,1024,64]{1,2,0:T(8,128)} %get-tuple-element.543, f32[12,512,1024]{2,1,0:T(8,128)} %fusion.137, f32[12,512]{1,0:T(8,128)S(1)} %dynamic-slice_bitcast_fusion.7, pred[512,1024]{1,0:T(8,128)(4,1)} %dynamic-slice_bitcast_fusion.8, pred[]{:T(512)S(6)} %compare.3, ...), kind=kOutput, calls=%fused_computation.26.clone.1 | convolution fusion | flops 825753600 | bytes 32793088 | tf_op jit(solution)/shard_map/while/body/eval_jaxpr/hqk,hqe->hke/dot_general | solution.py:48
  585.7 11.6 fusion.137
  598.1 17.6 %multiply_reduce_fusion.7 = (f32[12,512]{1,0:T(8,128)S(1)}, f32[12,512,1024]{2,1,0:T(8,128)}) fusion(f32[12,512,1024]{2,1,0:T(8,128)} %fusion.137, f32[12,512]{1,0:T(8,128)S(1)} %dynamic-slice_bitcast_fusion.7, pred[512,1024]{1,0:T(8,128)(4,1)} %dynamic-slice_bitcast_fusion.8, bf16[12,1024,64]{1,2,0:T(8,128)(2,1)} %get-tuple-element.563, ...), kind=kOutput, calls=%fused_computation.18.clone.1 | convolution fusion | flops 830466048 | bytes 53264896 | tf_op jit(solution)/shard_map/while/body/eval_jaxpr/hqe,hke->hqk/dot_general | solution.py:41
  615.7 22.0 %multiply_convert_fusion.8 = bf16[12,512,1024]{2,1,0:T(8,128)(2,1)} fusion(f32[12,512,1024]{2,1,0:T(8,128)} %get-tuple-element.502, f32[12,512,1024]{2,1,0:T(8,128)} %fusion.137, f32[12,512]{1,0:T(8,128)S(1)} %get-tuple-element.503, f32[12,512]{1,0:T(8,128)S(1)} %dynamic-slice_bitcast_fusion.7, pred[512,1024]{1,0:T(8,128)(4,1)} %dynamic-slice_bitcast_fusion.8), kind=kLoop, calls=%fused_computation.17.clone.1 | loop fusion | flops 31457280 | bytes 63488000 | tf_op jit(solution)/shard_map/while/body/eval_jaxpr/convert_element_type | solution.py:43
  637.7 10.5 select_add_fusion.4
  648.2 10.1 bitcast_dynamic-update-slice_fusion.5
  658.2 14.2 %select_add_fusion.5 = f32[12,1024,64]{1,2,0:T(8,128)} fusion(f32[12,1024,64]{1,2,0:T(8,128)} %get-tuple-element.543, f32[12,512,1024]{2,1,0:T(8,128)} %fusion.137, f32[12,512]{1,0:T(8,128)S(1)} %dynamic-slice_bitcast_fusion.7, pred[512,1024]{1,0:T(8,128)(4,1)} %dynamic-slice_bitcast_fusion.8, pred[]{:T(512)S(6)} %compare.3, ...), kind=kOutput, calls=%fused_computation.26.clone.1 | convolution fusion | flops 825753600 | bytes 32793088 | tf_op jit(solution)/shard_map/while/body/eval_jaxpr/hqk,hqe->hke/dot_general | solution.py:48
  672.6 6.5 copy.128
  687.1 7.0 fusion.51
  694.8 11.4 fusion.78
  707.7 10.8 fusion.77
  718.8 39.6 %reduce-scatter.5.cloned.1.call-done = f32[192,2304]{1,0:T(8,128)} async-done(((f32[768,2304]{1,0:T(8,128)}), f32[192,2304]{1,0:T(8,128)}) %reduce-scatter.5.cloned.1.call-update) | async-done | bytes 1769488 | tf_op jit(solution)/shard_map/reduce_scatter | solution.py:221
  758.5 81.1 %reduce-scatter.9.cloned.1.call-done = f32[192,3072]{1,0:T(8,128)} async-done(((f32[768,3072]{1,0:T(8,128)}), f32[192,3072]{1,0:T(8,128)}) %reduce-scatter.9.cloned.1.call-update) | async-done | bytes 2359312 | tf_op jit(solution)/shard_map/reduce_scatter | solution.py:227
  839.5 81.1 %reduce-scatter.11.cloned.1.call-done = f32[768,768]{1,0:T(8,128)} async-done(((f32[3072,768]{1,0:T(8,128)}), f32[768,768]{1,0:T(8,128)}) %reduce-scatter.11.cloned.1.call-update) | async-done | bytes 2359312 | tf_op jit(solution)/shard_map/reduce_scatter | solution.py:229
  929.0 8.9 fusion.84
  946.4 14.4 %multiply_reduce_fusion.1 = (f32[768]{0:T(1024)S(1)}, f32[768]{0:T(1024)S(1)}, f32[768]{0:T(1024)S(1)}, bf16[1024,768]{0,1:T(8,128)(2,1)}, bf16[1024,768]{0,1:T(8,128)(2,1)}) fusion(bf16[1024,768]{0,1:T(8,128)(2,1)S(1)} %copy-done.15, f32[1024]{0:T(1024)S(1)} %copy-done.60, f32[768]{0:T(1024)S(1)} %convert_element_type.118, f32[768]{0:T(1024)S(1)} %copy-done.67, ...), kind=kOutput, calls=%fused_computation.77 | convolution fusion | flops 4852282368 | bytes 29927424 | tf_op jit(solution)/shard_map/dot_general | solution.py:141
  960.8 11.6 all-reduce.18
  977.4 39.3 %all-reduce.16 = (f32[192]{0:T(256)}, f32[192]{0:T(256)}, f32[3,2,63]{2,1,0:T(2,128)}, f32[192]{0:T(256)}, f32[192]{0:T(256)}, /*index=5*/f32[192]{0:T(256)}, f32[768]{0:T(1024)}, f32[192]{0:T(256)}, f32[192]{0:T(256)}) all-reduce(f32[192]{0:T(256)S(1)} %dynamic-slice.8, ...), channel_id=1, replica_groups=mesh['dp'=8,'fsdp'=4] {'dp'}, use_global_device_ids=true, to_apply=%region_17.19 | all-reduce | flops 2490 | bytes 19920 | tf_op jit(solution)/shard_map/psum | solution.py:247
  1016.7 144.8 %all-reduce.22.cloned.1.call-done = (f32[192,2304]{1,0:T(8,128)}, f32[192,768]{1,0:T(8,128)}, f32[192,3072]{1,0:T(8,128)}, f32[768,768]{1,0:T(8,128)}) async-done(((f32[192,2304]{1,0:T(8,128)}, f32[192,768]{1,0:T(8,128)}, f32[192,3072]{1,0:T(8,128)}, f32[768,768]{1,0:T(8,128)}), (f32[192,2304]{1,0:T(8,128)}, f32[192,768]{1,0:T(8,128)}, f32[192,3072]{1,0:T(8,128)}, ...) | async-done | bytes 7077904 | tf_op jit(solution)/shard_map/psum | solution.py:247
  (324 shorter events, 110.8 us)
Async XLA Ops:
  7.2 6.8 copy-start.78
  7.2 8.0 copy-start.82
  7.2 8.2 copy-start.83
  7.3 8.5 copy-start.84
  7.3 8.7 copy-start.85
  7.3 8.9 copy-start.86
  7.3 9.1 copy-start.87
  7.3 9.4 copy-start.88
  7.3 24.7 %copy-start.21 = (bf16[1024,768]{1,0:T(8,128)(2,1)S(1)}, bf16[1024,768]{1,0:T(8,128)(2,1)}, u32[]{:S(2)}) copy-start(bf16[1024,768]{1,0:T(8,128)(2,1)} %param.24) | copy-start | bytes 4718596
  7.3 297.1 %all-gather.6.cloned.1.call-start = ((), (), s32[]{:S(2)}) async-start(), calls=%async_computation.4 | async-start | bytes 4423680 | tf_op jit(solution)/shard_map/all_gather | solution.py:90
  8.0 415.9 %all-gather.8.cloned.1.call-start = ((), (), s32[]{:S(2)}) async-start(), calls=%async_computation.5 | async-start | bytes 1474560 | tf_op jit(solution)/shard_map/all_gather | solution.py:92
  8.8 422.9 %all-gather.10.cloned.1.call-start = ((), (), s32[]{:S(2)}) async-start(), calls=%async_computation.6 | async-start | bytes 5898240 | tf_op jit(solution)/shard_map/all_gather | solution.py:96
  9.5 437.7 %all-gather.12.cloned.1.call-start = ((), (), s32[]{:S(2)}) async-start(), calls=%async_computation.7 | async-start | bytes 5898240 | tf_op jit(solution)/shard_map/all_gather | solution.py:98
  10.1 708.7 %reduce-scatter.7.cloned.1.call-start = ((), (), s32[]{:S(2)}) async-start(), calls=%async_computation.9 | async-start | bytes 2949120 | tf_op jit(solution)/shard_map/reduce_scatter | solution.py:223
  32.8 271.6 %copy-start.2 = (bf16[1024,768]{0,1:T(8,128)(2,1)}, bf16[1024,768]{0,1:T(8,128)(2,1)S(1)}, u32[]{:S(2)}) copy-start(bf16[1024,768]{0,1:T(8,128)(2,1)S(1)} %copy.110) | copy-start | bytes 4718596
  33.1 6.8 copy-start.38
  280.1 9.1 copy-start.57
  280.1 9.4 copy-start.56
  280.1 10.3 copy-start.47
  280.1 10.3 copy-start.58
  280.1 11.9 %copy-start.77 = (bf16[768]{0:T(1024)(128)(2,1)S(1)}, bf16[768]{0:T(1024)(128)(2,1)}, u32[]{:S(2)}) copy-start(bf16[768]{0:T(1024)(128)(2,1)} %get-tuple-element.353) | copy-start | bytes 4612
  280.1 12.5 %copy-start.76 = (bf16[768]{0:T(1024)(128)(2,1)S(1)}, bf16[768]{0:T(1024)(128)(2,1)}, u32[]{:S(2)}) copy-start(bf16[768]{0:T(1024)(128)(2,1)} %get-tuple-element.355) | copy-start | bytes 4612
  280.1 13.1 %copy-start.75 = (bf16[768]{0:T(1024)(128)(2,1)S(1)}, bf16[768]{0:T(1024)(128)(2,1)}, u32[]{:S(2)}) copy-start(bf16[768]{0:T(1024)(128)(2,1)} %get-tuple-element.354) | copy-start | bytes 4612
  280.1 13.7 %copy-start.79 = (bf16[768]{0:T(1024)(128)(2,1)S(1)}, bf16[768]{0:T(1024)(128)(2,1)}, u32[]{:S(2)}) copy-start(bf16[768]{0:T(1024)(128)(2,1)} %param.38) | copy-start | bytes 4612
  280.1 19.7 %copy-start.74 = (bf16[768]{0:T(1024)(128)(2,1)S(1)}, bf16[768]{0:T(1024)(128)(2,1)}, u32[]{:S(2)}) copy-start(bf16[768]{0:T(1024)(128)(2,1)} %get-tuple-element.357) | copy-start | bytes 4612
  289.2 13.8 %copy-start.32 = (pred[1024,32]{0,1:T(8,128)(4,1)S(1)}, pred[1024,32]{0,1:T(8,128)(4,1)}, u32[]{:S(2)}) copy-start(pred[1024,32]{0,1:T(8,128)(4,1)} %compare_and_fusion) | copy-start | bytes 98308
  289.2 13.8 %copy-start.33 = (pred[1024,32]{0,1:T(8,128)(4,1)S(1)}, pred[1024,32]{0,1:T(8,128)(4,1)}, u32[]{:S(2)}) copy-start(pred[1024,32]{0,1:T(8,128)(4,1)} %compare_and_fusion.1) | copy-start | bytes 98308
  319.0 5.6 copy-start.18
  358.5 11.6 copy-start.7
  395.2 11.6 copy-start.7
  429.5 50.9 %copy-start.41 = (f32[1024]{0:T(1024)}, f32[1024]{0:T(1024)S(1)}, u32[]{:S(2)}) copy-start(f32[1024]{0:T(1024)S(1)} %broadcast_multiply_fusion) | copy-start | bytes 12292
  431.7 48.7 %copy-start.52 = (f32[1024]{0:T(1024)}, f32[1024]{0:T(1024)S(1)}, u32[]{:S(2)}) copy-start(f32[1024]{0:T(1024)S(1)} %fusion.72) | copy-start | bytes 12292
  431.7 15.5 %copy-start.59 = (f32[1024]{0:T(1024)S(1)}, f32[1024]{0:T(1024)}, u32[]{:S(2)}) copy-start(f32[1024]{0:T(1024)} %compare_convert_fusion) | copy-start | bytes 12292
  431.7 15.5 %copy-start.66 = (f32[768]{0:T(1024)S(1)}, f32[768]{0:T(1024)}, u32[]{:S(2)}) copy-start(f32[768]{0:T(1024)} %convert_element_type.112) | copy-start | bytes 9220
  447.3 17.8 %copy-start.81 = (bf16[768,3072]{1,0:T(8,128)(2,1)S(1)}, bf16[768,3072]{1,0:T(8,128)(2,1)}, u32[]{:S(2)}) copy-start(bf16[768,3072]{1,0:T(8,128)(2,1)} %all-gather.10.cloned.1.call-done) | copy-start | bytes 14155780
  465.1 7.3 copy-start.89
  487.0 271.4 %reduce-scatter.5.cloned.1.call-start = ((), (), s32[]{:S(2)}) async-start(), calls=%async_computation.8 | async-start | bytes 8847360 | tf_op jit(solution)/shard_map/reduce_scatter | solution.py:221
  501.2 11.7 copy-start.8
  585.7 11.6 copy-start.8
  694.1 145.4 %reduce-scatter.9.cloned.1.call-start = ((), (), s32[]{:S(2)}) async-start(), calls=%async_computation.10 | async-start | bytes 11796480 | tf_op jit(solution)/shard_map/reduce_scatter | solution.py:227
  706.2 214.4 %reduce-scatter.11.cloned.1.call-start = ((), (), s32[]{:S(2)}) async-start(), calls=%async_computation.11 | async-start | bytes 11796480 | tf_op jit(solution)/shard_map/reduce_scatter | solution.py:229
  718.5 442.9 %all-reduce.22.cloned.1.call-start = ((), (), s32[]{:S(2)}) async-start(), calls=%async_computation.12 | async-start | bytes 14155776 | tf_op jit(solution)/shard_map/psum | solution.py:247
  923.2 5.8 copy-start.23
  923.2 5.8 copy-start.25
  946.4 14.4 %copy-start.63 = (f32[768]{0:T(1024)S(1)}, f32[768]{0:T(1024)}, u32[]{:S(2)}) copy-start(f32[768]{0:T(1024)} %get-tuple-element.286) | copy-start | bytes 9220
  946.4 14.4 %copy-start.65 = (f32[3072]{0:T(1024)S(1)}, f32[3072]{0:T(1024)}, u32[]{:S(2)}) copy-start(f32[3072]{0:T(1024)} %get-tuple-element.382) | copy-start | bytes 36868
  946.4 14.4 %copy-start.72 = (f32[768]{0:T(1024)S(1)}, f32[768]{0:T(1024)}, u32[]{:S(2)}) copy-start(f32[768]{0:T(1024)} %get-tuple-element.380) | copy-start | bytes 9220
  960.8 14.9 %copy-start.26 = (bf16[1024,768]{0,1:T(8,128)(2,1)S(1)}, bf16[1024,768]{0,1:T(8,128)(2,1)}, u32[]{:S(2)}) copy-start(bf16[1024,768]{0,1:T(8,128)(2,1)} %get-tuple-element.366) | copy-start | bytes 4718596
  (53 other events, 133.1 us)
Sparse Core Ops, SparseCore 0:
  9.7 33.7 all-gather.5
  45.0 17.5 all-gather.7
  64.1 37.4 all-gather.9
  103.1 37.4 all-gather.11
  487.2 33.4 reduce-scatter.6
  694.3 64.1 reduce-scatter.4
  761.1 78.4 reduce-scatter.8
  842.1 78.4 reduce-scatter.10
  925.0 236.4 all-reduce.21
where the time goes:
time: 1180 us; the launch traced here: 1170 us
  waiting for transfers between devices  349 us (30%)
  local copies, waits for them, and re-layouts  338 us (29%)
  matrix products  293 us (25%)
  other arithmetic  100 us (8%)
  blocking collectives  75.5 us (6%)
  between operations  17.6 us (1%)
    psum x1, waiting for transfers between devices, local(): lax.psum((r_gain_one, r_shift_one, r_wqkv, r_table, r_wout, r_scale_a, r_...  145 us
    gather x2, local copies, waits for them, and re-layouts, key_side(): bias_col = jnp.take(table[:, 1, :], index_col, axis=1)  124 us
    gather x2, local copies, waits for them, and re-layouts, key_side(): bias_row = jnp.take(table[:, 0, :], index_row, axis=1)  124 us
    reduce_scatter x1, waiting for transfers between devices, local(): lax.psum_scatter(d_wup, 'fsdp', scatter_dimension=0, tiled=True)  81.1 us
    reduce_scatter x1, waiting for transfers between devices, local(): lax.psum_scatter(d_wdown, 'fsdp', scatter_dimension=0, tiled=True)  81.1 us
    convert_element_type x2, other arithmetic, attend_back(): d_low = d_scores.astype(jnp.bfloat16)  44 us
    reduce_scatter x1, waiting for transfers between devices, local(): lax.psum_scatter(d_wqkv, 'fsdp', scatter_dimension=0, tiled=True)  39.6 us
    psum x1, blocking collectives, local(): lax.psum((r_gain_one, r_shift_one, r_wqkv, r_table, r_wout, r_scale_a, r_...  39.3 us
  transfers between devices with their start and end apart: 9, of which 4 were waited for; matrix products, arithmetic and copies ran while one was open for 57% of the time, Pallas kernels for 0%

commit v1 on v0

v1 whole, which is shorter than its diff:
```python
import jax
import jax.numpy as jnp
from jax import lax
from jax.experimental import pallas as pl
from jax.experimental.pallas import tpu as pltpu
from jax.sharding import PartitionSpec as P

F32 = jnp.float32
BF = jnp.bfloat16
NT = (((1,), (1,)), ((), ()))
NN = (((1,), (0,)), ((), ()))
VMEM = pl.BlockSpec(memory_space=pltpu.VMEM)
LIMIT = 60 << 20
MASKED = -1e30


def mm(a, b, dims=NN):
    return lax.dot_general(a, b, dims, preferred_element_type=F32)


def lanes(rows, width=128):
    return lax.broadcasted_iota(jnp.int32, (rows, width), 1)


def normalize(rows, gain, shift):
    center = rows - jnp.mean(rows, axis=-1, keepdims=True)
    spread = jnp.mean(center * center, axis=-1, keepdims=True)
    return center * lax.rsqrt(spread + 1e-06) * gain + shift


def pieces(x, lane):
    hi = x.astype(BF)
    rest = x - hi.astype(F32)
    mid = rest.astype(BF)
    low = (rest - mid.astype(F32)).astype(BF)
    third = lane % 3
    return jnp.where(third == 0, hi.astype(F32), jnp.where(third == 1, mid.astype(F32), low.astype(F32)))


def position_columns(pos, hot, page_q, page_k):
    for r in range(pos.shape[1]):
        code = (pos[0, r : r + 1, :] + 1) * 4096 + pos[1, r : r + 1, :] * 64 + pos[2, r : r + 1, :]
        code = jnp.broadcast_to(code.astype(F32), (128, 128)).T.astype(jnp.int32)
        lane = lanes(128)
        page, row, col = code >> 12, (code >> 6) & 63, code & 63
        near = lane & 63
        where = jnp.where(near < 32, row, col + 32)
        at = pl.ds(r * 128, 128)
        hot[at, :] = jnp.where(where == near, 1.0, 0.0).astype(BF)
        page_q[at, :] = jnp.where(page == lane, 1.0, 0.0)
        page_k[at, :] = jnp.where((lane < 6) & (page != lane), MASKED, 0.0).astype(BF)


def toeplitz(table, bias):
    lane = lanes(32)
    for p in range(bias.shape[0]):
        for axis in range(2):
            parts = []
            for head, at in ((2 * p + 1, 32 * axis), (2 * p, 64 + 32 * axis)):
                row = jnp.broadcast_to(table[2 * head + axis : 2 * head + axis + 1, :], (32, 128))
                rolled = pltpu.roll(row, (97 + at) % 128, axis=1, stride=1, stride_axis=0)
                parts.append(jnp.where((lane >= at) & (lane < at + 32), rolled, 0.0))
            bias[p, 32 * axis : 32 * axis + 32, :] = (parts[0] + parts[1]).astype(BF)


def forward_kernel(tok, pos, gain, shift, table, wqkv, norm, qkv, att, ext, hot, page_k, bias, lse, ka, va):
    count, width = tok.shape
    pairs = bias.shape[0]
    position_columns(pos, hot, lse, page_k)
    toeplitz(table, bias)

    @pl.loop(0, count // 256)
    def _(b):
        at = pl.ds(pl.multiple_of(b * 256, 256), 256)
        rows = normalize(tok[at, :].astype(F32), gain[...], shift[...]).astype(BF)
        norm[at, :] = rows
        for part in range(3):
            block = mm(rows, wqkv[:, part * width : (part + 1) * width]).astype(BF)
            if part == 0:
                block = block * jnp.asarray(0.125, BF)
            for p in range(pairs):
                qkv[part * pairs + p, at, :] = block[:, p * 128 : (p + 1) * 128]

    low_half = lanes(count) < 64

    @pl.loop(0, pairs)
    def _(p):
        keys, values = qkv[pairs + p], qkv[2 * pairs + p]
        side = mm(hot[:, :64], bias[p]).astype(BF)
        one = jnp.ones_like(values)
        ka[0, :, :128] = jnp.where(low_half, keys, side)
        ka[1, :, :128] = jnp.where(low_half, side, keys)
        va[0] = jnp.where(low_half, values, one)
        va[1] = jnp.where(low_half, one, values)
        for e in range(2):
            ka[e, :, 128:] = page_k[...]

        @pl.loop(0, count // 256)
        def _(b):
            at = pl.ds(pl.multiple_of(b * 256, 256), 256)
            queries, places = qkv[p, at, :], hot[at, :]
            kept = lse[at, :]
            lane = lanes(256)
            half = lane < 64
            page_hot = jnp.where(lane < 6, kept, 0.0).astype(BF)
            outs = []
            for e in range(2):
                first = jnp.where(half, queries, places) if e == 0 else jnp.where(half, places, queries)
                scores = mm(jnp.concatenate([first, page_hot], axis=1), ka[e], NT)
                top = jnp.max(scores, axis=1, keepdims=True)
                expo = jnp.exp(scores - top).astype(BF)
                out = mm(expo, va[e])
                turned = pltpu.roll(out, 64, axis=1)
                total = jnp.where(half, turned, out) if e == 0 else jnp.where(half, out, turned)
                outs.append(out / total)
                kept = jnp.where(lane // 3 == 2 + 2 * p + e, top + jnp.log(total), kept)
            lse[at, :] = kept
            att[at, pl.ds(pl.multiple_of(p * 128, 128), 128)] = jnp.where(half, outs[0], outs[1]).astype(BF)

    lane = lanes(count)
    ext[...] = jnp.where(lane < 6, lse[...], pieces(lse[...], lane)).astype(BF)


def forward_call(tok, pos, gain, shift, table, wqkv):
    count, width = tok.shape
    pairs = width // 128
    return pl.pallas_call(
        forward_kernel,
        out_shape=[
            jax.ShapeDtypeStruct((count, width), BF),
            jax.ShapeDtypeStruct((3 * pairs, count, 128), BF),
            jax.ShapeDtypeStruct((count, width), BF),
            jax.ShapeDtypeStruct((count, 128), BF),
            jax.ShapeDtypeStruct((count, 128), BF),
            jax.ShapeDtypeStruct((count, 128), BF),
            jax.ShapeDtypeStruct((pairs, 64, 128), BF),
        ],
        in_specs=[VMEM] * 6,
        out_specs=[VMEM] * 7,
        scratch_shapes=[
            pltpu.VMEM((count, 128), F32),
            pltpu.VMEM((2, count, 256), BF),
            pltpu.VMEM((2, count, 128), BF),
        ],
        compiler_params=pltpu.CompilerParams(vmem_limit_bytes=LIMIT),
        name="attention_forward",
    )(tok, pos, gain, shift, table, wqkv)


def backward_kernel(
    pos, qkv, ext, hot, page_k, bias, att, datt, dqkv, dtab, qa, ka, va, doa, kt, dqt, dext, hot_t, square
):
    count, width = att.shape
    pairs = bias.shape[0]
    col = lax.broadcasted_iota(jnp.int32, (width, 128), 0) // 64
    pick = jnp.where(lanes(width) // 3 == col, 1.0, 0.0).astype(BF)

    @pl.loop(0, count // 256)
    def _(b):
        at = pl.ds(pl.multiple_of(b * 256, 256), 256)
        prod = att[at, :].astype(F32) * datt[at, :].astype(F32)
        hi = prod.astype(BF)
        low = (prod - hi.astype(F32)).astype(BF)
        dext[at, :] = pieces(-(mm(hi, pick) + mm(low, pick)), lanes(256)).astype(BF)

    for r in range(pos.shape[1]):
        want = 31 - lax.broadcasted_iota(jnp.int32, (32, 128), 0)
        for axis in range(2):
            have = jnp.broadcast_to(pos[1 + axis, r : r + 1, :], (32, 128))
            hot_t[32 * axis : 32 * axis + 32, r * 128 : r * 128 + 128] = jnp.where(have == want, 1.0, 0.0).astype(BF)

    low_half = lanes(count) < 64
    third = lanes(count) // 3

    @pl.loop(0, pairs)
    def _(p):
        queries, keys, values = qkv[p], qkv[pairs + p], qkv[2 * pairs + p]
        side = mm(hot[:, :64], bias[p]).astype(BF)
        zero = jnp.zeros_like(values)
        places = hot[...]
        qa[0, :, :128] = jnp.where(low_half, queries, places)
        qa[1, :, :128] = jnp.where(low_half, places, queries)
        ka[0, :, :128] = jnp.where(low_half, keys, side)
        ka[1, :, :128] = jnp.where(low_half, side, keys)
        va[0, :, :128] = jnp.where(low_half, values, zero)
        va[1, :, :128] = jnp.where(low_half, zero, values)
        for e in range(2):
            head = 2 * p + e
            qa[e, :, 128:] = ext[...]
            ka[e, :, 128:] = jnp.where(third == 2 + head, -1.0, page_k[...].astype(F32)).astype(BF)
            va[e, :, 128:] = jnp.where(third == head, 1.0, 0.0).astype(BF)
        doa[:, :128] = datt[:, pl.ds(pl.multiple_of(p * 128, 128), 128)]
        doa[:, 128:] = dext[...]
        kt[...] = keys.T
        dqt[...] = jnp.zeros_like(dqt)
        square[...] = jnp.zeros_like(square)

        @pl.loop(0, count // 256)
        def _(b):
            at = pl.ds(pl.multiple_of(b * 256, 256), 256)
            dks, dvs = [], []
            for e in range(2):
                prob = jnp.exp(mm(ka[e, at, :], qa[e], NT))
                d_prob = mm(va[e, at, :], doa[...], NT)
                d_scores = (prob * d_prob).astype(BF)
                dvs.append(mm(prob.astype(BF), doa[:, :128]))
                dks.append(mm(d_scores, qa[e, :, :128]))
                dqt[64 * e : 64 * e + 64, :] += mm(kt[64 * e : 64 * e + 64, at], d_scores)
            half = lanes(256) < 64
            dqkv[at, pl.ds(pl.multiple_of(width + p * 128, 128), 128)] = jnp.where(half, dks[0], dks[1]).astype(BF)
            dqkv[at, pl.ds(pl.multiple_of(2 * width + p * 128, 128), 128)] = jnp.where(half, dvs[0], dvs[1]).astype(BF)
            part = jnp.where(half, dks[1], dks[0])
            hi = part.astype(BF)
            low = (part - hi.astype(F32)).astype(BF)
            both = mm(hot_t[:, at], jnp.concatenate([hi, low], axis=1))
            square[...] += both[:, :128] + both[:, 128:]

        dqkv[:, pl.ds(pl.multiple_of(p * 128, 128), 128)] = (dqt[...].T * 0.125).astype(BF)
        near = lanes(32) & 63
        for axis in range(2):
            part = square[32 * axis : 32 * axis + 32, :]
            part = jnp.where((near >= 32) if axis else (near < 32), part, 0.0)
            rolled = pltpu.roll(part, 96 * axis, axis=1, stride=1, stride_axis=0)
            dtab[p, axis : axis + 1, :] = jnp.sum(rolled, axis=0, keepdims=True)


def backward_call(pos, qkv, ext, hot, page_k, bias, att, datt):
    count, width = att.shape
    pairs = width // 128
    return pl.pallas_call(
        backward_kernel,
        out_shape=[
            jax.ShapeDtypeStruct((count, 3 * width), BF),
            jax.ShapeDtypeStruct((pairs, 2, 128), F32),
        ],
        in_specs=[VMEM] * 8,
        out_specs=[VMEM] * 2,
        scratch_shapes=[
            pltpu.VMEM((2, count, 256), BF),
            pltpu.VMEM((2, count, 256), BF),
            pltpu.VMEM((2, count, 256), BF),
            pltpu.VMEM((count, 256), BF),
            pltpu.VMEM((128, count), BF),
            pltpu.VMEM((128, count), F32),
            pltpu.VMEM((count, 128), BF),
            pltpu.VMEM((64, count), BF),
            pltpu.VMEM((64, 128), F32),
        ],
        compiler_params=pltpu.CompilerParams(vmem_limit_bytes=LIMIT),
        name="attention_backward",
    )(pos, qkv, ext, hot, page_k, bias, att, datt)


def gather(x):
    return lax.all_gather(x, "fsdp", axis=0, tiled=True)


def local(
    tokens,
    cotangent,
    page_id,
    pos_row,
    pos_col,
    ln1_gain,
    ln1_shift,
    w_qkv,
    rel_table,
    w_out,
    scale_attn,
    ln2_gain,
    ln2_shift,
    w_up,
    b_up,
    w_down,
    b_down,
    scale_mlp,
):
    f32 = F32
    bf16 = BF
    count, width = tokens.shape
    small = [ln1_gain, ln1_shift, scale_attn, ln2_gain, ln2_shift, b_down, scale_mlp]
    rows = jnp.stack(small)
    own = rows.shape[1]
    mine = jnp.concatenate([rows.reshape(-1), b_up, rel_table.reshape(-1)])
    pad = -mine.shape[0] % 1024
    every = lax.all_gather(jnp.pad(mine, (0, pad)), "fsdp", axis=0, tiled=False)
    shards = every.shape[0]
    n_small = len(small) * own
    vectors = jnp.transpose(every[:, :n_small].reshape(shards, len(small), own), (1, 0, 2)).reshape(len(small), -1)
    bup = every[:, n_small : n_small + b_up.shape[0]].reshape(-1)
    heads = rel_table.shape[0] * shards
    offsets = rel_table.shape[2]
    table = every[:, n_small + b_up.shape[0] : n_small + b_up.shape[0] + rel_table.size].reshape(heads * 2, offsets)
    table = jnp.pad(table.astype(f32), ((0, 0), (0, 128 - offsets)))
    vectors = vectors.astype(f32)
    g_one, s_one, scale_a, g_two, s_two, bdown, scale_m = [vectors[i] for i in range(len(small))]
    wqkv = gather(w_qkv)
    wout = gather(w_out)
    wup = gather(w_up)
    wdown = gather(w_down)
    pos = jnp.stack([page_id, pos_row, pos_col]).reshape(3, count // 128, 128)
    norm_one, qkv, att, ext, hot, page_k, bias = forward_call(tokens, pos, g_one[None], s_one[None], table, wqkv)
    tok = tokens.astype(f32)
    proj = jnp.dot(att, wout, preferred_element_type=f32)
    mid = tok + scale_a * proj
    norm_two = normalize(mid, g_two, s_two).astype(bf16)
    upper = jnp.dot(norm_two, wup, preferred_element_type=f32) + bup.astype(f32)
    act = jax.nn.gelu(upper, approximate=True).astype(bf16)
    down = jnp.dot(act, wdown, preferred_element_type=f32) + bdown
    layer_out = (mid + scale_m * down).astype(bf16)
    grad = cotangent.astype(f32) * (page_id >= 0).astype(f32)[:, None]
    d_scale_m = jnp.sum(grad * down, axis=0)
    d_down = (grad * scale_m).astype(bf16)
    d_bdown = jnp.sum(d_down.astype(f32), axis=0)
    d_wdown = jnp.einsum("nf,nd->fd", act, d_down, preferred_element_type=f32).astype(bf16)
    d_act = jnp.einsum("nd,fd->nf", d_down, wdown, preferred_element_type=f32)
    _, gelu_back = jax.vjp(lambda v: jax.nn.gelu(v, approximate=True), upper)
    d_upper = gelu_back(d_act)[0].astype(bf16)
    d_bup = jnp.sum(d_upper.astype(f32), axis=0)
    d_wup = jnp.einsum("nd,nf->df", norm_two, d_upper, preferred_element_type=f32).astype(bf16)
    d_norm_two = jnp.einsum("nf,df->nd", d_upper, wup, preferred_element_type=f32)
    _, norm_two_back = jax.vjp(normalize, mid, g_two, s_two)
    d_mid_norm, d_gain_two, d_shift_two = norm_two_back(d_norm_two)
    d_mid = grad + d_mid_norm
    d_scale_a = jnp.sum(d_mid * proj, axis=0)
    d_proj = (d_mid * scale_a).astype(bf16)
    d_wout = jnp.einsum("nd,ne->de", att, d_proj, preferred_element_type=f32).astype(bf16)
    d_att = jnp.einsum("ne,de->nd", d_proj, wout, preferred_element_type=f32).astype(bf16)
    d_qkv, d_tab = backward_call(pos, qkv, ext, hot, page_k, bias, att, d_att)
    d_wqkv = jnp.einsum("nd,nc->dc", norm_one, d_qkv, preferred_element_type=f32).astype(bf16)
    d_norm_one = jnp.einsum("nc,dc->nd", d_qkv, wqkv, preferred_element_type=f32)
    _, norm_one_back = jax.vjp(normalize, tok, g_one, s_one)
    d_rows_norm, d_gain_one, d_shift_one = norm_one_back(d_norm_one)
    grad_tokens = (d_mid + d_rows_norm).astype(bf16)
    d_table = jnp.transpose(d_tab.reshape(-1, 2, 2, 64)[:, :, ::-1, :offsets], (0, 2, 1, 3)).reshape(heads, 2, offsets)

    def scatter(g):
        return lax.psum(lax.psum_scatter(g, "fsdp", scatter_dimension=0, tiled=True), "dp").astype(f32)

    r_wdown = scatter(d_wdown)
    r_wup = scatter(d_wup)
    r_wout = scatter(d_wout)
    r_wqkv = scatter(d_wqkv)
    flat = jnp.concatenate(
        [
            jnp.stack([d_gain_one, d_shift_one, d_scale_a, d_gain_two, d_shift_two, d_bdown, d_scale_m]).reshape(-1),
            d_bup,
            d_table.reshape(-1),
        ]
    )
    total = lax.psum(flat, ("dp", "fsdp"))
    me = lax.axis_index("fsdp")
    vec = lax.dynamic_slice(total[: len(small) * width].reshape(len(small), width), (0, me * own), (len(small), own))
    r_bup = lax.dynamic_slice(total[len(small) * width :][: d_bup.shape[0]], (me * b_up.shape[0],), b_up.shape)
    r_table = lax.dynamic_slice(
        total[len(small) * width + d_bup.shape[0] :].reshape(heads, 2, offsets), (me * rel_table.shape[0], 0, 0), rel_table.shape
    )
    return (
        layer_out,
        grad_tokens,
        vec[0],
        vec[1],
        r_wqkv,
        r_table,
        r_wout,
        vec[2],
        vec[3],
        vec[4],
        r_wup,
        r_bup,
        r_wdown,
        vec[5],
        vec[6],
    )


def solution(mesh):
    rows = P(("dp", "fsdp"))
    slab = P(("dp", "fsdp"), None)
    vec = P("fsdp")
    mat = P("fsdp", None)
    cube = P("fsdp", None, None)
    in_specs = (slab, slab, rows, rows, rows, vec, vec, mat, cube, mat, vec, vec, vec, mat, vec, mat, vec, vec)
    out_specs = (slab, slab, vec, vec, mat, cube, mat, vec, vec, vec, mat, vec, mat, vec, vec)
    return jax.shard_map(local, mesh=mesh, in_specs=in_specs, out_specs=out_specs, check_vma=False)
```

time: 1180 us -> 558 us (0.47)
  local copies, waits for them, and re-layouts: 338 us -> 21.6 us
  matrix products: 293 us -> 114 us
  waiting for transfers between devices: 349 us -> 239 us
  Pallas kernels: 0 us -> 95.3 us
  other arithmetic: 100 us -> 20.7 us
  blocking collectives: 75.5 us -> 48.4 us
    gather x4 -> x0, local copies, waits for them, and re-layouts: 248 us -> none  [the longest x2 124 us: key_side(): bias_col = jnp.take(table[:, 1, :], index_col, axis=1)]
    dot_general x22 -> x3, matrix products: 215 us -> 27.7 us  [the longest x1 15.7 us: local(): down = jnp.dot(act, wdown, preferred_element_type=f32) + bdown]
    reduce_scatter x4, waiting for transfers between devices: 202 us -> 106 us  [scatter(): lax.psum_scatter(g, 'fsdp', scatter_dimension=0, tiled=True)]
    pallas_call x0 -> x2, Pallas kernels: none -> 95.3 us  [the longest x1 52.5 us: backward_call(): pl.pallas_call(backward_kernel, out_shape=[jax.ShapeDtypeStruct((count, 3...]
    psum x1, waiting for transfers between devices: 145 us -> 77.5 us  [scatter(): lax.psum(lax.psum_scatter(g, 'fsdp', scatter_dimension=0, tiled=True), 'dp')]
    all_gather x4, waiting for transfers between devices: 0.03 us -> 53.3 us  [gather(): return lax.all_gather(x, 'fsdp', axis=0, tiled=True)]
    convert_element_type x12 -> x6, other arithmetic: 49.2 us -> 8.28 us  [the longest x4 7.69 us: scatter(): lax.psum(lax.psum_scatter(g, 'fsdp', scatter_dimension=0, tiled=True), 'dp')]
    unnamed x2 -> x0, blocking collectives: 25.6 us -> none
  transfers between devices with their start and end apart: 9 -> 9, of which waited for: 4 -> 7; matrix products, arithmetic and copies ran while one was open for 57% -> 18% of each run, Pallas kernels for 0% -> 17%
where the time goes in v1:
time: 558 us; the launch traced here: 555 us
  waiting for transfers between devices  239 us (43%)
  matrix products  114 us (20%)
  Pallas kernels  95.3 us (17%)
  blocking collectives  48.4 us (9%)
  local copies, waits for them, and re-layouts  21.6 us (4%)
  other arithmetic  20.7 us (4%)
  between operations  14.5 us (3%)
    reduce_scatter x4, waiting for transfers between devices, scatter(): lax.psum_scatter(g, 'fsdp', scatter_dimension=0, tiled=True)  106 us
    psum x1, waiting for transfers between devices, scatter(): lax.psum(lax.psum_scatter(g, 'fsdp', scatter_dimension=0, tiled=True), 'dp')  77.5 us
    all_gather x4, waiting for transfers between devices, gather(): return lax.all_gather(x, 'fsdp', axis=0, tiled=True)  53.3 us
    pallas_call x1, Pallas kernels, backward_call(): pl.pallas_call(backward_kernel, out_shape=[jax.ShapeDtypeStruct((count, 3...  52.5 us
    pallas_call x1, Pallas kernels, forward_call(): pl.pallas_call(forward_kernel, out_shape=[jax.ShapeDtypeStruct((count, wi...  42.8 us
    psum x1, blocking collectives, local(): total = lax.psum(flat, ('dp', 'fsdp'))  42.2 us
    dot_general x1, matrix products, local(): d_act = jnp.einsum('nd,fd->nf', d_down, wdown, preferred_element_type=f32)  27.8 us
    dot_general x1, matrix products, local(): down = jnp.dot(act, wdown, preferred_element_type=f32) + bdown  15.7 us
  transfers between devices with their start and end apart: 9, of which 7 were waited for; matrix products, arithmetic and copies ran while one was open for 18% of the time, Pallas kernels for 17%

profile of v1, /device:TPU:0, one launch (start us, length us, event | category | flops | bytes accessed | tf_op | source)
XLA Modules:
  0.0 554.7 jit_solution(1266619298241135518)
XLA Ops:
  7.3 0.7 all-gather.6.cloned.1.call-update
  8.1 0.7 all-gather.8.cloned.1.call-update
  8.8 0.7 all-gather.10.cloned.1.call-update
  10.2 1.6 copy.55
  12.2 6.2 %all-gather = bf16[12288]{0:T(1024)(128)(2,1)S(1)} all-gather(bf16[3072]{0:T(1024)(128)(2,1)S(1)} %pad.10), channel_id=2, replica_groups=mesh['dp'=8,'fsdp'=4] {'fsdp'}, dimensions={0}, use_global_device_ids=true | all-gather | bytes 30720 | tf_op jit(solution)/shard_map/all_gather | solution.py:286
  18.9 1.6 copy.53
  20.5 0.7 slice.79.gain
  21.2 0.7 slice.81.shift
  22.1 0.6 pad_convert_fusion.table
  22.8 0.6 pad_add_fusion.pos
  23.4 19.8 %all-gather.6.cloned.1.call-done.wqkv = bf16[768,2304]{1,0:T(8,128)(2,1)} async-done(((bf16[192,2304]{1,0:T(8,128)(2,1)}), bf16[768,2304]{1,0:T(8,128)(2,1)}) %all-gather.6.cloned.1.call-update) | async-done | bytes 3538960 | tf_op jit(solution)/shard_map/all_gather | solution.py:255
  43.2 42.8 %attention_forward.1 = (bf16[1024,768]{1,0:T(8,128)(2,1)}, bf16[18,1024,128]{2,1,0:T(8,128)(2,1)}, bf16[1024,768]{1,0:T(8,128)(2,1)}, bf16[1024,128]{1,0:T(8,128...) custom-call(bf16[1024,768]{1,0:T(8,128)(2,1)} %tok.1, ...), custom_call_target="tpu_custom_call" | custom-call | tf_op jit(solution)/shard_map/attention_forward/pallas_call | solution.py:127
  85.9 5.6 %fusion.20 = (f32[1024]{0:T(1024)S(1)}, f32[1024,768]{0,1:T(8,128)S(1)}, f32[1024]{0:T(1024)S(1)}, f32[1024,768]{0,1:T(8,128)}) fusion(f32[768]{0:T(1024)S(1)} %mul.211, bf16[1024,768]{0,1:T(8,128)(2,1)} %copy.53, bf16[1024,768]{1,0:T(8,128)(2,1)} %get-tuple-element.24.att, bf16[768,768]{1,0:T(8,128)(2,1)} %all-gather.8.cloned.1.call-done), kind=kOutput, calls=%fused_computation.71 | convolution fusion | flops 1211889664 | bytes 10628096 | tf_op jit(solution)/shard_map/dot_general | solution.py:304
  91.9 9.4 %all-gather.10.cloned.1.call-done = bf16[768,3072]{1,0:T(8,128)(2,1)} async-done(((bf16[192,3072]{1,0:T(8,128)(2,1)}), bf16[768,3072]{1,0:T(8,128)(2,1)}) %all-gather.10.cloned.1.call-update) | async-done | bytes 4718608 | tf_op jit(solution)/shard_map/all_gather | solution.py:255
  101.3 14.8 %multiply_convert_fusion = (bf16[1024,3072]{1,0:T(8,128)(2,1)}, f32[1024,3072]{1,0:T(8,128)}) fusion(f32[3072]{0:T(1024)S(1)} %reshape.163, bf16[768,3072]{1,0:T(8,128)(2,1)} %all-gather.10.cloned.1.call-done, f32[1024,768]{0,1:T(8,128)S(1)} %get-tuple-element.101, f32[768]{0:T(1024)S(1)} %add.103, f32[768]{0:T(1024)S(1)} %mul.219, f32[1024]{0:T(1024)S(1)} %fusion.16, ...), kind=kOutput, calls=%fused_computation.10 | convolution fusion | flops 4867227648 | bytes 26765312 | tf_op jit(solution)/shard_map/dot_general | solution.py:307
  116.1 24.1 %all-gather.12.cloned.1.call-done = bf16[3072,768]{1,0:T(8,128)(2,1)} async-done(((bf16[768,768]{1,0:T(8,128)(2,1)}), bf16[3072,768]{1,0:T(8,128)(2,1)}) %all-gather.12.cloned.1.call-update) | async-done | bytes 4718608 | tf_op jit(solution)/shard_map/all_gather | solution.py:255
  140.2 27.8 %convert_reduce_fusion = (f32[3072]{0:T(1024)S(1)}, bf16[1024,3072]{1,0:T(8,128)(2,1)S(1)}) fusion(f32[1024,3072]{1,0:T(8,128)} %get-tuple-element.116, f32[3072]{0:T(1024)S(1)} %reshape.163, bf16[3072,768]{1,0:T(8,128)(2,1)} %all-gather.12.cloned.1.call-done, bf16[1024,768]{0,1:T(8,128)(2,1)} %copy.55, f32[1024]{0:T(1024)S(1)} %compare_convert_fusion, ...), kind=kOutput, calls=%fused_computation.9 | convolution fusion | flops 4907332608 | bytes 25197568 | tf_op jit(solution)/shard_map/nd,fd->nf/dot_general | solution.py:316
  168.1 6.8 %fusion.23 = (f32[768]{0:T(1024)S(1)}, f32[1024,768]{1,0:T(8,128)}) fusion(bf16[1024,3072]{1,0:T(8,128)(2,1)S(1)} %get-tuple-element.118, bf16[768,3072]{1,0:T(8,128)(2,1)S(1)} %copy-done.17), kind=kOutput, calls=%fused_computation.74 | convolution fusion | flops 4832623616 | bytes 14158848 | tf_op jit(solution)/shard_map/nf,df->nd/dot_general | solution.py:321
  174.9 3.6 copy.56
  178.5 3.0 multiply_reduce_fusion.1
  181.5 0.9 fusion.19
  182.9 0.6 multiply_convert_fusion.1
  183.5 0.6 copy-done.2
  184.0 1.1 copy-done.8
  185.2 2.5 convolution_convert_fusion.4
  187.7 4.3 convolution_convert_fusion.3.datt
  192.0 52.5 %attention_backward.1 = (bf16[1024,2304]{1,0:T(8,128)(2,1)}, f32[6,2,128]{2,1,0:T(2,128)}) custom-call(s32[3,8,128]{2,1,0:T(8,128)} %pad_add_fusion.pos, bf16[18,1024,128]{2,1,0:T(8,128)(2,1)} %get-tuple-element.25.qkv, bf16[1024,128]{1,0:T(8,128)(2,1)} %get-tuple-element.26.ext, bf16[1024,128]{1,0:T(8,128)(2,1)} %get-tuple-element.27.hot, ...), custom_call_target="tpu_custom_call" | custom-call | tf_op jit(solution)/shard_map/attention_backward/pallas_call | solution.py:230
  244.6 8.6 %convolution_convert_fusion.2 = bf16[768,2304]{1,0:T(8,128)(2,1)} fusion(bf16[1024,768]{1,0:T(8,128)(2,1)} %get-tuple-element.32, bf16[1024,2304]{1,0:T(8,128)(2,1)} %get-tuple-element.30), kind=kOutput, calls=%fused_computation.13 | convolution fusion | flops 3625648128 | bytes 9830400 | tf_op jit(solution)/shard_map/nd,nc->dc/dot_general | solution.py:330
  253.2 9.8 %convolution_convert_fusion.1 = bf16[768,3072]{1,0:T(8,128)(2,1)} fusion(bf16[1024,3072]{1,0:T(8,128)(2,1)} %copy-done.25, f32[1024,768]{0,1:T(8,128)S(1)} %get-tuple-element.101, f32[768]{0:T(1024)S(1)} %add.103, f32[768]{0:T(1024)S(1)} %mul.219, f32[1024]{0:T(1024)S(1)} %fusion.16, f32[1024]{0:T(1024)S(1)} %broadcast_multiply_fusion.1), kind=kOutput, calls=%fused_computation.12 | convolution fusion | flops 4838129664 | bytes 14170112 | tf_op jit(solution)/shard_map/nd,nf->df/dot_general | solution.py:320
  263.1 9.5 %convolution_convert_fusion = bf16[3072,768]{1,0:T(8,128)(2,1)} fusion(bf16[1024,3072]{1,0:T(8,128)(2,1)} %get-tuple-element.115, bf16[1024,768]{0,1:T(8,128)(2,1)} %copy.55, f32[1024]{0:T(1024)S(1)} %compare_convert_fusion, f32[768]{0:T(1024)S(1)} %mul.214), kind=kOutput, calls=%fused_computation.11 | convolution fusion | flops 4837343232 | bytes 12590080 | tf_op jit(solution)/shard_map/nf,nd->fd/dot_general | solution.py:315
  273.0 8.9 %fusion.22 = (f32[768]{0:T(1024)S(1)}, f32[1024,768]{1,0:T(8,128)}) fusion(bf16[1024,2304]{1,0:T(8,128)(2,1)} %get-tuple-element.30, bf16[768,2304]{1,0:T(8,128)(2,1)} %all-gather.6.cloned.1.call-done.wqkv), kind=kOutput, calls=%fused_computation.73 | convolution fusion | flops 3624664320 | bytes 11406336 | tf_op jit(solution)/shard_map/nc,dc->nd/dot_general | solution.py:331
  281.9 3.5 copy.57
  285.7 3.1 fusion.11
  288.8 4.8 reduce-scatter.5.cloned.1.call-done
  293.7 50.4 %reduce-scatter.9.cloned.1.call-done = bf16[192,3072]{1,0:T(8,128)(2,1)} async-done(((bf16[768,3072]{1,0:T(8,128)(2,1)}), bf16[192,3072]{1,0:T(8,128)(2,1)}) %reduce-scatter.9.cloned.1.call-update) | async-done | bytes 1179664 | tf_op jit(solution)/shard_map/reduce_scatter | solution.py:338
  344.1 50.6 %reduce-scatter.11.cloned.1.call-done = bf16[768,768]{1,0:T(8,128)(2,1)} async-done(((bf16[3072,768]{1,0:T(8,128)(2,1)}), bf16[768,768]{1,0:T(8,128)(2,1)}) %reduce-scatter.11.cloned.1.call-update) | async-done | bytes 1179664 | tf_op jit(solution)/shard_map/reduce_scatter | solution.py:338
  394.7 3.8 fusion.14
  398.5 15.7 %multiply_reduce_fusion = (f32[768]{0:T(1024)S(1)}, f32[768]{0:T(1024)S(1)}, f32[768]{0:T(1024)S(1)}, bf16[1024,768]{0,1:T(8,128)(2,1)}, bf16[1024,768]{0,1:T(8,128)(2,1)}) fusion(bf16[1024,768]{0,1:T(8,128)(2,1)} %copy.55, f32[1024]{0:T(1024)S(1)} %compare_convert_fusion, f32[768]{0:T(1024)S(1)} %add.110, f32[768]{0:T(1024)S(1)} %mul.214, ...), kind=kOutput, calls=%fused_computation.27 | convolution fusion | flops 4852282368 | bytes 29927424 | tf_op jit(solution)/shard_map/dot_general | solution.py:309
  414.4 42.2 %psum.35 = f32[9960]{0:T(1024)S(1)} all-reduce(f32[9960]{0:T(1024)S(1)} %pad_maximum_fusion), channel_id=1, replica_groups=mesh['dp'=8,'fsdp'=4] {'dp','fsdp'}, use_global_device_ids=true, to_apply=%region_16.17 | all-reduce | flops 9960 | bytes 79680 | tf_op jit(solution)/shard_map/psum | solution.py:351
  456.7 2.6 copy.61
  459.3 1.6 copy.62
  460.9 0.7 dynamic_slice.11
  462.2 0.7 fusion.21
  462.8 77.5 %all-reduce.5.cloned.1.call-done = (bf16[192,2304]{1,0:T(8,128)(2,1)}, bf16[192,768]{1,0:T(8,128)(2,1)}, bf16[192,3072]{1,0:T(8,128)(2,1)}, bf16[768,768]{1,0:T(8,128)(2,1)}) async-done(((bf16[192,2304]{1,0:T(8,128)(2,1)}, bf16[192,768]{1,0:T(8,128)(2,1)}, bf16[192,3072]{1,0:T(8,128)(2,1)}, bf16[768,768]{1,0:T(8,128)(2,1)}), (bf16[192,2304]{1,0:T(8,128)(2,1)}, bf16[192,768]{1,0:T(8,128)(2,1)}, ...) | async-done | bytes 3538960 | tf_op jit(solution)/shard_map/psum | solution.py:338
  540.3 2.6 convert_element_type.111
  542.9 1.8 convert_element_type.113
  544.8 1.7 convert_element_type.115
  546.4 1.6 convert_element_type.117
  (122 shorter events, 4.4 us)
Async XLA Ops:
  7.2 3.0 copy-start.6
  7.2 4.6 copy-start.18
  7.2 4.6 copy-start.19
  7.2 4.6 copy-start.20
  7.2 4.6 copy-start.21
  7.2 4.6 copy-start.22
  7.2 4.7 copy-start.23
  7.3 4.7 copy-start.24
  7.3 4.8 copy-start.16
  7.3 4.9 copy-start.15
  7.3 35.9 %all-gather.6.cloned.1.call-start = ((), (), s32[]{:S(2)}) async-start(), calls=%async_computation.4 | async-start | bytes 4423680 | tf_op jit(solution)/shard_map/all_gather | solution.py:255
  8.0 10.9 %copy-start.3 = (bf16[1024,768]{1,0:T(8,128)(2,1)S(1)}, bf16[1024,768]{1,0:T(8,128)(2,1)}, u32[]{:S(2)}) copy-start(bf16[1024,768]{1,0:T(8,128)(2,1)} %tok.1) | copy-start | bytes 4718596
  8.0 77.9 %all-gather.8.cloned.1.call-start = ((), (), s32[]{:S(2)}) async-start(), calls=%async_computation.5 | async-start | bytes 1474560 | tf_op jit(solution)/shard_map/all_gather | solution.py:255
  8.8 92.5 %all-gather.10.cloned.1.call-start = ((), (), s32[]{:S(2)}) async-start(), calls=%async_computation.6 | async-start | bytes 5898240 | tf_op jit(solution)/shard_map/all_gather | solution.py:255
  9.5 130.7 %all-gather.12.cloned.1.call-start = ((), (), s32[]{:S(2)}) async-start(), calls=%async_computation.7 | async-start | bytes 5898240 | tf_op jit(solution)/shard_map/all_gather | solution.py:255
  10.1 12.7 %copy-start.11 = (s32[1024]{0:T(1024)S(1)}, s32[1024]{0:T(1024)}, u32[]{:S(2)}) copy-start(s32[1024]{0:T(1024)} %param.20) | copy-start | bytes 12292
  10.1 12.7 %copy-start.13 = (s32[1024]{0:T(1024)S(1)}, s32[1024]{0:T(1024)}, u32[]{:S(2)}) copy-start(s32[1024]{0:T(1024)} %param.22) | copy-start | bytes 12292
  10.1 12.6 %copy-start.14 = (s32[1024]{0:T(1024)S(1)}, s32[1024]{0:T(1024)}, u32[]{:S(2)}) copy-start(s32[1024]{0:T(1024)} %param.21) | copy-start | bytes 12292
  10.1 278.7 %reduce-scatter.7.cloned.1.call-start = ((), (), s32[]{:S(2)}) async-start(), calls=%async_computation.9 | async-start | bytes 1474560 | tf_op jit(solution)/shard_map/reduce_scatter | solution.py:338
  140.2 27.8 %copy-start.17 = (bf16[768,3072]{1,0:T(8,128)(2,1)S(1)}, bf16[768,3072]{1,0:T(8,128)(2,1)}, u32[]{:S(2)}) copy-start(bf16[768,3072]{1,0:T(8,128)(2,1)} %all-gather.10.cloned.1.call-done) | copy-start | bytes 14155780
  168.0 6.8 %copy-start.25 = (bf16[1024,3072]{1,0:T(8,128)(2,1)}, bf16[1024,3072]{1,0:T(8,128)(2,1)S(1)}, u32[]{:S(2)}) copy-start(bf16[1024,3072]{1,0:T(8,128)(2,1)S(1)} %get-tuple-element.118) | copy-start | bytes 18874372
  178.5 3.0 copy-start.1
  181.5 1.4 copy-start.4
  182.3 1.7 copy-start.2
  182.9 2.3 copy-start.5
  184.0 1.1 copy-start.8
  187.7 106.0 %reduce-scatter.5.cloned.1.call-start = ((), (), s32[]{:S(2)}) async-start(), calls=%async_computation.8 | async-start | bytes 4423680 | tf_op jit(solution)/shard_map/reduce_scatter | solution.py:338
  253.2 90.9 %reduce-scatter.9.cloned.1.call-start = ((), (), s32[]{:S(2)}) async-start(), calls=%async_computation.10 | async-start | bytes 5898240 | tf_op jit(solution)/shard_map/reduce_scatter | solution.py:338
  263.0 131.6 %reduce-scatter.11.cloned.1.call-start = ((), (), s32[]{:S(2)}) async-start(), calls=%async_computation.11 | async-start | bytes 5898240 | tf_op jit(solution)/shard_map/reduce_scatter | solution.py:338
  272.6 267.7 %all-reduce.5.cloned.1.call-start = ((), (), s32[]{:S(2)}) async-start(), calls=%async_computation.12 | async-start | bytes 7077888 | tf_op jit(solution)/shard_map/psum | solution.py:338
  281.9 3.5 copy-start.12
  394.7 3.8 copy-start
  414.2 45.0 %copy-start.7 = (bf16[1024,768]{0,1:T(8,128)(2,1)S(1)}, bf16[1024,768]{0,1:T(8,128)(2,1)}, u32[]{:S(2)}) copy-start(bf16[1024,768]{0,1:T(8,128)(2,1)} %get-tuple-element.102) | copy-start | bytes 4718596
  540.3 4.5 copy-start.10
  540.3 6.1 %copy-start.9 = (bf16[768,768]{1,0:T(8,128)(2,1)S(1)}, bf16[768,768]{1,0:T(8,128)(2,1)}, u32[]{:S(2)}) copy-start(bf16[768,768]{1,0:T(8,128)(2,1)} %get-tuple-element.97) | copy-start | bytes 3538948
Sparse Core Ops, SparseCore 0:
  9.7 33.4 all-gather.5
  44.7 17.4 all-gather.7
  63.8 37.4 all-gather.9
  102.7 37.4 all-gather.11
  187.8 25.7 reduce-scatter.6
  253.3 40.3 reduce-scatter.4
  296.2 47.8 reduce-scatter.8
  346.8 47.8 reduce-scatter.10
  398.6 141.6 all-reduce.4

commit v2 on v1

v2 whole, which is shorter than its diff:
```python
import functools

import jax
import jax.numpy as jnp
from jax import lax
from jax.experimental import pallas as pl
from jax.experimental.pallas import tpu as pltpu
from jax.sharding import PartitionSpec as P

F32 = jnp.float32
BF = jnp.bfloat16
NT = (((1,), (1,)), ((), ()))
NN = (((1,), (0,)), ((), ()))
VMEM = pl.BlockSpec(memory_space=pltpu.VMEM)
ANY = pl.BlockSpec(memory_space=pl.ANY)
MESH = pl.DeviceIdType.MESH
LIMIT = 63 << 20
MASKED = -1e30


def mm(a, b, dims=NN):
    return lax.dot_general(a, b, dims, preferred_element_type=F32)


def lanes(rows, width=128):
    return lax.broadcasted_iota(jnp.int32, (rows, width), 1)


def normalize(rows, gain, shift):
    center = rows - jnp.mean(rows, axis=-1, keepdims=True)
    spread = jnp.mean(center * center, axis=-1, keepdims=True)
    return center * lax.rsqrt(spread + 1e-06) * gain + shift


def pieces(x, lane):
    hi = x.astype(BF)
    rest = x - hi.astype(F32)
    mid = rest.astype(BF)
    low = (rest - mid.astype(F32)).astype(BF)
    third = lane % 3
    return jnp.where(third == 0, hi.astype(F32), jnp.where(third == 1, mid.astype(F32), low.astype(F32)))


def position_columns(pos, hot, page_q, page_k):
    for r in range(pos.shape[1]):
        code = (pos[0, r : r + 1, :] + 1) * 4096 + pos[1, r : r + 1, :] * 64 + pos[2, r : r + 1, :]
        code = jnp.broadcast_to(code.astype(F32), (128, 128)).T.astype(jnp.int32)
        lane = lanes(128)
        page, row, col = code >> 12, (code >> 6) & 63, code & 63
        near = lane & 63
        where = jnp.where(near < 32, row, col + 32)
        at = pl.ds(r * 128, 128)
        hot[at, :] = jnp.where(where == near, 1.0, 0.0).astype(BF)
        page_q[at, :] = jnp.where(page == lane, 1.0, 0.0)
        page_k[at, :] = jnp.where((lane < 6) & (page != lane), MASKED, 0.0).astype(BF)


def toeplitz(table, bias):
    lane = lanes(32)
    for p in range(bias.shape[0]):
        for axis in range(2):
            parts = []
            for head, at in ((2 * p + 1, 32 * axis), (2 * p, 64 + 32 * axis)):
                row = jnp.broadcast_to(table[2 * head + axis : 2 * head + axis + 1, :], (32, 128))
                rolled = pltpu.roll(row, (97 + at) % 128, axis=1, stride=1, stride_axis=0)
                parts.append(jnp.where((lane >= at) & (lane < at + 32), rolled, 0.0))
            bias[p, 32 * axis : 32 * axis + 32, :] = (parts[0] + parts[1]).astype(BF)


def forward_kernel(tok, pos, gain, shift, table, wqkv, norm, qkv, att, ext, hot, page_k, bias, lse, ka, va):
    count, width = tok.shape
    pairs = bias.shape[0]
    position_columns(pos, hot, lse, page_k)
    toeplitz(table, bias)

    @pl.loop(0, count // 256)
    def _(b):
        at = pl.ds(pl.multiple_of(b * 256, 256), 256)
        rows = normalize(tok[at, :].astype(F32), gain[...], shift[...]).astype(BF)
        norm[:, at] = rows.T
        for part in range(3):
            block = mm(rows, wqkv[:, part * width : (part + 1) * width]).astype(BF)
            if part == 0:
                block = block * jnp.asarray(0.125, BF)
            for p in range(pairs):
                qkv[part * pairs + p, at, :] = block[:, p * 128 : (p + 1) * 128]

    low_half = lanes(count) < 64

    @pl.loop(0, pairs)
    def _(p):
        keys, values = qkv[pairs + p], qkv[2 * pairs + p]
        side = mm(hot[:, :64], bias[p]).astype(BF)
        one = jnp.ones_like(values)
        ka[0, :, :128] = jnp.where(low_half, keys, side)
        ka[1, :, :128] = jnp.where(low_half, side, keys)
        va[0] = jnp.where(low_half, values, one)
        va[1] = jnp.where(low_half, one, values)
        for e in range(2):
            ka[e, :, 128:] = page_k[...]

        @pl.loop(0, count // 256)
        def _(b):
            at = pl.ds(pl.multiple_of(b * 256, 256), 256)
            queries, places = qkv[p, at, :], hot[at, :]
            kept = lse[at, :]
            lane = lanes(256)
            half = lane < 64
            page_hot = jnp.where(lane < 6, kept, 0.0).astype(BF)
            outs = []
            for e in range(2):
                first = jnp.where(half, queries, places) if e == 0 else jnp.where(half, places, queries)
                scores = mm(jnp.concatenate([first, page_hot], axis=1), ka[e], NT)
                top = jnp.max(scores, axis=1, keepdims=True)
                expo = jnp.exp(scores - top).astype(BF)
                out = mm(expo, va[e])
                turned = pltpu.roll(out, 64, axis=1)
                total = jnp.where(half, turned, out) if e == 0 else jnp.where(half, out, turned)
                outs.append(out / total)
                kept = jnp.where(lane // 3 == 2 + 2 * p + e, top + jnp.log(total), kept)
            lse[at, :] = kept
            att[at, pl.ds(pl.multiple_of(p * 128, 128), 128)] = jnp.where(half, outs[0], outs[1]).astype(BF)

    lane = lanes(count)
    ext[...] = jnp.where(lane < 6, lse[...], pieces(lse[...], lane)).astype(BF)


def forward_call(tok, pos, gain, shift, table, wqkv):
    count, width = tok.shape
    pairs = width // 128
    return pl.pallas_call(
        forward_kernel,
        out_shape=[
            jax.ShapeDtypeStruct((width, count), BF),
            jax.ShapeDtypeStruct((3 * pairs, count, 128), BF),
            jax.ShapeDtypeStruct((count, width), BF),
            jax.ShapeDtypeStruct((count, 128), BF),
            jax.ShapeDtypeStruct((count, 128), BF),
            jax.ShapeDtypeStruct((count, 128), BF),
            jax.ShapeDtypeStruct((pairs, 64, 128), BF),
        ],
        in_specs=[VMEM] * 6,
        out_specs=[VMEM] * 7,
        scratch_shapes=[
            pltpu.VMEM((count, 128), F32),
            pltpu.VMEM((2, count, 256), BF),
            pltpu.VMEM((2, count, 128), BF),
        ],
        compiler_params=pltpu.CompilerParams(vmem_limit_bytes=LIMIT),
        name="attention_forward",
    )(tok, pos, gain, shift, table, wqkv)


class Links:
    def __init__(self, ndp):
        self.dp, self.f = lax.axis_index("dp"), lax.axis_index("fsdp")
        self.core, self.x = self.f % 2, self.f // 2
        self.bits = ndp.bit_length() - 1
        self.bit = [(self.dp // 2**k) % 2 for k in range(self.bits)]

    def partner(self, kind, k=0):
        if kind == "core":
            return (self.dp, self.f + 1 - 2 * self.core)
        if kind == "x":
            return (self.dp, self.f + 2 - 4 * self.x)
        return (self.dp + (1 - 2 * self.bit[k]) * 2**k, self.f)

    def everyone(self):
        return [self.partner("core"), self.partner("x")] + [self.partner("dp", k) for k in range(self.bits)]

    def greet(self):
        barrier = pltpu.get_barrier_semaphore()
        for other in self.everyone():
            pl.semaphore_signal(barrier, inc=1, device_id=other, device_id_type=MESH)
        pl.semaphore_wait(barrier, self.bits + 2)


def remote(src, dst, send, recv, device):
    return pltpu.make_async_remote_copy(
        src_ref=src, dst_ref=dst, send_sem=send, recv_sem=recv, device_id=device, device_id_type=MESH
    )


def pick_index(n, table):
    out = 0
    for i, v in enumerate(table):
        if v:
            out = out + jnp.where(n == i, v, 0)
    return out


class Reduction:
    def __init__(self, links, order, parts, own, acc, bufs, total_h, load_sem, send_sem, recv_sem, out_sem):
        self.l, self.order, self.parts, self.own, self.acc, self.bufs = links, order, parts, own, acc, bufs
        self.total_h, self.load_sem, self.send_sem, self.recv_sem, self.out_sem = (
            total_h,
            load_sem,
            send_sem,
            recv_sem,
            out_sem,
        )
        self.halvings = min(3, links.bits)
        self.extra = links.bits - self.halvings
        self.stages = 2 + 2 * self.halvings + self.extra
        self.kept = (links.x,) + tuple(links.bit[: self.halvings])

    def source(self, n):
        mine = pick_index(n, [i for _, i in self.order])
        return mine, sum(jnp.where(n == i, 1, 0) for i, (kind, _) in enumerate(self.order) if kind == "q")

    def copy(self, k, n):
        l, h = self.l, self.halvings
        sems = (self.send_sem.at[k, n], self.recv_sem.at[k, n])
        if k == 1:
            return remote(self.acc.at[n, 1 - l.x], self.bufs[1].at[n], *sems, l.partner("x"))
        if k < 2 + h:
            j = k - 2
            at = (n,) + self.kept[: 1 + j] + (1 - l.bit[j],)
            return remote(self.acc.at[at], self.bufs[2 + j].at[n], *sems, l.partner("dp", j))
        if k < 2 + h + self.extra:
            j = k - 2
            src = self.bufs[2 + j - 1] if j > h else None
            at = (n,) + self.kept[1:]
            src = self.bufs[1].at[at] if j == h else self.bufs[1].at[at]
            return remote(src, self.bufs[2 + j].at[n], *sems, l.partner("dp", j))
        j = h - 1 - (k - 2 - h - self.extra)
        at = (n,) + self.kept[1 : 2 + j]
        return remote(self.bufs[1].at[at], self.bufs[1].at[at], *sems, l.partner("dp", j))

    def first(self, n, act):
        l = self.l
        mine, is_own = self.source(n)
        sems = (self.send_sem.at[0, n], self.recv_sem.at[0, n])

        def both(home):
            act(
                lambda: remote(home.at[mine, 1 - l.core], self.bufs[0].at[n], *sems, l.partner("core")),
                lambda: pltpu.make_async_copy(home.at[mine, l.core], self.acc.at[n], self.load_sem.at[n]),
            )

        @pl.when(is_own == 0)
        def _():
            both(self.parts)

        @pl.when(is_own == 1)
        def _():
            both(self.own)

    def out(self, n):
        return pltpu.make_async_copy(self.bufs[1].at[n], self.total_h.at[n], self.out_sem.at[n])

    def step(self, k, n):
        h = self.halvings
        if k == 0:

            def start(send, load):
                send().start()
                load().start()

            self.first(n, start)
            return
        if k == 1:

            def arrive(send, load):
                send().wait_recv()
                load().wait()

            self.first(n, arrive)
            self.acc[n] = self.acc[n] + self.bufs[0][n]
        elif k <= 1 + h:
            self.copy(k - 1, n).wait_recv()
            at = (n,) + self.kept[: k - 1]
            self.acc[at] = self.acc[at] + self.bufs[k - 1][n]
        elif k == 2 + h:
            self.copy(k - 1, n).wait_recv()
            self.bufs[1][(n,) + self.kept[1:]] = self.acc[(n,) + self.kept] + self.bufs[k - 1][n]
        elif k <= 2 + h + self.extra:
            self.copy(k - 1, n).wait()
            at = (n,) + self.kept[1:]
            self.bufs[1][at] = self.bufs[1][at] + self.bufs[k - 1][n]
        else:
            self.copy(k - 1, n).wait_recv()
        if k < self.stages:
            self.copy(k, n).start()
        else:
            self.out(n).start()

    def tick(self, t, period, lags):
        for k in reversed(range(self.stages + 1)):
            m = t - lags[k] + 64 * period
            n = m // period - 64

            @pl.when((m % period == 0) & (n >= 0) & (n < len(self.order)))
            def _(k=k, n=n):
                self.step(k, n)

    def finish(self):
        @pl.loop(0, len(self.order))
        def _(n):
            self.first(n, lambda send, load: send().wait_send())
            for k in range(1, self.stages):
                if not 2 + self.halvings <= k < 2 + self.halvings + self.extra:
                    self.copy(k, n).wait_send()
            self.out(n).wait()


ORDER = [("g", 0), ("g", 1), ("g", 2), ("q", 0), ("g", 3), ("g", 4), ("q", 1), ("g", 5), ("q", 2), ("g", 6), ("g", 7), ("g", 8)]
PERIOD = 3


def lag_list(stages, extra):
    lags = [0, 1, 5]
    while len(lags) < stages + 1:
        lags.append(lags[-1] + 2)
    return lags


def backward_kernel(
    ndp,
    pos,
    vec,
    small_in,
    qkv_h,
    ext_h,
    hot_h,
    page_k_h,
    bias,
    dext_h,
    datt_h,
    normt_h,
    wq_h,
    tok_h,
    dmid_h,
    parts_h,
    gtok_h,
    total_h,
    small_out,
    qkv,
    ext,
    hot,
    page_k,
    dext,
    datt,
    normt,
    wq,
    tok,
    dmid,
    gtok,
    dqkv,
    qa,
    ka,
    va,
    doa,
    kt,
    dqt,
    hot_t,
    square,
    dtab,
    own,
    acc,
    b0,
    b1,
    b2,
    b3,
    b4,
    more,
    small_acc,
    small_recv,
    in_sem,
    gt_sem,
    load_sem,
    send_sem,
    recv_sem,
    out_sem,
    small_send,
    small_got,
):
    count, width = tok.shape
    pairs = bias.shape[0]
    blocks = count // 256
    loads = []
    for i, (src, dst) in enumerate(
        [
            (qkv_h, qkv),
            (ext_h, ext),
            (hot_h, hot),
            (page_k_h, page_k),
            (dext_h, dext),
            (datt_h, datt),
            (normt_h, normt),
            (wq_h, wq),
            (tok_h, tok),
            (dmid_h, dmid),
        ]
    ):
        copy = pltpu.make_async_copy(src, dst, in_sem.at[i])
        copy.start()
        loads.append(copy)
    links = Links(ndp)
    links.greet()
    bufs = [b0, b1, b2, b3, b4] + [more.at[k] for k in range(max(0, links.bits - 3))]
    red = Reduction(links, ORDER, parts_h, own, acc, bufs, total_h, load_sem, send_sem, recv_sem, out_sem)
    lags = lag_list(red.stages, red.extra)

    for r in range(pos.shape[1]):
        want = 31 - lax.broadcasted_iota(jnp.int32, (32, 128), 0)
        for axis in range(2):
            have = jnp.broadcast_to(pos[1 + axis, r : r + 1, :], (32, 128))
            hot_t[32 * axis : 32 * axis + 32, r * 128 : r * 128 + 128] = jnp.where(have == want, 1.0, 0.0).astype(BF)
    small_acc[0] = small_in[...]
    low_half = lanes(count) < 64
    third = lanes(count) // 3
    for copy in loads[:6]:
        copy.wait()

    @pl.loop(0, pairs // 2)
    def _(g):
        @pl.loop(0, 2)
        def _(s):
            p = 2 * g + s
            queries, keys, values = qkv[p], qkv[pairs + p], qkv[2 * pairs + p]
            side = mm(hot[:, :64], bias[p]).astype(BF)
            zero = jnp.zeros_like(values)
            places = hot[...]
            qa[0, :, :128] = jnp.where(low_half, queries, places)
            qa[1, :, :128] = jnp.where(low_half, places, queries)
            ka[0, :, :128] = jnp.where(low_half, keys, side)
            ka[1, :, :128] = jnp.where(low_half, side, keys)
            va[0, :, :128] = jnp.where(low_half, values, zero)
            va[1, :, :128] = jnp.where(low_half, zero, values)
            for e in range(2):
                head = 2 * p + e
                qa[e, :, 128:] = ext[...]
                ka[e, :, 128:] = jnp.where(third == 2 + head, -1.0, page_k[...].astype(F32)).astype(BF)
                va[e, :, 128:] = jnp.where(third == head, 1.0, 0.0).astype(BF)
            doa[:, :128] = datt[:, pl.ds(pl.multiple_of(p * 128, 128), 128)]
            doa[:, 128:] = dext[...]
            kt[...] = keys.T
            dqt[...] = jnp.zeros_like(dqt)
            square[...] = jnp.zeros_like(square)

            @pl.loop(0, blocks)
            def _(b):
                red.tick(p * blocks + b, PERIOD, lags)
                at = pl.ds(pl.multiple_of(b * 256, 256), 256)
                dks, dvs = [], []
                for e in range(2):
                    prob = jnp.exp(mm(ka[e, at, :], qa[e], NT))
                    d_prob = mm(va[e, at, :], doa[...], NT)
                    d_scores = (prob * d_prob).astype(BF)
                    dvs.append(mm(prob.astype(BF), doa[:, :128]))
                    dks.append(mm(d_scores, qa[e, :, :128]))
                    dqt[64 * e : 64 * e + 64, :] += mm(kt[64 * e : 64 * e + 64, at], d_scores)
                half = lanes(256) < 64
                dqkv[g, at, pl.ds(pl.multiple_of(256 + s * 128, 128), 128)] = jnp.where(half, dks[0], dks[1]).astype(BF)
                dqkv[g, at, pl.ds(pl.multiple_of(512 + s * 128, 128), 128)] = jnp.where(half, dvs[0], dvs[1]).astype(BF)
                part = jnp.where(half, dks[1], dks[0])
                hi = part.astype(BF)
                low = (part - hi.astype(F32)).astype(BF)
                both = mm(hot_t[:, at], jnp.concatenate([hi, low], axis=1))
                square[...] += both[:, :128] + both[:, 128:]

            dqkv[g, :, pl.ds(pl.multiple_of(s * 128, 128), 128)] = (dqt[...].T * 0.125).astype(BF)
            near = lanes(32) & 63
            for axis in range(2):
                part = square[32 * axis : 32 * axis + 32, :]
                part = jnp.where((near >= 32) if axis else (near < 32), part, 0.0)
                rolled = pltpu.roll(part, 96 * axis, axis=1, stride=1, stride_axis=0)
                dtab[p, axis : axis + 1, :] = jnp.sum(rolled, axis=0, keepdims=True)

        @pl.when(g == 0)
        def _():
            for copy in loads[6:]:
                copy.wait()

        value = mm(normt[...], dqkv[g])
        for f in range(4):
            for r in range(4):
                for c in range(2):
                    rows = slice(192 * f + 48 * r, 192 * f + 48 * r + 48)
                    own[g, f % 2, f // 2, c, r // 2, r % 2] = value[rows, 384 * c : 384 * c + 384].astype(BF)

    for p in range(pairs):
        small_acc[0, 12 + 2 * p : 14 + 2 * p, 0:128] = dtab[p]

    def gtok_out(b):
        at = pl.ds(pl.multiple_of(b * 256, 256), 256)
        return pltpu.make_async_copy(gtok.at[at, :], gtok_h.at[at, :], gt_sem.at[b])

    first_tick = pairs * blocks

    @pl.loop(0, blocks)
    def _(b):
        red.tick(first_tick + b, PERIOD, lags)
        at = pl.ds(pl.multiple_of(b * 256, 256), 256)
        d_norm = mm(dqkv[0, at, :], wq[0], NT)
        for g in range(1, pairs // 2):
            d_norm += mm(dqkv[g, at, :], wq[g], NT)
        rows = tok[at, :].astype(F32)
        center = rows - jnp.mean(rows, axis=-1, keepdims=True)
        scale = lax.rsqrt(jnp.mean(center * center, axis=-1, keepdims=True) + 1e-06)
        unit = center * scale
        small_acc[0, 0:1, :] += jnp.sum(d_norm * unit, axis=0, keepdims=True)
        small_acc[0, 1:2, :] += jnp.sum(d_norm, axis=0, keepdims=True)
        d_unit = d_norm * vec[0:1, :]
        back = scale * (
            d_unit - jnp.mean(d_unit, axis=-1, keepdims=True) - unit * jnp.mean(d_unit * unit, axis=-1, keepdims=True)
        )
        gtok[at, :] = (dmid[at, :] + back).astype(BF)
        gtok_out(b).start()

    others = links.everyone()

    def small_copy(i):
        return remote(small_acc.at[i], small_recv.at[i], small_send.at[i], small_got.at[i], others[i])

    small_copy(0).start()
    at_tick = first_tick + blocks
    for i in range(len(others)):
        red.tick(at_tick + i, PERIOD, lags)
        small_copy(i).wait_recv()
        small_acc[i + 1] = small_acc[i] + small_recv[i]
        if i + 1 < len(others):
            small_copy(i + 1).start()
    small_out[...] = small_acc[len(others)]
    at_tick = at_tick + len(others)
    last = PERIOD * (len(ORDER) - 1) + lags[-1] + 1

    @pl.loop(at_tick, last)
    def _(t):
        red.tick(t, PERIOD, lags)

    red.finish()
    for i in range(len(others)):
        small_copy(i).wait_send()
    for b in range(blocks):
        gtok_out(b).wait()


def backward_call(ndp, pos, vec, small, qkv, ext, hot, page_k, bias, dext, datt, normt, wq, tok, dmid, parts):
    count, width = datt.shape
    bits = ndp.bit_length() - 1
    n = len(ORDER)
    stages = 2 + 2 * min(3, bits) + max(0, bits - 3)
    tall = pltpu.VMEM((count, width), BF)
    side = pltpu.VMEM((count, 128), BF)
    pair = pltpu.VMEM((2, count, 256), BF)
    return pl.pallas_call(
        functools.partial(backward_kernel, ndp),
        out_shape=[
            jax.ShapeDtypeStruct((count, width), BF),
            jax.ShapeDtypeStruct((n, 2, 2, 2, 48, 384), BF),
            jax.ShapeDtypeStruct(small.shape, F32),
        ],
        in_specs=[VMEM] * 3 + [ANY] * 4 + [VMEM] + [ANY] * 7,
        out_specs=[ANY] * 2 + [VMEM],
        scratch_shapes=[
            pltpu.VMEM(qkv.shape, BF),
            side,
            side,
            side,
            side,
            tall,
            pltpu.VMEM((width, count), BF),
            pltpu.VMEM(wq.shape, BF),
            tall,
            pltpu.VMEM((count, width), F32),
            tall,
            pltpu.VMEM((3, count, width), BF),
            pair,
            pair,
            pair,
            pltpu.VMEM((count, 256), BF),
            pltpu.VMEM((128, count), BF),
            pltpu.VMEM((128, count), F32),
            pltpu.VMEM((64, count), BF),
            pltpu.VMEM((64, 128), F32),
            pltpu.VMEM((width // 128, 2, 128), F32),
            pltpu.VMEM((3, 2, 2, 2, 2, 2, 48, 384), BF),
            pltpu.VMEM((n, 2, 2, 2, 2, 48, 384), BF),
            pltpu.VMEM((n, 2, 2, 2, 2, 48, 384), BF),
            pltpu.VMEM((n, 2, 2, 2, 48, 384), BF),
            pltpu.VMEM((n, 2, 2, 48, 384), BF),
            pltpu.VMEM((n, 2, 48, 384), BF),
            pltpu.VMEM((n, 48, 384), BF),
            pltpu.VMEM((max(1, bits - 3), n, 48, 384) if bits > 3 else (1, 1, 8, 128), BF),
            pltpu.VMEM((bits + 3,) + small.shape, F32),
            pltpu.VMEM((bits + 2,) + small.shape, F32),
            pltpu.SemaphoreType.DMA((10,)),
            pltpu.SemaphoreType.DMA((count // 256,)),
            pltpu.SemaphoreType.DMA((n,)),
            pltpu.SemaphoreType.DMA((stages, n)),
            pltpu.SemaphoreType.DMA((stages, n)),
            pltpu.SemaphoreType.DMA((n,)),
            pltpu.SemaphoreType.DMA((bits + 2,)),
            pltpu.SemaphoreType.DMA((bits + 2,)),
        ],
        compiler_params=pltpu.CompilerParams(vmem_limit_bytes=LIMIT, collective_id=1, has_side_effects=True),
        name="backward",
    )(pos, vec, small, qkv, ext, hot, page_k, bias, dext, datt, normt, wq, tok, dmid, parts)


def block_columns(ref, at, start, size=768):
    return ref[at, start : start + size]


def gelu_both(u):
    c = 0.7978845608028654
    square = u * u
    t = jnp.tanh(c * u * (1.0 + 0.044715 * square))
    half = 0.5 + 0.5 * t
    slope = half + (0.5 * c) * u * (1.0 - t * t) * (1.0 + 0.134145 * square)
    return u * half, slope


def middle_kernel(
    tok_h,
    cot_h,
    att_h,
    ext_h,
    vec,
    wout_h,
    wup_h,
    wdown_h,
    layer_h,
    dmid_h,
    datt_h,
    dext_h,
    part_h,
    small,
    tok,
    cot,
    att,
    ext,
    wout,
    wup,
    wdown,
    act,
    dup,
    n2t,
    ddt,
    att_t,
    dproj,
    slope,
    layer,
    dmid,
    datt,
    dext,
    stage,
    in_sem,
    out_sem,
    part_sem,
):
    count, width = tok.shape
    ff = wup.shape[1]
    cols = ff // width
    loads = []
    for i, (src, dst) in enumerate(
        [(att_h, att), (wout_h, wout), (tok_h, tok), (wup_h, wup), (wdown_h, wdown), (cot_h, cot), (ext_h, ext)]
    ):
        copy = pltpu.make_async_copy(src, dst, in_sem.at[i])
        copy.start()
        loads.append(copy)
    small[...] = jnp.zeros_like(small)
    head = lax.broadcasted_iota(jnp.int32, (width, 128), 0) // 64
    pick = jnp.where(lanes(width) // 3 == head, 1.0, 0.0).astype(BF)
    for copy in loads:
        copy.wait()

    def outs(b):
        at = pl.ds(pl.multiple_of(b * 256, 256), 256)
        return [
            pltpu.make_async_copy(src.at[at, :], dst.at[at, :], out_sem.at[i, b])
            for i, (src, dst) in enumerate([(layer, layer_h), (dmid, dmid_h), (datt, datt_h), (dext, dext_h)])
        ]

    @pl.loop(0, count // 256)
    def _(b):
        at = pl.ds(pl.multiple_of(b * 256, 256), 256)
        rows_att = att[at, :]
        proj = mm(rows_att, wout[...])
        mid = tok[at, :].astype(F32) + vec[2:3, :] * proj
        center = mid - jnp.mean(mid, axis=-1, keepdims=True)
        scale = lax.rsqrt(jnp.mean(center * center, axis=-1, keepdims=True) + 1e-06)
        unit = center * scale
        norm = (unit * vec[3:4, :] + vec[4:5, :]).astype(BF)
        down = jnp.zeros((256, width), F32)
        for j in range(cols):
            u = mm(norm, wup[:, j * width : (j + 1) * width]) + vec[8 + j : 9 + j, :]
            a, s = gelu_both(u)
            a = a.astype(BF)
            act[at, j * width : (j + 1) * width] = a
            slope[:, j * width : (j + 1) * width] = s
            down += mm(a, wdown[j * width : (j + 1) * width, :])
        down += vec[5:6, :]
        layer[at, :] = (mid + vec[6:7, :] * down).astype(BF)
        grad = cot[at, :].astype(F32) * (1.0 - ext[at, :].astype(F32)[:, 0:1])
        d_down = (grad * vec[6:7, :]).astype(BF)
        small[6:7, :] += jnp.sum(grad * down, axis=0, keepdims=True)
        small[5:6, :] += jnp.sum(d_down.astype(F32), axis=0, keepdims=True)
        d_norm = jnp.zeros((256, width), F32)
        for j in range(cols):
            d_act = mm(d_down, wdown[j * width : (j + 1) * width, :], NT)
            d_up = (d_act * slope[:, j * width : (j + 1) * width]).astype(BF)
            dup[at, j * width : (j + 1) * width] = d_up
            small[8 + j : 9 + j, :] += jnp.sum(d_up.astype(F32), axis=0, keepdims=True)
            d_norm += mm(d_up, wup[:, j * width : (j + 1) * width], NT)
        small[3:4, :] += jnp.sum(d_norm * unit, axis=0, keepdims=True)
        small[4:5, :] += jnp.sum(d_norm, axis=0, keepdims=True)
        d_unit = d_norm * vec[3:4, :]
        d_mid = grad + scale * (
            d_unit
            - jnp.mean(d_unit, axis=-1, keepdims=True)
            - unit * jnp.mean(d_unit * unit, axis=-1, keepdims=True)
        )
        dmid[at, :] = d_mid
        small[2:3, :] += jnp.sum(d_mid * proj, axis=0, keepdims=True)
        d_proj = (d_mid * vec[2:3, :]).astype(BF)
        dproj[at, :] = d_proj
        d_att = mm(d_proj, wout[...], NT).astype(BF)
        datt[at, :] = d_att
        prod = rows_att.astype(F32) * d_att.astype(F32)
        hi = prod.astype(BF)
        low = (prod - hi.astype(F32)).astype(BF)
        dext[at, :] = pieces(-(mm(hi, pick) + mm(low, pick)), lanes(256)).astype(BF)
        n2t[:, at] = norm.T
        ddt[:, at] = d_down.T
        att_t[:, at] = rows_att.T
        for copy in outs(b):
            copy.start()

    def put(slot, value):
        for i in range(4):
            for r in range(4):
                for c in range(2):
                    rows = slice(192 * i + 48 * r, 192 * i + 48 * r + 48)
                    stage[slot, i, c, r // 2, r % 2] = value[rows, 384 * c : 384 * c + 384].astype(BF)

    def sends(kind, j, slot):
        copies = []
        for i in range(4):
            if kind == 0:
                chunk, f = i, j
            elif kind == 1:
                chunk, f = 4 + j, i
            else:
                chunk, f = 8, i
            copies.append(pltpu.make_async_copy(stage.at[slot, i], part_h.at[chunk, f & 1, f >> 1], part_sem.at[slot, i]))
        return copies

    @pl.loop(0, cols)
    def _(j):
        col = pl.ds(pl.multiple_of(j * width, width), width)

        @pl.when(j > 0)
        def _():
            for copy in sends(0, j - 1, 0):
                copy.wait()

        put(0, mm(ddt[...], act[:, col]))
        for copy in sends(0, j, 0):
            copy.start()

        @pl.when(j > 0)
        def _():
            for copy in sends(1, j - 1, 1):
                copy.wait()

        put(1, mm(n2t[...], dup[:, col]))
        for copy in sends(1, j, 1):
            copy.start()

    for copy in sends(0, cols - 1, 0):
        copy.wait()
    put(0, mm(att_t[...], dproj[...]))
    for copy in sends(2, 0, 0):
        copy.start()
    for copy in sends(1, cols - 1, 1) + sends(2, 0, 0):
        copy.wait()
    for b in range(count // 256):
        for copy in outs(b):
            copy.wait()


def middle_call(tok, cot, att, ext, vec, wout, wup, wdown):
    count, width = tok.shape
    ff = wup.shape[1]
    tall = pltpu.VMEM((count, width), BF)
    wide = pltpu.VMEM((width, count), BF)
    return pl.pallas_call(
        middle_kernel,
        out_shape=[
            jax.ShapeDtypeStruct((count, width), BF),
            jax.ShapeDtypeStruct((count, width), F32),
            jax.ShapeDtypeStruct((count, width), BF),
            jax.ShapeDtypeStruct((count, 128), BF),
            jax.ShapeDtypeStruct((9, 2, 2, 2, 2, 2, 48, 384), BF),
            jax.ShapeDtypeStruct((24, width), F32),
        ],
        in_specs=[ANY] * 4 + [VMEM] + [ANY] * 3,
        out_specs=[ANY] * 5 + [VMEM],
        scratch_shapes=[
            tall,
            tall,
            tall,
            pltpu.VMEM((count, 128), BF),
            pltpu.VMEM(wout.shape, BF),
            pltpu.VMEM(wup.shape, BF),
            pltpu.VMEM(wdown.shape, BF),
            pltpu.VMEM((count, ff), BF),
            pltpu.VMEM((count, ff), BF),
            wide,
            wide,
            wide,
            tall,
            pltpu.VMEM((256, ff), F32),
            tall,
            pltpu.VMEM((count, width), F32),
            tall,
            pltpu.VMEM((count, 128), BF),
            pltpu.VMEM((2, 4, 2, 2, 2, 48, 384), BF),
            pltpu.SemaphoreType.DMA((7,)),
            pltpu.SemaphoreType.DMA((4, count // 256)),
            pltpu.SemaphoreType.DMA((2, 4)),
        ],
        compiler_params=pltpu.CompilerParams(vmem_limit_bytes=LIMIT),
        name="middle",
    )(tok, cot, att, ext, vec, wout, wup, wdown)


def gather(x):
    return lax.all_gather(x, "fsdp", axis=0, tiled=True)


def local(
    tokens,
    cotangent,
    page_id,
    pos_row,
    pos_col,
    ln1_gain,
    ln1_shift,
    w_qkv,
    rel_table,
    w_out,
    scale_attn,
    ln2_gain,
    ln2_shift,
    w_up,
    b_up,
    w_down,
    b_down,
    scale_mlp,
):
    f32 = F32
    bf16 = BF
    count, width = tokens.shape
    small = [ln1_gain, ln1_shift, scale_attn, ln2_gain, ln2_shift, b_down, scale_mlp]
    rows = jnp.stack(small)
    own = rows.shape[1]
    mine = jnp.concatenate([rows.reshape(-1), b_up, rel_table.reshape(-1)])
    pad = -mine.shape[0] % 1024
    every = lax.all_gather(jnp.pad(mine, (0, pad)), "fsdp", axis=0, tiled=False)
    shards = every.shape[0]
    n_small = len(small) * own
    vectors = jnp.transpose(every[:, :n_small].reshape(shards, len(small), own), (1, 0, 2)).reshape(len(small), -1)
    bup = every[:, n_small : n_small + b_up.shape[0]].reshape(-1)
    heads = rel_table.shape[0] * shards
    offsets = rel_table.shape[2]
    table = every[:, n_small + b_up.shape[0] : n_small + b_up.shape[0] + rel_table.size].reshape(heads * 2, offsets)
    table = jnp.pad(table.astype(f32), ((0, 0), (0, 128 - offsets)))
    vectors = vectors.astype(f32)
    g_one, s_one, scale_a, g_two, s_two, bdown, scale_m = [vectors[i] for i in range(len(small))]
    wqkv = gather(w_qkv)
    wout = gather(w_out)
    wup = gather(w_up)
    wdown = gather(w_down)
    pos = jnp.stack([page_id, pos_row, pos_col]).reshape(3, count // 128, 128)
    norm_one, qkv, att, ext, hot, page_k, bias = forward_call(tokens, pos, g_one[None], s_one[None], table, wqkv)
    tok = tokens.astype(f32)
    vec = jnp.pad(jnp.concatenate([vectors, jnp.zeros((1, width), f32), bup.astype(f32).reshape(-1, width)]), ((0, 12), (0, 0)))
    layer_out, d_mid, d_att, d_ext, parts, small_g = middle_call(tokens, cotangent, att, ext, vec, wout, wup, wdown)
    ndp = lax.axis_size("dp")
    wq = jnp.transpose(wqkv.reshape(width, 3, 3, 256), (2, 0, 1, 3)).reshape(3, width, width)
    grad_tokens, total, small_t = backward_call(
        ndp, pos, vec, small_g, qkv, ext, hot, page_k, bias, d_ext, d_att, norm_one, wq, tokens, d_mid, parts
    )
    total = jnp.transpose(total, (0, 2, 3, 4, 1, 5)).reshape(12, 192, 768).astype(f32)
    where = {kind: i for i, kind in enumerate(ORDER)}
    r_wdown = jnp.concatenate([total[where["g", i]] for i in range(4)], axis=0).T
    r_wup = jnp.concatenate([total[where["g", 4 + i]] for i in range(4)], axis=1)
    r_wout = total[where["g", 8]]
    r_wqkv = jnp.concatenate([total[where["q", g]][:, 256 * k : 256 * k + 256] for k in range(3) for g in range(3)], axis=1)
    me = lax.axis_index("fsdp")
    vec = lax.dynamic_slice(small_t, (0, me * own), (len(small), own))
    r_bup = lax.dynamic_slice(small_t, (8 + me, 0), (1, width)).reshape(-1)
    d_table = jnp.transpose(small_t[12:, :128].reshape(-1, 2, 2, 64)[:, :, ::-1, :offsets], (0, 2, 1, 3)).reshape(heads, 2, offsets)
    r_table = lax.dynamic_slice(d_table, (me * rel_table.shape[0], 0, 0), rel_table.shape)
    return (
        layer_out,
        grad_tokens,
        vec[0],
        vec[1],
        r_wqkv,
        r_table,
        r_wout,
        vec[2],
        vec[3],
        vec[4],
        r_wup,
        r_bup,
        r_wdown,
        vec[5],
        vec[6],
    )


def solution(mesh):
    rows = P(("dp", "fsdp"))
    slab = P(("dp", "fsdp"), None)
    vec = P("fsdp")
    mat = P("fsdp", None)
    cube = P("fsdp", None, None)
    in_specs = (slab, slab, rows, rows, rows, vec, vec, mat, cube, mat, vec, vec, vec, mat, vec, mat, vec, vec)
    out_specs = (slab, slab, vec, vec, mat, cube, mat, vec, vec, vec, mat, vec, mat, vec, vec)
    return jax.shard_map(local, mesh=mesh, in_specs=in_specs, out_specs=out_specs, check_vma=False)
```

time: 558 us -> 364 us (0.65)
  waiting for transfers between devices: 239 us -> 67.6 us
  Pallas kernels: 95.3 us -> 235 us
  matrix products: 114 us -> 0 us
  blocking collectives: 48.4 us -> 6.19 us
  other arithmetic: 20.7 us -> 6.13 us
  local copies, waits for them, and re-layouts: 21.6 us -> 33.2 us
    pallas_call x2 -> x3, Pallas kernels: 95.3 us -> 235 us  [the longest x1 138 us: backward_call(): pl.pallas_call(functools.partial(backward_kernel, ndp), out_shape=[jax.Sh...]
    dot_general x11 -> x0, matrix products: 114 us -> none  [the longest x1 27.8 us: local(): d_act = jnp.einsum('nd,fd->nf', d_down, wdown, preferred_element_type=f32)]
    reduce_scatter x4 -> x0, waiting for transfers between devices: 106 us -> none  [scatter(): lax.psum_scatter(g, 'fsdp', scatter_dimension=0, tiled=True)]
    psum x1 -> x0, waiting for transfers between devices: 77.5 us -> none  [scatter(): lax.psum(lax.psum_scatter(g, 'fsdp', scatter_dimension=0, tiled=True), 'dp')]
    psum x1 -> x0, blocking collectives: 42.2 us -> none  [local(): total = lax.psum(flat, ('dp', 'fsdp'))]
    all_gather x4, waiting for transfers between devices: 53.3 us -> 65 us  [gather(): return lax.all_gather(x, 'fsdp', axis=0, tiled=True)]
    reduce_sum x5 -> x0, other arithmetic: 11.1 us -> none  [the longest x2 6.73 us: normalize(): return center * lax.rsqrt(spread + 1e-06) * gain + shift]
    slice x3 -> x14, local copies, waits for them, and re-layouts: 0.01 us -> 9.23 us  [the longest x5 3.75 us: local(): total[where['g', i]]]
  transfers between devices with their start and end apart: 9 -> 4, of which waited for: 7 -> 3; matrix products, arithmetic and copies ran while one was open for 18% -> 4% of each run, Pallas kernels for 17% -> 12%
where the time goes in v2:
time: 364 us; the launch traced here: 363 us
  Pallas kernels  235 us (65%)
  waiting for transfers between devices  67.6 us (19%)
  local copies, waits for them, and re-layouts  33.2 us (9%)
  between operations  14.3 us (4%)
  blocking collectives  6.19 us (2%)
  other arithmetic  6.13 us (2%)
    pallas_call x1, Pallas kernels, backward_call(): pl.pallas_call(functools.partial(backward_kernel, ndp), out_shape=[jax.Sh...  138 us
    all_gather x4, waiting for transfers between devices, gather(): return lax.all_gather(x, 'fsdp', axis=0, tiled=True)  65 us
    pallas_call x1, Pallas kernels, middle_call(): pl.pallas_call(middle_kernel, out_shape=[jax.ShapeDtypeStruct((count, wid...  54.4 us
    pallas_call x1, Pallas kernels, forward_call(): pl.pallas_call(forward_kernel, out_shape=[jax.ShapeDtypeStruct((width, co...  42.8 us
  transfers between devices with their start and end apart: 4, of which 3 were waited for; matrix products, arithmetic and copies ran while one was open for 4% of the time, Pallas kernels for 12%

profile of v2, /device:TPU:0, one launch (start us, length us, event | category | flops | bytes accessed | tf_op | source)
XLA Modules:
  0.0 362.8 jit_solution(2127643645731433296)
XLA Ops:
  7.3 0.7 all-gather.6.cloned.1.call-update
  8.1 0.7 all-gather.8.cloned.1.call-update
  8.8 0.7 all-gather.10.cloned.1.call-update
  9.6 0.5 all-gather.12.cloned.1.call-update
  10.3 0.1 reshape.96
  10.5 0.1 concatenate.16
  10.6 6.2 %all-gather = bf16[12288]{0:T(1024)(128)(2,1)S(1)} all-gather(bf16[3072]{0:T(1024)(128)(2,1)S(1)} %pad.14), channel_id=2, replica_groups=mesh['dp'=8,'fsdp'=4] {'fsdp'}, dimensions={0}, use_global_device_ids=true | all-gather | bytes 30720 | tf_op jit(solution)/shard_map/all_gather | solution.py:863
  16.9 0.1 reshape.103
  17.0 0.7 slice.131.gain
  17.7 0.7 slice.133.shift
  18.4 0.1 convert_element_type.37
  18.7 0.6 pad.17.vec
  19.3 0.6 pad_convert_fusion.table
  20.0 0.6 pad_add_fusion.pos
  20.6 22.6 %all-gather.6.cloned.1.call-done.wqkv = bf16[768,2304]{1,0:T(8,128)(2,1)} async-done(((bf16[192,2304]{1,0:T(8,128)(2,1)}), bf16[768,2304]{1,0:T(8,128)(2,1)}) %all-gather.6.cloned.1.call-update) | async-done | bytes 3538960 | tf_op jit(solution)/shard_map/all_gather | solution.py:832
  43.2 5.8 %copy.55 = bf16[768,2304]{0,1:T(8,128)(2,1)} copy(bf16[768,2304]{1,0:T(8,128)(2,1)} %all-gather.6.cloned.1.call-done.wqkv) | data formatting | bytes 7077888 | tf_op jit(solution)/shard_map/all_gather | solution.py:832
  48.9 2.3 copy.56
  51.2 3.8 %copy.57.wq_h = bf16[3,768,768]{2,1,0:T(8,128)(2,1)} copy(bf16[3,768,768]{1,2,0:T(8,128)(2,1)S(1)} %bitcast.59) | data formatting | bytes 7077888 | tf_op jit(solution)/shard_map/reshape | solution.py:884
  55.0 42.8 %attention_forward.1 = (bf16[768,1024]{1,0:T(8,128)(2,1)}, bf16[18,1024,128]{2,1,0:T(8,128)(2,1)}, bf16[1024,768]{1,0:T(8,128)(2,1)}, bf16[1024,128]{1,0:T(8,128...) custom-call(bf16[1024,768]{1,0:T(8,128)(2,1)} %tok_h.3, ...), custom_call_target="tpu_custom_call" | custom-call | tf_op jit(solution)/shard_map/attention_forward/pallas_call | solution.py:131
  97.8 3.5 all-gather.10.cloned.1.call-done.wup_h
  101.3 38.9 %all-gather.12.cloned.1.call-done.wdown_h = bf16[3072,768]{1,0:T(8,128)(2,1)} async-done(((bf16[768,768]{1,0:T(8,128)(2,1)}), bf16[3072,768]{1,0:T(8,128)(2,1)}) %all-gather.12.cloned.1.call-update) | async-done | bytes 4718608 | tf_op jit(solution)/shard_map/all_gather | solution.py:832
  140.2 54.4 %middle.1 = (bf16[1024,768]{1,0:T(8,128)(2,1)}, f32[1024,768]{1,0:T(8,128)}, bf16[1024,768]{1,0:T(8,128)(2,1)}, bf16[1024,128]{1,0:T(8,128)(2,1)}, bf16[9,2,2,2,...) custom-call(bf16[1024,768]{1,0:T(8,128)(2,1)} %tok_h.3, bf16[1024,768]{1,0:T(8,128)(2,1)} %cot_h.1, ...), custom_call_target="tpu_custom_call" | custom-call | tf_op jit(solution)/shard_map/middle/pallas_call | solution.py:790
  194.6 138.0 %backward.1 = (bf16[1024,768]{1,0:T(8,128)(2,1)}, bf16[12,2,2,2,48,384]{5,4,3,2,1,0:T(8,128)(2,1)}, f32[24,768]{1,0:T(8,128)}) custom-call(s32[3,8,128]{2,1,0:T(8,128)} %pad_add_fusion.pos, f32[24,768]{1,0:T(8,128)} %pad.17.vec, f32[24,768]{1,0:T(8,128)} %get-tuple-element.34.small_in, bf16[18,1024,128]{2,1,0:T(8,128)(2,1)} %get-tuple-element.35.qkv_h, ...), custom_call_target="tpu_custom_call" | custom-call | tf_op jit(solution)/shard_map/backward/pallas_call | solution.py:548
  332.6 2.9 convert_bitcast_fusion
  335.6 1.9 fusion
  337.5 0.5 copy.67
  338.0 0.5 copy.68
  338.5 0.5 copy.69
  339.0 0.5 copy.70
  339.5 0.2 maximum_bitcast_fusion
  339.7 2.0 copy.71
  341.6 1.6 copy.63
  343.3 0.5 copy.64
  343.8 0.5 copy-done.3
  344.3 0.5 copy.65
  344.9 0.5 copy.66
  345.4 0.5 copy-done.1
  345.8 0.5 copy.58
  346.4 0.5 copy.59
  346.9 0.5 copy.60
  347.7 0.5 copy.62
  348.1 0.9 copy.75
  349.0 0.7 slice.150
  349.9 1.4 dynamic-slice_reduce_fusion
  351.2 0.6 constant_dynamic-slice_fusion.1
  351.8 1.7 pad_maximum_fusion
  353.5 1.6 fusion.1
  355.1 1.1 copy.93
  (83 shorter events, 1.7 us)
Async XLA Ops:
  7.2 2.9 copy-start.12
  7.2 2.9 copy-start.13
  7.2 2.9 copy-start.14
  7.2 3.0 copy-start.15
  7.2 3.0 copy-start.16
  7.2 3.0 copy-start.17
  7.2 3.0 copy-start.18
  7.3 3.1 copy-start.11
  7.3 3.2 copy-start.10
  7.3 35.9 %all-gather.6.cloned.1.call-start = ((), (), s32[]{:S(2)}) async-start(), calls=%async_computation | async-start | bytes 4423680 | tf_op jit(solution)/shard_map/all_gather | solution.py:832
  8.0 11.9 %copy-start.7 = (s32[1024]{0:T(1024)S(1)}, s32[1024]{0:T(1024)}, u32[]{:S(2)}) copy-start(s32[1024]{0:T(1024)} %param.22) | copy-start | bytes 12292
  8.0 11.9 %copy-start.8 = (s32[1024]{0:T(1024)S(1)}, s32[1024]{0:T(1024)}, u32[]{:S(2)}) copy-start(s32[1024]{0:T(1024)} %param.21) | copy-start | bytes 12292
  8.0 11.9 %copy-start.9 = (s32[1024]{0:T(1024)S(1)}, s32[1024]{0:T(1024)}, u32[]{:S(2)}) copy-start(s32[1024]{0:T(1024)} %param.20) | copy-start | bytes 12292
  8.0 89.7 %all-gather.8.cloned.1.call-start = ((), (), s32[]{:S(2)}) async-start(), calls=%async_computation.1 | async-start | bytes 1474560 | tf_op jit(solution)/shard_map/all_gather | solution.py:832
  8.8 92.5 %all-gather.10.cloned.1.call-start = ((), (), s32[]{:S(2)}) async-start(), calls=%async_computation.2 | async-start | bytes 5898240 | tf_op jit(solution)/shard_map/all_gather | solution.py:832
  9.5 130.7 %all-gather.12.cloned.1.call-start = ((), (), s32[]{:S(2)}) async-start(), calls=%async_computation.3 | async-start | bytes 5898240 | tf_op jit(solution)/shard_map/all_gather | solution.py:832
  341.6 1.6 copy-start.4
  343.2 1.1 copy-start.3
  343.8 1.1 copy-start.2
  344.7 1.1 copy-start.1
  345.3 1.1 copy-start
  347.6 1.4 copy-start.6
  351.8 3.3 copy-start.5
Sparse Core Ops, SparseCore 0:
  9.7 33.4 all-gather.5
  44.7 17.4 all-gather.7
  63.8 37.4 all-gather.9
  102.7 37.4 all-gather.11

commit v3 on v1

v3 whole, which is shorter than its diff:
```python
import functools

import jax
import jax.numpy as jnp
from jax import lax
from jax.experimental import pallas as pl
from jax.experimental.pallas import tpu as pltpu
from jax.sharding import PartitionSpec as P

F32 = jnp.float32
BF = jnp.bfloat16
NT = (((1,), (1,)), ((), ()))
NN = (((1,), (0,)), ((), ()))
VMEM = pl.BlockSpec(memory_space=pltpu.VMEM)
ANY = pl.BlockSpec(memory_space=pl.ANY)
MESH = pl.DeviceIdType.MESH
LIMIT = 63 << 20
MASKED = -1e30


def mm(a, b, dims=NN):
    return lax.dot_general(a, b, dims, preferred_element_type=F32)


def lanes(rows, width=128):
    return lax.broadcasted_iota(jnp.int32, (rows, width), 1)


def normalize(rows, gain, shift):
    center = rows - jnp.mean(rows, axis=-1, keepdims=True)
    spread = jnp.mean(center * center, axis=-1, keepdims=True)
    return center * lax.rsqrt(spread + 1e-06) * gain + shift


def pieces(x, lane):
    hi = x.astype(BF)
    rest = x - hi.astype(F32)
    mid = rest.astype(BF)
    low = (rest - mid.astype(F32)).astype(BF)
    third = lane % 3
    return jnp.where(third == 0, hi.astype(F32), jnp.where(third == 1, mid.astype(F32), low.astype(F32)))


def position_columns(pages, rows, cols, hot, page_q, page_k):
    for r in range(pages.shape[0]):
        code = (pages[r : r + 1, :] + 1) * 4096 + rows[r : r + 1, :] * 64 + cols[r : r + 1, :]
        code = jnp.broadcast_to(code.astype(F32), (128, 128)).T.astype(jnp.int32)
        lane = lanes(128)
        page, row, col = code >> 12, (code >> 6) & 63, code & 63
        near = lane & 63
        where = jnp.where(near < 32, row, col + 32)
        at = pl.ds(r * 128, 128)
        hot[at, :] = jnp.where(where == near, 1.0, 0.0).astype(BF)
        page_q[at, :] = jnp.where(page == lane, 1.0, 0.0)
        page_k[at, :] = jnp.where((lane < 6) & (page != lane), MASKED, 0.0).astype(BF)


def toeplitz(table, bias):
    lane = lanes(32)
    for p in range(bias.shape[0]):
        for axis in range(2):
            parts = []
            for head, at in ((2 * p + 1, 32 * axis), (2 * p, 64 + 32 * axis)):
                row = jnp.broadcast_to(table[2 * head + axis : 2 * head + axis + 1, :], (32, 128))
                rolled = pltpu.roll(row, (97 + at) % 128, axis=1, stride=1, stride_axis=0)
                parts.append(jnp.where((lane >= at) & (lane < at + 32), rolled, 0.0))
            bias[p, 32 * axis : 32 * axis + 32, :] = (parts[0] + parts[1]).astype(BF)


class Links:
    def __init__(self, ndp):
        self.dp, self.f = lax.axis_index("dp"), lax.axis_index("fsdp")
        self.core, self.x = self.f % 2, self.f // 2
        self.bits = ndp.bit_length() - 1
        self.bit = [(self.dp // 2**k) % 2 for k in range(self.bits)]

    def partner(self, kind, k=0):
        if kind == "core":
            return (self.dp, self.f + 1 - 2 * self.core)
        if kind == "x":
            return (self.dp, self.f + 2 - 4 * self.x)
        return (self.dp + (1 - 2 * self.bit[k]) * 2**k, self.f)

    def everyone(self):
        return [self.partner("core"), self.partner("x")] + [self.partner("dp", k) for k in range(self.bits)]

    def greet(self, others):
        barrier = pltpu.get_barrier_semaphore()
        for other in others:
            pl.semaphore_signal(barrier, inc=1, device_id=other, device_id_type=MESH)
        pl.semaphore_wait(barrier, len(others))


def remote(src, dst, send, recv, device):
    return pltpu.make_async_remote_copy(
        src_ref=src, dst_ref=dst, send_sem=send, recv_sem=recv, device_id=device, device_id_type=MESH
    )


def pick_index(n, table):
    out = 0
    for i, v in enumerate(table):
        if v:
            out = out + jnp.where(n == i, v, 0)
    return out


class Reduction:
    def __init__(self, links, halvings, order, homes, first, last, acc, recv, final, out_h, load_sem, send_sem, recv_sem, out_sem):
        self.l, self.order, self.homes, self.first = links, order, homes, first
        self.acc, self.recv, self.final, self.out_h = acc, recv, final, out_h
        self.load_sem, self.send_sem, self.recv_sem, self.out_sem = load_sem, send_sem, recv_sem, out_sem
        self.depth = max(0, first - 1)
        self.halvings = halvings
        self.halved = 1 + halvings
        self.extra = links.bits - halvings
        self.stages = 2 + 2 * halvings + self.extra
        self.last = self.stages if last is None else last
        self.kept = (links.x,) + tuple(links.bit[:halvings])

    def sems(self, k, n):
        return self.send_sem.at[k, n], self.recv_sem.at[k, n]

    def partner(self, k):
        l = self.l
        if k == 0:
            return l.partner("core")
        if k == 1:
            return l.partner("x")
        if k <= self.halved + self.extra:
            return l.partner("dp", k - 2)
        return l.partner("dp", self.halvings - 1 - (k - 1 - self.halved - self.extra))

    def copy(self, k, n):
        l = self.l
        if k <= self.halved:
            at = (n,) + self.kept[self.depth : k - 1] + (1 - self.kept[k - 1],)
            return remote(self.acc.at[at], self.recv[k].at[n], *self.sems(k, n), self.partner(k))
        if k <= self.halved + self.extra:
            return remote(self.final.at[(n,) + self.kept[1:]], self.recv[k].at[n], *self.sems(k, n), self.partner(k))
        j = self.halvings - 1 - (k - 1 - self.halved - self.extra)
        at = (n,) + self.kept[1 : 2 + j]
        return remote(self.final.at[at], self.final.at[at], *self.sems(k, n), self.partner(k))

    def opening(self, n, act):
        l = self.l
        for kind in sorted(self.homes):
            places = [i for i, (name, _) in enumerate(self.order) if name == kind]
            mine = pick_index(n, [i for _, i in self.order])
            home = self.homes[kind]

            @pl.when(sum(jnp.where(n == i, 1, 0) for i in places) > 0)
            def _(home=home):
                if self.first == 0:
                    act(
                        lambda: remote(
                            home.at[mine, 1 - l.core], self.recv[0].at[n], *self.sems(0, n), self.partner(0)
                        ),
                        lambda: pltpu.make_async_copy(home.at[mine, l.core], self.acc.at[n], self.load_sem.at[n]),
                    )
                else:
                    act(None, lambda: pltpu.make_async_copy(home.at[mine], self.acc.at[n], self.load_sem.at[n]))

    def out(self, n):
        if self.last == self.stages:
            return pltpu.make_async_copy(self.final.at[n], self.out_h.at[n], self.out_sem.at[n])
        src = self.acc.at[(n,) + self.kept[self.depth : self.last - 1]]
        return pltpu.make_async_copy(src, self.out_h.at[n], self.out_sem.at[n])

    def launch(self, n):
        def start(send, load):
            if send is not None:
                send().start()
            load().start()

        self.opening(n, start)

    def step(self, k, n):
        l = self.l

        def arrive(send, load):
            if send is not None:
                send().wait_recv()
            load().wait()

        if k == max(self.first, 1):
            self.opening(n, arrive)
            if self.first == 0:
                self.acc[n] = self.acc[n] + self.recv[0][n]
        elif k <= self.halved:
            self.copy(k - 1, n).wait_recv()
            at = (n,) + self.kept[self.depth : k - 1]
            self.acc[at] = self.acc[at] + self.recv[k - 1][n]
        elif k == self.halved + 1:
            self.copy(k - 1, n).wait_recv()
            at = (n,) + self.kept[self.depth :]
            self.final[(n,) + self.kept[1:]] = self.acc[at] + self.recv[k - 1][n]
        elif k <= self.halved + self.extra + 1:
            self.copy(k - 1, n).wait()
            at = (n,) + self.kept[1:]
            self.final[at] = self.final[at] + self.recv[k - 1][n]
        else:
            self.copy(k - 1, n).wait_recv()
        if k < self.last:
            self.copy(k, n).start()
        else:
            self.out(n).start()

    def tick(self, t, turns, lags):
        for k, lag in sorted(lags.items(), reverse=True):
            n = sum(jnp.where(t - lag >= turn, 1, 0) for turn in turns) - 1
            due = sum(jnp.where(t - lag == turn, 1, 0) for turn in turns)

            @pl.when(due > 0)
            def _(k=k, n=n):
                if k == -1:
                    self.launch(n)
                else:
                    self.step(k, n)

    def finish(self):
        l = self.l

        @pl.loop(0, len(self.order))
        def _(n):
            if self.first == 0:
                self.opening(n, lambda send, load: send().wait_send())
            for k in range(max(1, self.first), self.last):
                if not self.halved < k <= self.halved + self.extra:
                    self.copy(k, n).wait_send()
            self.out(n).wait()


def lag_table(first, last, start, step, special):
    table = {-1: start}
    at = start
    for k in range(max(1, first), last + 1):
        at += special.get(k, step)
        table[k] = at
    return table


def last_tick(lags, turns):
    return max(lags.values()) + max(turns) + 1


class Weights:
    def __init__(self, links, own, home, send_sem, recv_sem, keep_sem):
        self.l, self.own, self.home = links, own, home
        self.send_sem, self.recv_sem, self.keep_sem = send_sem, recv_sem, keep_sem
        l = links
        self.f = l.f
        self.y = l.bit[0]
        self.sibling = l.f + 1 - 2 * l.core
        self.across = l.f + 2 - 4 * l.x
        self.halves = (pl.ds(pl.multiple_of(self.y * 96, 32), 96), pl.ds(pl.multiple_of((1 - self.y) * 96, 32), 96))

    def branch(self, n, act):
        for (low, high), own, home in zip(((0, 3), (3, 4), (4, 8), (8, 12)), self.own, self.home):

            @pl.when((n >= low) & (n < high))
            def _(low=low, own=own, home=home):
                act(own(n - low), lambda f: home(n - low, f), low > 0)

    def copies(self, n, own, home):
        l, (this, other) = self.l, self.halves
        s = [(self.send_sem.at[k, n], self.recv_sem.at[k, n]) for k in range(5)]
        mine, across = home(self.f), home(self.across)
        sibling = l.partner("core")
        return [
            lambda: remote(own, mine, *s[0], sibling),
            lambda: remote(own.at[this, :], mine.at[this, :], *s[1], l.partner("x")),
            lambda: remote(across.at[this, :], across.at[this, :], *s[2], l.partner("dp", 0)),
            lambda: remote(across.at[this, :], across.at[this, :], *s[3], sibling),
            lambda: remote(across.at[other, :], across.at[other, :], *s[4], sibling),
        ]

    def step(self, k, n):
        def act(own, home, keep):
            copies = self.copies(n, own, home)
            if k == 0:
                copies[1]().start()
                copies[0]().start()
                if keep:
                    pltpu.make_async_copy(own, home(self.f), self.keep_sem.at[n]).start()
            elif k == 1:
                copies[1]().wait_recv()
                copies[2]().start()
                copies[3]().start()
            elif k == 2:
                copies[2]().wait_recv()
                copies[4]().start()
            elif k == 3:
                for i in (0, 3, 4):
                    copies[i]().wait_recv()
            else:
                for copy in copies:
                    copy().wait_send()
                if keep:
                    pltpu.make_async_copy(own, home(self.f), self.keep_sem.at[n]).wait()

        self.branch(n, act)

    def tick(self, t):
        for k, lag in ((3, 7), (2, 4), (1, 0)):
            m = t - lag + 128
            n = m // 2 - 63

            @pl.when((m % 2 == 0) & (n >= 1) & (n < 12))
            def _(k=k, n=n):
                self.step(k, n)
                if k == 1:

                    @pl.when(n + 3 < 12)
                    def _():
                        self.step(0, n + 3)


def pack_own(mine, vectors, bup, table):
    own = vectors[0].shape[0]
    mine[...] = jnp.zeros_like(mine)
    for i, ref in enumerate(vectors):
        mine[i : i + 1, 0:own] = ref[...].astype(F32).reshape(1, own)
    line = bup[...].astype(F32).reshape(1, bup.shape[0])
    for i in range(4):
        mine[7 + i : 8 + i, 0:own] = line[:, own * i : own * i + own]
    for h in range(table.shape[0]):
        for axis in range(2):
            at = 11 + 2 * h + axis
            mine[at : at + 1, 0 : table.shape[2]] = table[h, axis : axis + 1, :].astype(F32)


def unpack(shards, vec, table, own):
    for v in range(7):
        vec[v : v + 1, :] = jnp.concatenate([shards[f, v : v + 1, 0:own] for f in range(4)], axis=1)
    for f in range(4):
        vec[8 + f : 9 + f, :] = jnp.concatenate([shards[f, 7 + i : 8 + i, 0:own] for i in range(4)], axis=1)
        table[6 * f : 6 * f + 6, :] = shards[f, 11:17, 0:128]


def forward_kernel(
    ndp,
    page,
    row,
    col,
    v0,
    v1,
    v2,
    v3,
    v4,
    v5,
    v6,
    bup,
    rel,
    tok_h,
    wqkv_h,
    wout_s,
    wup_s,
    wdown_s,
    normt_h,
    qkv_h,
    att_h,
    ext_h,
    hot_h,
    page_k_h,
    bias,
    vec,
    wq_h,
    wout_h,
    wup_h,
    wdown_h,
    tok,
    norm,
    normt,
    qkv,
    att,
    ext,
    hot,
    page_k,
    lse,
    ka,
    va,
    wq,
    mine,
    shards,
    table,
    tok_sem,
    mine_sem,
    local_sem,
    pack_send,
    pack_got,
    send_sem,
    recv_sem,
    keep_sem,
    out_sem,
    group_sem,
):
    count, width = tok.shape
    pairs = bias.shape[0]
    blocks = count // 256
    links = Links(ndp)
    tok_copy = pltpu.make_async_copy(tok_h, tok, tok_sem)
    tok_copy.start()

    def own_group(g):
        return [
            pltpu.make_async_copy(
                wqkv_h.at[:, width * part + 256 * g + 128 * s : width * part + 256 * g + 128 * s + 128],
                wq.at[g, links.f, :, 384 * s + 128 * part : 384 * s + 128 * part + 128],
                local_sem.at[g, 3 * s + part],
            )
            for s in range(2)
            for part in range(3)
        ]

    for g in range(3):
        for copy in own_group(g):
            copy.start()
    own_loads = [pltpu.make_async_copy(wout_s, mine.at[0], mine_sem.at[0])]
    for j in range(4):
        part = pl.ds(j * width, width)
        own_loads.append(pltpu.make_async_copy(wup_s.at[:, part], mine.at[1 + j], mine_sem.at[1 + j]))
    for j in range(4):
        part = pl.ds(j * 192, 192)
        own_loads.append(pltpu.make_async_copy(wdown_s.at[part, :], mine.at[5 + j], mine_sem.at[5 + j]))
    for copy in own_loads:
        copy.start()
    pack_own(shards.at[links.f], [v0, v1, v2, v3, v4, v5, v6], bup, rel)
    diagonal = (links.dp, 3 - links.f)
    peers = [links.partner("core"), links.partner("x"), diagonal]
    barrier = pltpu.get_barrier_semaphore()
    for other in peers + [links.partner("dp", 0)]:
        pl.semaphore_signal(barrier, inc=1, device_id=other, device_id_type=MESH)
    pl.semaphore_wait(barrier, 4)

    gather = Weights(
        links,
        [
            lambda j: wq.at[j, links.f],
            lambda j: mine.at[j],
            lambda j: mine.at[1 + j],
            lambda j: mine.at[5 + j],
        ],
        [
            lambda j, f: wq.at[j, f],
            lambda j, f: wout_h.at[f],
            lambda j, f: wup_h.at[j, f],
            lambda j, f: wdown_h.at[f, j],
        ],
        send_sem,
        recv_sem,
        keep_sem,
    )

    def pack_copy(i):
        return remote(shards.at[links.f], shards.at[links.f], pack_send.at[i], pack_got.at[i], peers[i])

    for copy in own_group(0):
        copy.wait()
    gather.step(0, 0)
    for i in range(3):
        pack_copy(i).start()
    for g in (1, 2):
        for copy in own_group(g):
            copy.wait()
    for copy in own_loads:
        copy.wait()
    gather.step(0, 1)
    gather.step(0, 2)
    gather.step(0, 3)
    position_columns(page, row, col, hot, lse, page_k)
    for i in range(3):
        pack_copy(i).wait_recv()
    vec[...] = jnp.zeros_like(vec)
    unpack(shards, vec, table, v0.shape[0])
    toeplitz(table, bias)
    tok_copy.wait()

    @pl.loop(0, blocks)
    def _(b):
        at = pl.ds(pl.multiple_of(b * 256, 256), 256)
        rows = normalize(tok[at, :].astype(F32), vec[0:1, :], vec[1:2, :]).astype(BF)
        norm[at, :] = rows
        normt[:, at] = rows.T

    outs = [
        pltpu.make_async_copy(src, dst, out_sem.at[i])
        for i, (src, dst) in enumerate([(normt, normt_h), (hot, hot_h), (page_k, page_k_h), (att, att_h), (ext, ext_h)])
    ]
    for copy in outs[:3]:
        copy.start()
    for k in (1, 2, 3):
        gather.step(k, 0)
    low_half = lanes(count) < 64

    def group_out(g):
        copies = [pltpu.make_async_copy(wq.at[g], wq_h.at[g], group_sem.at[3, g])]
        for part in range(3):
            some = pl.ds(part * pairs + 2 * g, 2)
            copies.append(pltpu.make_async_copy(qkv.at[some], qkv_h.at[some], group_sem.at[part, g]))
        return copies

    @pl.loop(0, pairs // 2)
    def _(g):
        @pl.loop(0, blocks)
        def _(b):
            at = pl.ds(pl.multiple_of(b * 256, 256), 256)
            block = mm(norm[at, :], wq[g].reshape(width, width)).astype(BF)
            for s in range(2):
                for part in range(3):
                    value = block[:, 384 * s + 128 * part : 384 * s + 128 * part + 128]
                    qkv[part * pairs + 2 * g + s, at, :] = value if part else value * jnp.asarray(0.125, BF)

        for copy in group_out(g):
            copy.start()

        @pl.loop(0, 2)
        def _(s):
            p = 2 * g + s
            keys, values = qkv[pairs + p], qkv[2 * pairs + p]
            side = mm(hot[:, :64], bias[p]).astype(BF)
            one = jnp.ones_like(values)
            ka[0, :, :128] = jnp.where(low_half, keys, side)
            ka[1, :, :128] = jnp.where(low_half, side, keys)
            va[0] = jnp.where(low_half, values, one)
            va[1] = jnp.where(low_half, one, values)
            for e in range(2):
                ka[e, :, 128:] = page_k[...]

            @pl.loop(0, blocks)
            def _(b):
                gather.tick(p * blocks + b)
                at = pl.ds(pl.multiple_of(b * 256, 256), 256)
                queries, places = qkv[p, at, :], hot[at, :]
                kept = lse[at, :]
                lane = lanes(256)
                half = lane < 64
                page_hot = jnp.where(lane < 6, kept, 0.0).astype(BF)
                results = []
                for e in range(2):
                    first = jnp.where(half, queries, places) if e == 0 else jnp.where(half, places, queries)
                    scores = mm(jnp.concatenate([first, page_hot], axis=1), ka[e], NT)
                    top = jnp.max(scores, axis=1, keepdims=True)
                    expo = jnp.exp(scores - top).astype(BF)
                    out = mm(expo, va[e])
                    turned = pltpu.roll(out, 64, axis=1)
                    total = jnp.where(half, turned, out) if e == 0 else jnp.where(half, out, turned)
                    results.append(out / total)
                    kept = jnp.where(lane // 3 == 2 + 2 * p + e, top + jnp.log(total), kept)
                lse[at, :] = kept
                att[at, pl.ds(pl.multiple_of(p * 128, 128), 128)] = jnp.where(half, results[0], results[1]).astype(BF)

    lane = lanes(256)

    @pl.loop(0, blocks)
    def _(b):
        at = pl.ds(pl.multiple_of(b * 256, 256), 256)
        ext[at, :] = jnp.where(lane < 6, lse[at, :], pieces(lse[at, :], lane)).astype(BF)

    for copy in outs[3:]:
        copy.start()
    @pl.loop(pairs * blocks, 28)
    def _(t):
        gather.tick(t)


    @pl.loop(0, 12)
    def _(n):
        gather.step(4, n)

    for i in range(3):
        pack_copy(i).wait_send()

    @pl.loop(0, pairs // 2)
    def _(g):
        for copy in group_out(g):
            copy.wait()

    for copy in outs:
        copy.wait()


def forward_call(ndp, places, vectors, bup, rel, tok, wqkv, wout, wup, wdown):
    count, width = tok.shape
    pairs = width // 128
    tall = pltpu.VMEM((count, width), BF)
    side = pltpu.VMEM((count, 128), BF)
    return pl.pallas_call(
        functools.partial(forward_kernel, ndp),
        out_shape=[
            jax.ShapeDtypeStruct((width, count), BF),
            jax.ShapeDtypeStruct((3 * pairs, count, 128), BF),
            jax.ShapeDtypeStruct((count, width), BF),
            jax.ShapeDtypeStruct((count, 128), BF),
            jax.ShapeDtypeStruct((count, 128), BF),
            jax.ShapeDtypeStruct((count, 128), BF),
            jax.ShapeDtypeStruct((pairs, 64, 128), BF),
            jax.ShapeDtypeStruct((12, width), F32),
            jax.ShapeDtypeStruct((3, 4, 192, width), BF),
            jax.ShapeDtypeStruct((4, 192, width), BF),
            jax.ShapeDtypeStruct((4, 4, 192, width), BF),
            jax.ShapeDtypeStruct((4, 4, 192, width), BF),
        ],
        in_specs=[VMEM] * 12 + [ANY] * 5,
        out_specs=[ANY] * 6 + [VMEM] * 2 + [ANY] * 4,
        scratch_shapes=[
            tall,
            tall,
            pltpu.VMEM((width, count), BF),
            pltpu.VMEM((3 * pairs, count, 128), BF),
            tall,
            side,
            side,
            side,
            pltpu.VMEM((count, 128), F32),
            pltpu.VMEM((2, count, 256), BF),
            pltpu.VMEM((2, count, 128), BF),
            pltpu.VMEM((3, 4, 192, width), BF),
            pltpu.VMEM((9, 192, width), BF),
            pltpu.VMEM((4, 24, 256), F32),
            pltpu.VMEM((24, 128), F32),
            pltpu.SemaphoreType.DMA,
            pltpu.SemaphoreType.DMA((9,)),
            pltpu.SemaphoreType.DMA((3, 6)),
            pltpu.SemaphoreType.DMA((3,)),
            pltpu.SemaphoreType.DMA((3,)),
            pltpu.SemaphoreType.DMA((5, 12)),
            pltpu.SemaphoreType.DMA((5, 12)),
            pltpu.SemaphoreType.DMA((12,)),
            pltpu.SemaphoreType.DMA((5,)),
            pltpu.SemaphoreType.DMA((4, 3)),
        ],
        compiler_params=pltpu.CompilerParams(vmem_limit_bytes=LIMIT, collective_id=0, has_side_effects=True),
        name="forward",
    )(*places, *vectors, bup, rel, tok, wqkv, wout, wup, wdown)


def gelu_both(u):
    c = 0.7978845608028654
    square = u * u
    t = jnp.tanh(c * u * (1.0 + 0.044715 * square))
    half = 0.5 + 0.5 * t
    slope = half + (0.5 * c) * u * (1.0 - t * t) * (1.0 + 0.134145 * square)
    return u * half, slope


EARLY = [("d", 0), ("d", 1), ("d", 2), ("d", 3)]
EARLY_STOP = 3
EARLY_TURNS = [0, 5, 10, 15]
EARLY_LAGS = {1: 0, 2: 6, 3: 10}


def middle_kernel(
    ndp,
    tok_h,
    cot_h,
    att_h,
    ext_h,
    vec,
    wout_h,
    wup_h,
    wdown_h,
    layer_h,
    dmid_h,
    datt_h,
    dext_h,
    part_h,
    half_h,
    small,
    tok,
    cot,
    att,
    ext,
    wout,
    wup,
    wdown,
    act,
    dup,
    n2t,
    ddt,
    att_t,
    ddown,
    dproj,
    layer,
    dmid,
    datt,
    dext,
    stage,
    own,
    acc,
    r0,
    r1,
    r2,
    in_sem,
    out_sem,
    layer_sem,
    part_sem,
    load_sem,
    send_sem,
    recv_sem,
    half_sem,
):
    count, width = tok.shape
    cols = wup.shape[0]
    blocks = count // 256
    loads = []
    for i, (src, dst) in enumerate(
        [(att_h, att), (wout_h, wout), (tok_h, tok), (wup_h, wup), (wdown_h, wdown), (cot_h, cot), (ext_h, ext)]
    ):
        copy = pltpu.make_async_copy(src, dst, in_sem.at[i])
        copy.start()
        loads.append(copy)
    links = Links(ndp)
    links.greet(links.everyone()[:3])
    red = Reduction(
        links, 3, EARLY, {"d": own}, 0, EARLY_STOP, acc, [r0, r1, r2], None, half_h, load_sem, send_sem, recv_sem, half_sem
    )
    small[...] = jnp.zeros_like(small)
    head = lax.broadcasted_iota(jnp.int32, (width, 128), 0) // 64
    pick = jnp.where(lanes(width) // 3 == head, 1.0, 0.0).astype(BF)
    for copy in loads:
        copy.wait()

    def spot(b):
        return pl.ds(pl.multiple_of(b * 256, 256), 256)

    def layer_out(b):
        return pltpu.make_async_copy(layer.at[spot(b), :], layer_h.at[spot(b), :], layer_sem.at[b])

    def outs(b):
        at = spot(b)
        return [
            pltpu.make_async_copy(src.at[at, :], dst.at[at, :], out_sem.at[i, b])
            for i, (src, dst) in enumerate([(dmid, dmid_h), (datt, datt_h), (dext, dext_h)])
        ]

    def masked(at):
        return cot[at, :].astype(F32) * (1.0 - ext[at, :].astype(F32)[:, 0:1])

    def center_scale(mid):
        center = mid - jnp.mean(mid, axis=-1, keepdims=True)
        return center, lax.rsqrt(jnp.mean(center * center, axis=-1, keepdims=True) + 1e-06)

    @pl.loop(0, blocks)
    def _(b):
        at = spot(b)
        rows_att = att[at, :]
        proj = mm(rows_att, wout[...])
        mid = tok[at, :].astype(F32) + vec[2:3, :] * proj
        dmid[at, :] = mid
        datt[at, :] = proj.astype(BF)
        center, scale = center_scale(mid)
        norm = (center * scale * vec[3:4, :] + vec[4:5, :]).astype(BF)
        down = jnp.zeros((256, width), F32)
        for j in range(cols):
            u = mm(norm, wup[j]) + vec[8 + j : 9 + j, :]
            a, s = gelu_both(u)
            a = a.astype(BF)
            act[at, j * width : (j + 1) * width] = a
            dup[at, j * width : (j + 1) * width] = s.astype(BF)
            down += mm(a, wdown[j * width : (j + 1) * width, :])
        down += vec[5:6, :]
        layer[at, :] = (mid + vec[6:7, :] * down).astype(BF)
        layer_out(b).start()
        grad = masked(at)
        d_down = (grad * vec[6:7, :]).astype(BF)
        ddown[at, :] = d_down
        small[6:7, :] += jnp.sum(grad * down, axis=0, keepdims=True)
        small[5:6, :] += jnp.sum(d_down.astype(F32), axis=0, keepdims=True)
        n2t[:, at] = norm.T
        ddt[:, at] = d_down.T
        att_t[:, at] = rows_att.T

    @pl.loop(0, 2)
    def _(h):
        @pl.loop(0, cols)
        def _(j):
            col = pl.ds(pl.multiple_of(j * width, width), width)
            value = mm(ddt[pl.ds(pl.multiple_of(h * 384, 384), 384), :], act[:, col])
            for i in range(2):
                for r in range(4):
                    for c in range(2):
                        rows = slice(192 * i + 48 * r, 192 * i + 48 * r + 48)
                        own[2 * h + i, j % 2, j // 2, c, r // 2, r % 2] = value[rows, 384 * c : 384 * c + 384].astype(BF)

        red.launch(2 * h)
        red.launch(2 * h + 1)

    @pl.loop(0, blocks)
    def _(b):
        at = spot(b)
        d_down = ddown[at, :]
        d_norm = jnp.zeros((256, width), F32)
        for j in range(cols):
            red.tick(cols * b + j, EARLY_TURNS, EARLY_LAGS)
            d_act = mm(d_down, wdown[j * width : (j + 1) * width, :], NT)
            some = slice(j * width, (j + 1) * width)
            d_up = (d_act * dup[at, some].astype(F32)).astype(BF)
            dup[at, some] = d_up
            small[8 + j : 9 + j, :] += jnp.sum(d_up.astype(F32), axis=0, keepdims=True)
            d_norm += mm(d_up, wup[j], NT)
        center, scale = center_scale(dmid[at, :])
        unit = center * scale
        small[3:4, :] += jnp.sum(d_norm * unit, axis=0, keepdims=True)
        small[4:5, :] += jnp.sum(d_norm, axis=0, keepdims=True)
        d_unit = d_norm * vec[3:4, :]
        d_mid = masked(at) + scale * (
            d_unit - jnp.mean(d_unit, axis=-1, keepdims=True) - unit * jnp.mean(d_unit * unit, axis=-1, keepdims=True)
        )
        dmid[at, :] = d_mid
        small[2:3, :] += jnp.sum(d_mid * datt[at, :].astype(F32), axis=0, keepdims=True)
        d_proj = (d_mid * vec[2:3, :]).astype(BF)
        dproj[at, :] = d_proj
        d_att = mm(d_proj, wout[...], NT).astype(BF)
        datt[at, :] = d_att
        prod = att[at, :].astype(F32) * d_att.astype(F32)
        hi = prod.astype(BF)
        low = (prod - hi.astype(F32)).astype(BF)
        dext[at, :] = pieces(-(mm(hi, pick) + mm(low, pick)), lanes(256)).astype(BF)
        for copy in outs(b):
            copy.start()

    def put(slot, value):
        for i in range(4):
            for r in range(4):
                for c in range(2):
                    rows = slice(192 * i + 48 * r, 192 * i + 48 * r + 48)
                    stage[slot, i, c, r // 2, r % 2] = value[rows, 384 * c : 384 * c + 384].astype(BF)

    def sends(chunk, slot):
        return [
            pltpu.make_async_copy(stage.at[slot, i], part_h.at[chunk, i % 2, i // 2], part_sem.at[slot, i])
            for i in range(4)
        ]

    @pl.loop(0, cols)
    def _(j):
        red.tick(cols * blocks + j, EARLY_TURNS, EARLY_LAGS)
        col = pl.ds(pl.multiple_of(j * width, width), width)
        slot = j % 2

        @pl.when(j > 1)
        def _():
            for copy in sends(j - 2, slot):
                copy.wait()

        put(slot, mm(n2t[...], dup[:, col]))
        for copy in sends(j, slot):
            copy.start()

    for copy in sends(cols - 2, 0):
        copy.wait()
    put(0, mm(att_t[...], dproj[...]))
    for copy in sends(cols, 0):
        copy.start()

    @pl.loop(cols * blocks + cols, last_tick(EARLY_LAGS, EARLY_TURNS))
    def _(t):
        red.tick(t, EARLY_TURNS, EARLY_LAGS)

    for copy in sends(cols - 1, 1) + sends(cols, 0):
        copy.wait()

    @pl.loop(0, blocks)
    def _(b):
        layer_out(b).wait()
        for copy in outs(b):
            copy.wait()

    red.finish()


def middle_call(ndp, tok, cot, att, ext, vec, wout, wup, wdown):
    count, width = tok.shape
    ff = wdown.shape[0]
    n = len(EARLY)
    tall = pltpu.VMEM((count, width), BF)
    wide = pltpu.VMEM((width, count), BF)
    return pl.pallas_call(
        functools.partial(middle_kernel, ndp),
        out_shape=[
            jax.ShapeDtypeStruct((count, width), BF),
            jax.ShapeDtypeStruct((count, width), F32),
            jax.ShapeDtypeStruct((count, width), BF),
            jax.ShapeDtypeStruct((count, 128), BF),
            jax.ShapeDtypeStruct((5, 2, 2, 2, 2, 2, 48, 384), BF),
            jax.ShapeDtypeStruct((n, 2, 2, 48, 384), BF),
            jax.ShapeDtypeStruct((24, width), F32),
        ],
        in_specs=[ANY] * 4 + [VMEM] + [ANY] * 3,
        out_specs=[ANY] * 6 + [VMEM],
        scratch_shapes=[
            tall,
            tall,
            tall,
            pltpu.VMEM((count, 128), BF),
            pltpu.VMEM(wout.shape, BF),
            pltpu.VMEM(wup.shape, BF),
            pltpu.VMEM(wdown.shape, BF),
            pltpu.VMEM((count, ff), BF),
            pltpu.VMEM((count, ff), BF),
            wide,
            wide,
            wide,
            tall,
            tall,
            tall,
            pltpu.VMEM((count, width), F32),
            tall,
            pltpu.VMEM((count, 128), BF),
            pltpu.VMEM((2, 4, 2, 2, 2, 48, 384), BF),
            pltpu.VMEM((n, 2, 2, 2, 2, 2, 48, 384), BF),
            pltpu.VMEM((n, 2, 2, 2, 2, 48, 384), BF),
            pltpu.VMEM((n, 2, 2, 2, 2, 48, 384), BF),
            pltpu.VMEM((n, 2, 2, 2, 48, 384), BF),
            pltpu.VMEM((n, 2, 2, 48, 384), BF),
            pltpu.SemaphoreType.DMA((7,)),
            pltpu.SemaphoreType.DMA((3, count // 256)),
            pltpu.SemaphoreType.DMA((count // 256,)),
            pltpu.SemaphoreType.DMA((2, 4)),
            pltpu.SemaphoreType.DMA((n,)),
            pltpu.SemaphoreType.DMA((EARLY_STOP, n)),
            pltpu.SemaphoreType.DMA((EARLY_STOP, n)),
            pltpu.SemaphoreType.DMA((n,)),
        ],
        compiler_params=pltpu.CompilerParams(vmem_limit_bytes=LIMIT, collective_id=2, has_side_effects=True),
        name="middle",
    )(tok, cot, att, ext, vec, wout, wup, wdown)


ORDER = [("g", 0), ("g", 1), ("g", 2), ("q", 0), ("g", 3), ("g", 4), ("q", 1)]
TURNS = [0, 3, 6, 9, 12, 15, 18]
LAGS = {1: 1, 2: 5, 3: 4, 4: 3, 5: 3, 6: 3, 7: 3, 8: 4}
LATE_TURNS = [1, 4, 7, 10]
HALF = [("h", 0), ("h", 1)]
HALF_TURNS = [21, 24]


def backward_kernel(
    ndp,
    page,
    row,
    col,
    vec,
    small_in,
    qkv_h,
    ext_h,
    hot_h,
    page_k_h,
    bias,
    dext_h,
    datt_h,
    normt_h,
    wq_h,
    tok_h,
    dmid_h,
    parts_h,
    early_h,
    gtok_h,
    total_h,
    late_h,
    last_h,
    small_out,
    qkv,
    ext,
    hot,
    page_k,
    dext,
    datt,
    normt,
    wq,
    tok,
    dmid,
    gtok,
    dqkv,
    qa,
    ka,
    va,
    doa,
    kt,
    dqt,
    hot_t,
    square,
    dtab,
    own,
    own_half,
    acc,
    b0,
    b1,
    b2,
    b3,
    b4,
    late_acc,
    late_final,
    late_3,
    late_4,
    half_acc,
    half_final,
    half_0,
    half_1,
    half_2,
    half_3,
    more,
    late_more,
    half_more,
    small_acc,
    small_recv,
    in_sem,
    gt_sem,
    load_sem,
    send_sem,
    recv_sem,
    out_sem,
    late_load,
    late_send,
    late_recv,
    late_out,
    half_load,
    half_send,
    half_recv,
    half_out,
    small_send,
    small_got,
):
    count, width = tok.shape
    pairs = bias.shape[0]
    blocks = count // 256
    loads = []
    for i, (src, dst) in enumerate(
        [
            (qkv_h, qkv),
            (ext_h, ext),
            (hot_h, hot),
            (page_k_h, page_k),
            (dext_h, dext),
            (datt_h, datt),
            (normt_h, normt),
            (wq_h, wq),
            (tok_h, tok),
            (dmid_h, dmid),
        ]
    ):
        copy = pltpu.make_async_copy(src, dst, in_sem.at[i])
        copy.start()
        loads.append(copy)
    links = Links(ndp)
    links.greet(links.everyone())
    red = Reduction(
        links,
        3,
        ORDER,
        {"g": parts_h, "q": own},
        0,
        None,
        acc,
        [b0, b1, b2, b3, b4] + [more.at[k] for k in range(links.bits - 3)],
        b1,
        total_h,
        load_sem,
        send_sem,
        recv_sem,
        out_sem,
    )
    late = Reduction(
        links,
        3,
        EARLY,
        {"d": early_h},
        EARLY_STOP,
        None,
        late_acc,
        [None, None, None, late_3, late_4] + [late_more.at[k] for k in range(links.bits - 3)],
        late_final,
        late_h,
        late_load,
        late_send,
        late_recv,
        late_out,
    )
    half = Reduction(
        links,
        2,
        HALF,
        {"h": own_half},
        0,
        None,
        half_acc,
        [half_0, half_1, half_2, half_3] + [half_more.at[k] for k in range(links.bits - 2)],
        half_final,
        last_h,
        half_load,
        half_send,
        half_recv,
        half_out,
    )
    lags = lag_table(0, red.stages, 0, 3, LAGS)
    late_lags = lag_table(EARLY_STOP, late.stages, 0, 3, {EARLY_STOP: 1})
    half_lags = lag_table(0, half.stages, 0, 2, {1: 1})

    def tick(t):
        red.tick(t, TURNS, lags)
        late.tick(t, LATE_TURNS, late_lags)
        half.tick(t, HALF_TURNS, half_lags)

    for r in range(page.shape[0]):
        want = 31 - lax.broadcasted_iota(jnp.int32, (32, 128), 0)
        for axis in range(2):
            have = jnp.broadcast_to((col if axis else row)[r : r + 1, :], (32, 128))
            hot_t[32 * axis : 32 * axis + 32, r * 128 : r * 128 + 128] = jnp.where(have == want, 1.0, 0.0).astype(BF)
    small_acc[0] = small_in[...]
    low_half = lanes(count) < 64
    third = lanes(count) // 3
    for copy in loads[:6]:
        copy.wait()

    @pl.loop(0, pairs)
    def _(p):
        g, s = p // 2, p % 2
        queries, keys, values = qkv[p], qkv[pairs + p], qkv[2 * pairs + p]
        side = mm(hot[:, :64], bias[p]).astype(BF)
        zero = jnp.zeros_like(values)
        places = hot[...]
        qa[0, :, :128] = jnp.where(low_half, queries, places)
        qa[1, :, :128] = jnp.where(low_half, places, queries)
        ka[0, :, :128] = jnp.where(low_half, keys, side)
        ka[1, :, :128] = jnp.where(low_half, side, keys)
        va[0, :, :128] = jnp.where(low_half, values, zero)
        va[1, :, :128] = jnp.where(low_half, zero, values)
        for e in range(2):
            head = 2 * p + e
            qa[e, :, 128:] = ext[...]
            ka[e, :, 128:] = jnp.where(third == 2 + head, -1.0, page_k[...].astype(F32)).astype(BF)
            va[e, :, 128:] = jnp.where(third == head, 1.0, 0.0).astype(BF)
        doa[:, :128] = datt[:, pl.ds(pl.multiple_of(p * 128, 128), 128)]
        doa[:, 128:] = dext[...]
        kt[...] = keys.T
        dqt[...] = jnp.zeros_like(dqt)
        square[...] = jnp.zeros_like(square)

        @pl.loop(0, blocks)
        def _(b):
            tick(p * blocks + b)
            at = pl.ds(pl.multiple_of(b * 256, 256), 256)
            dks, dvs = [], []
            for e in range(2):
                prob = jnp.exp(mm(ka[e, at, :], qa[e], NT))
                d_prob = mm(va[e, at, :], doa[...], NT)
                d_scores = (prob * d_prob).astype(BF)
                dvs.append(mm(prob.astype(BF), doa[:, :128]))
                dks.append(mm(d_scores, qa[e, :, :128]))
                dqt[64 * e : 64 * e + 64, :] += mm(kt[64 * e : 64 * e + 64, at], d_scores)
            half = lanes(256) < 64
            dqkv[g, at, pl.ds(pl.multiple_of(s * 384 + 128, 128), 128)] = jnp.where(half, dks[0], dks[1]).astype(BF)
            dqkv[g, at, pl.ds(pl.multiple_of(s * 384 + 256, 128), 128)] = jnp.where(half, dvs[0], dvs[1]).astype(BF)
            part = jnp.where(half, dks[1], dks[0])
            hi = part.astype(BF)
            low = (part - hi.astype(F32)).astype(BF)
            both = mm(hot_t[:, at], jnp.concatenate([hi, low], axis=1))
            square[...] += both[:, :128] + both[:, 128:]

        dqkv[g, :, pl.ds(pl.multiple_of(s * 384, 128), 128)] = (dqt[...].T * 0.125).astype(BF)
        near = lanes(32) & 63
        for axis in range(2):
            part = square[32 * axis : 32 * axis + 32, :]
            part = jnp.where((near >= 32) if axis else (near < 32), part, 0.0)
            rolled = pltpu.roll(part, 96 * axis, axis=1, stride=1, stride_axis=0)
            dtab[p, axis : axis + 1, :] = jnp.sum(rolled, axis=0, keepdims=True)

        @pl.when(p == 0)
        def _():
            for copy in loads[6:]:
                copy.wait()

        value = mm(normt[...], dqkv[g, :, pl.ds(pl.multiple_of(s * 384, 128), 384)]).astype(BF)

        @pl.when(p < 2 * own.shape[0])
        def _():
            for f in range(4):
                for r in range(4):
                    own[g, f % 2, f // 2, s, r // 2, r % 2] = value[192 * f + 48 * r : 192 * f + 48 * r + 48, :]

        @pl.when(p >= 2 * own.shape[0])
        def _():
            for f in range(4):
                for r in range(4):
                    at = (p - 2 * own.shape[0], f % 2, f // 2, r // 2, r % 2)
                    own_half[at] = value[192 * f + 48 * r : 192 * f + 48 * r + 48, :]

    for p in range(pairs):
        small_acc[0, 12 + 2 * p : 14 + 2 * p, 0:128] = dtab[p]

    def gtok_out(b):
        at = pl.ds(pl.multiple_of(b * 256, 256), 256)
        return pltpu.make_async_copy(gtok.at[at, :], gtok_h.at[at, :], gt_sem.at[b])

    first_tick = pairs * blocks

    @pl.loop(0, blocks)
    def _(b):
        tick(first_tick + b)
        at = pl.ds(pl.multiple_of(b * 256, 256), 256)
        d_norm = mm(dqkv[0, at, :], wq[0], NT)
        for g in range(1, pairs // 2):
            d_norm += mm(dqkv[g, at, :], wq[g], NT)
        rows = tok[at, :].astype(F32)
        center = rows - jnp.mean(rows, axis=-1, keepdims=True)
        scale = lax.rsqrt(jnp.mean(center * center, axis=-1, keepdims=True) + 1e-06)
        unit = center * scale
        small_acc[0, 0:1, :] += jnp.sum(d_norm * unit, axis=0, keepdims=True)
        small_acc[0, 1:2, :] += jnp.sum(d_norm, axis=0, keepdims=True)
        d_unit = d_norm * vec[0:1, :]
        back = scale * (
            d_unit - jnp.mean(d_unit, axis=-1, keepdims=True) - unit * jnp.mean(d_unit * unit, axis=-1, keepdims=True)
        )
        gtok[at, :] = (dmid[at, :] + back).astype(BF)
        gtok_out(b).start()

    others = links.everyone()

    def small_copy(i):
        return remote(small_acc.at[i], small_recv.at[i], small_send.at[i], small_got.at[i], others[i])

    small_copy(0).start()
    at_tick = first_tick + blocks
    for i in range(len(others)):
        tick(at_tick + i)
        small_copy(i).wait_recv()
        small_acc[i + 1] = small_acc[i] + small_recv[i]
        if i + 1 < len(others):
            small_copy(i + 1).start()
    small_out[...] = small_acc[len(others)]
    at_tick = at_tick + len(others)
    last = max(last_tick(lags, TURNS), last_tick(late_lags, LATE_TURNS), last_tick(half_lags, HALF_TURNS))

    @pl.loop(at_tick, last)
    def _(t):
        tick(t)

    red.finish()
    late.finish()
    half.finish()
    for i in range(len(others)):
        small_copy(i).wait_send()
    for b in range(blocks):
        gtok_out(b).wait()


def backward_call(ndp, places, vec, small, qkv, ext, hot, page_k, bias, dext, datt, normt, wq, tok, dmid, parts, half):
    count, width = datt.shape
    bits = ndp.bit_length() - 1
    n, m, q = len(ORDER), len(EARLY), len(HALF)
    last_extra = max(0, bits - 2)
    extra = max(0, bits - 3)
    stages = 2 + 2 * min(3, bits) + extra
    tall = pltpu.VMEM((count, width), BF)
    side = pltpu.VMEM((count, 128), BF)
    pair = pltpu.VMEM((2, count, 256), BF)
    return pl.pallas_call(
        functools.partial(backward_kernel, ndp),
        out_shape=[
            jax.ShapeDtypeStruct((count, width), BF),
            jax.ShapeDtypeStruct((n, 2, 2, 2, 48, 384), BF),
            jax.ShapeDtypeStruct((m, 2, 2, 2, 48, 384), BF),
            jax.ShapeDtypeStruct((q, 2, 2, 48, 384), BF),
            jax.ShapeDtypeStruct(small.shape, F32),
        ],
        in_specs=[VMEM] * 5 + [ANY] * 4 + [VMEM] + [ANY] * 8,
        out_specs=[ANY] * 4 + [VMEM],
        scratch_shapes=[
            pltpu.VMEM(qkv.shape, BF),
            side,
            side,
            side,
            side,
            tall,
            pltpu.VMEM((width, count), BF),
            pltpu.VMEM(wq.shape, BF),
            tall,
            pltpu.VMEM((count, width), F32),
            tall,
            pltpu.VMEM((3, count, width), BF),
            pair,
            pair,
            pair,
            pltpu.VMEM((count, 256), BF),
            pltpu.VMEM((128, count), BF),
            pltpu.VMEM((128, count), F32),
            pltpu.VMEM((64, count), BF),
            pltpu.VMEM((64, 128), F32),
            pltpu.VMEM((width // 128, 2, 128), F32),
            pltpu.VMEM((2, 2, 2, 2, 2, 2, 48, 384), BF),
            pltpu.VMEM((q, 2, 2, 2, 2, 48, 384), BF),
            pltpu.VMEM((n, 2, 2, 2, 2, 48, 384), BF),
            pltpu.VMEM((n, 2, 2, 2, 2, 48, 384), BF),
            pltpu.VMEM((n, 2, 2, 2, 48, 384), BF),
            pltpu.VMEM((n, 2, 2, 48, 384), BF),
            pltpu.VMEM((n, 2, 48, 384), BF),
            pltpu.VMEM((n, 48, 384), BF),
            pltpu.VMEM((m, 2, 2, 48, 384), BF),
            pltpu.VMEM((m, 2, 2, 2, 48, 384), BF),
            pltpu.VMEM((m, 2, 48, 384), BF),
            pltpu.VMEM((m, 48, 384), BF),
            pltpu.VMEM((q, 2, 2, 2, 48, 384), BF),
            pltpu.VMEM((q, 2, 2, 48, 384), BF),
            pltpu.VMEM((q, 2, 2, 2, 48, 384), BF),
            pltpu.VMEM((q, 2, 2, 48, 384), BF),
            pltpu.VMEM((q, 2, 48, 384), BF),
            pltpu.VMEM((q, 48, 384), BF),
            pltpu.VMEM((extra, n, 48, 384) if extra else (1, 1, 16, 128), BF),
            pltpu.VMEM((extra, m, 48, 384) if extra else (1, 1, 16, 128), BF),
            pltpu.VMEM((last_extra, q, 48, 384) if last_extra else (1, 1, 16, 128), BF),
            pltpu.VMEM((bits + 3,) + small.shape, F32),
            pltpu.VMEM((bits + 2,) + small.shape, F32),
            pltpu.SemaphoreType.DMA((10,)),
            pltpu.SemaphoreType.DMA((count // 256,)),
            pltpu.SemaphoreType.DMA((n,)),
            pltpu.SemaphoreType.DMA((stages, n)),
            pltpu.SemaphoreType.DMA((stages, n)),
            pltpu.SemaphoreType.DMA((n,)),
            pltpu.SemaphoreType.DMA((m,)),
            pltpu.SemaphoreType.DMA((stages, m)),
            pltpu.SemaphoreType.DMA((stages, m)),
            pltpu.SemaphoreType.DMA((m,)),
            pltpu.SemaphoreType.DMA((q,)),
            pltpu.SemaphoreType.DMA((stages, q)),
            pltpu.SemaphoreType.DMA((stages, q)),
            pltpu.SemaphoreType.DMA((q,)),
            pltpu.SemaphoreType.DMA((bits + 2,)),
            pltpu.SemaphoreType.DMA((bits + 2,)),
        ],
        compiler_params=pltpu.CompilerParams(vmem_limit_bytes=LIMIT, collective_id=1, has_side_effects=True),
        name="backward",
    )(*places, vec, small, qkv, ext, hot, page_k, bias, dext, datt, normt, wq, tok, dmid, parts, half)


def finish_kernel(
    total_h,
    late_h,
    last_h,
    layer_i,
    gtok_i,
    small,
    layer_h,
    gtok_h,
    wqkv_h,
    rel,
    wout_h,
    wup_h,
    bup,
    wdown_h,
    v0,
    v1,
    v2,
    v3,
    v4,
    v5,
    v6,
    total,
    late,
    last,
    wqkv,
    wout,
    wup,
    wdown,
    layer,
    gtok,
    in_sem,
    out_sem,
):
    f = lax.axis_index("fsdp")
    own = v0.shape[0]
    n, m = total.shape[0], late.shape[0]
    loads = [pltpu.make_async_copy(late_h.at[i], late.at[i], in_sem.at[i]) for i in range(m)]
    loads += [pltpu.make_async_copy(total_h.at[i], total.at[i], in_sem.at[m + i]) for i in range(n)]
    loads.append(pltpu.make_async_copy(last_h, last, in_sem.at[m + n]))
    through = [(layer_i, layer, layer_h), (gtok_i, gtok, gtok_h)]
    loads += [pltpu.make_async_copy(src, mid, in_sem.at[m + n + 1 + i]) for i, (src, mid, _) in enumerate(through)]
    for copy in loads:
        copy.start()
    pending = []

    def leave(src, dst):
        copy = pltpu.make_async_copy(src, dst, out_sem.at[len(pending)])
        copy.start()
        pending.append(copy)

    for h in range(m // 2):
        for i in (2 * h, 2 * h + 1):
            loads[i].wait()
        sides = []
        for c in range(2):
            rows = [late[2 * h + i, c, r // 2, r % 2].astype(F32) for i in range(2) for r in range(4)]
            sides.append(jnp.concatenate(rows, axis=0).T)
        for c in range(2):
            wdown[384 * c : 384 * c + 384, 384 * h : 384 * h + 384] = sides[c]
    leave(wdown, wdown_h)
    for i, (_, mid, dst) in enumerate(through):
        loads[m + n + 1 + i].wait()
        leave(mid, dst)
    for i, (kind, j) in enumerate(ORDER):
        loads[m + i].wait()
        for c in range(2):
            for r in range(4):
                at = slice(48 * r, 48 * r + 48)
                value = total[i, c, r // 2, r % 2].astype(F32)
                if kind == "g" and j < 4:
                    wup[at, 768 * j + 384 * c : 768 * j + 384 * c + 384] = value
                elif kind == "g":
                    wout[at, 384 * c : 384 * c + 384] = value
                else:
                    for part in range(3):
                        start = 768 * part + 256 * j + 128 * c
                        wqkv[at, start : start + 128] = value[:, 128 * part : 128 * part + 128]
    leave(wup, wup_h)
    leave(wout, wout_h)
    loads[m + n].wait()
    for i in range(last.shape[0]):
        for r in range(4):
            value = last[i, r // 2, r % 2].astype(F32)
            for part in range(3):
                start = 768 * part + 128 * (4 + i)
                wqkv[48 * r : 48 * r + 48, start : start + 128] = value[:, 128 * part : 128 * part + 128]
    leave(wqkv, wqkv_h)

    def mine(rows, width, stride):
        out = jnp.zeros((rows.stop - rows.start, width), F32)
        for k in range(4):
            out = jnp.where(f == k, small[rows, stride * k : stride * k + width], out)
        return out

    vectors = mine(slice(0, 8), own, own)
    for i, ref in enumerate((v0, v1, v2, v3, v4, v5, v6)):
        ref[...] = vectors[i : i + 1, :].reshape(own)
    line = jnp.zeros((1, bup.shape[0]), F32)
    for k in range(4):
        line = jnp.where(f == k, small[8 + k : 9 + k, :], line)
    bup[...] = line.reshape(bup.shape[0])
    offsets = rel.shape[2]
    for i in range(rel.shape[0]):
        for axis in range(2):
            value = jnp.zeros((1, offsets), F32)
            for k in range(4):
                head = rel.shape[0] * k + i
                start = 64 * (1 - head % 2)
                at = 12 + 2 * (head // 2) + axis
                value = jnp.where(f == k, small[at : at + 1, start : start + offsets], value)
            rel[i, axis : axis + 1, :] = value
    for copy in pending:
        copy.wait()


def finish_call(total, late, last, layer, gtok, small, own, rel):
    width = small.shape[1]
    vec = jax.ShapeDtypeStruct((own,), F32)
    shapes = [(own, 3 * width), (own, width), (own, 4 * width), (4 * own, width)]
    wqkv, wout, wup, wdown = [jax.ShapeDtypeStruct(s, F32) for s in shapes]
    return pl.pallas_call(
        finish_kernel,
        out_shape=[jax.ShapeDtypeStruct(layer.shape, BF), jax.ShapeDtypeStruct(gtok.shape, BF)]
        + [wqkv, jax.ShapeDtypeStruct(rel.shape, F32), wout, wup, jax.ShapeDtypeStruct((4 * own,), F32), wdown]
        + [vec] * 7,
        in_specs=[ANY] * 5 + [VMEM],
        out_specs=[ANY, ANY, ANY, VMEM, ANY, ANY, VMEM, ANY] + [VMEM] * 7,
        scratch_shapes=[pltpu.VMEM(x.shape, BF) for x in (total, late, last)]
        + [pltpu.VMEM(s, F32) for s in shapes]
        + [pltpu.VMEM(layer.shape, BF), pltpu.VMEM(gtok.shape, BF)]
        + [pltpu.SemaphoreType.DMA((total.shape[0] + late.shape[0] + 3,)), pltpu.SemaphoreType.DMA((6,))],
        compiler_params=pltpu.CompilerParams(vmem_limit_bytes=LIMIT),
        name="finish",
    )(total, late, last, layer, gtok, small)


def local(
    tokens,
    cotangent,
    page_id,
    pos_row,
    pos_col,
    ln1_gain,
    ln1_shift,
    w_qkv,
    rel_table,
    w_out,
    scale_attn,
    ln2_gain,
    ln2_shift,
    w_up,
    b_up,
    w_down,
    b_down,
    scale_mlp,
):
    ndp = lax.axis_size("dp")
    count, width = tokens.shape
    places = [x.reshape(count // 128, 128) for x in (page_id, pos_row, pos_col)]
    vectors = [ln1_gain, ln1_shift, scale_attn, ln2_gain, ln2_shift, b_down, scale_mlp]
    normt, qkv, att, ext, hot, page_k, bias, vec, wq, wout, wup, wdown = forward_call(
        ndp, places, vectors, b_up, rel_table, tokens, w_qkv, w_out, w_up, w_down
    )
    wq = wq.reshape(-1, width, width)
    wout = wout.reshape(width, width)
    wup = wup.reshape(-1, width, width)
    wdown = wdown.reshape(-1, width)
    layer_out, d_mid, d_att, d_ext, parts, early, small = middle_call(ndp, tokens, cotangent, att, ext, vec, wout, wup, wdown)
    grad_tokens, total, late, last, small = backward_call(
        ndp, places, vec, small, qkv, ext, hot, page_k, bias, d_ext, d_att, normt, wq, tokens, d_mid, parts, early
    )
    layer_out, grad_tokens, g_wqkv, g_rel, g_wout, g_wup, g_bup, g_wdown, *g = finish_call(
        total, late, last, layer_out, grad_tokens, small, ln1_gain.shape[0], rel_table
    )
    return (
        layer_out,
        grad_tokens,
        g[0],
        g[1],
        g_wqkv,
        g_rel,
        g_wout,
        g[2],
        g[3],
        g[4],
        g_wup,
        g_bup,
        g_wdown,
        g[5],
        g[6],
    )


def solution(mesh):
    rows = P(("dp", "fsdp"))
    slab = P(("dp", "fsdp"), None)
    vec = P("fsdp")
    mat = P("fsdp", None)
    cube = P("fsdp", None, None)
    in_specs = (slab, slab, rows, rows, rows, vec, vec, mat, cube, mat, vec, vec, vec, mat, vec, mat, vec, vec)
    out_specs = (slab, slab, vec, vec, mat, cube, mat, vec, vec, vec, mat, vec, mat, vec, vec)
    return jax.shard_map(local, mesh=mesh, in_specs=in_specs, out_specs=out_specs, check_vma=False)
```

time: 558 us -> 258 us (0.46)
  waiting for transfers between devices: 239 us -> 0 us
  Pallas kernels: 95.3 us -> 256 us
  matrix products: 114 us -> 0 us
  blocking collectives: 48.4 us -> 0 us
  local copies, waits for them, and re-layouts: 21.6 us -> 0 us
  other arithmetic: 20.7 us -> 0 us
  between operations: 14.5 us -> 0.86 us
    pallas_call x2 -> x4, Pallas kernels: 95.3 us -> 256 us  [the longest x1 116 us: backward_call(): pl.pallas_call(functools.partial(backward_kernel, ndp), out_shape=[jax.Sh...]
    dot_general x11 -> x0, matrix products: 114 us -> none  [the longest x1 27.8 us: local(): d_act = jnp.einsum('nd,fd->nf', d_down, wdown, preferred_element_type=f32)]
    reduce_scatter x4 -> x0, waiting for transfers between devices: 106 us -> none  [scatter(): lax.psum_scatter(g, 'fsdp', scatter_dimension=0, tiled=True)]
    psum x1 -> x0, waiting for transfers between devices: 77.5 us -> none  [scatter(): lax.psum(lax.psum_scatter(g, 'fsdp', scatter_dimension=0, tiled=True), 'dp')]
    all_gather x4 -> x0, waiting for transfers between devices: 53.3 us -> none  [gather(): return lax.all_gather(x, 'fsdp', axis=0, tiled=True)]
    psum x1 -> x0, blocking collectives: 42.2 us -> none  [local(): total = lax.psum(flat, ('dp', 'fsdp'))]
    reduce_sum x5 -> x0, other arithmetic: 11.1 us -> none  [the longest x2 6.73 us: normalize(): return center * lax.rsqrt(spread + 1e-06) * gain + shift]
    unnamed x57 -> x0, local copies, waits for them, and re-layouts: 9.72 us -> none
  transfers between devices with their start and end apart: 9 -> 0, of which waited for: 7 -> 0; matrix products, arithmetic and copies ran while one was open for 18% -> 0% of each run, Pallas kernels for 17% -> 0%
where the time goes in v3:
time: 258 us; the launch traced here: 257 us
  Pallas kernels  256 us (99%)
    pallas_call x1, Pallas kernels, backward_call(): pl.pallas_call(functools.partial(backward_kernel, ndp), out_shape=[jax.Sh...  116 us
    pallas_call x1, Pallas kernels, middle_call(): pl.pallas_call(functools.partial(middle_kernel, ndp), out_shape=[jax.Shap...  68.4 us
    pallas_call x1, Pallas kernels, forward_call(): pl.pallas_call(functools.partial(forward_kernel, ndp), out_shape=[jax.Sha...  63.4 us
    pallas_call x1, Pallas kernels, finish_call(): pl.pallas_call(finish_kernel, out_shape=[jax.ShapeDtypeStruct(layer.shape...  8.42 us

profile of v3, /device:TPU:0, one launch (start us, length us, event | category | flops | bytes accessed | tf_op | source)
XLA Modules:
  0.0 257.3 jit_solution(14652133272300982700)
XLA Ops:
  0.7 63.4 %forward.1 = (bf16[768,1024]{1,0:T(8,128)(2,1)}, bf16[18,1024,128]{2,1,0:T(8,128)(2,1)}, bf16[1024,768]{1,0:T(8,128)(2,1)}, bf16[1024,128]{1,0:T(8,128)(2,1)}, b...) custom-call(s32[8,128]{1,0:T(8,128)} %bitcast.11, ...), custom_call_target="tpu_custom_call" | custom-call | tf_op jit(solution)/shard_map/forward/pallas_call | solution.py:588
  64.1 68.4 %middle.1 = (bf16[1024,768]{1,0:T(8,128)(2,1)}, f32[1024,768]{1,0:T(8,128)}, bf16[1024,768]{1,0:T(8,128)(2,1)}, bf16[1024,128]{1,0:T(8,128)(2,1)}, bf16[5,2,2,2,...) custom-call(bf16[1024,768]{1,0:T(8,128)(2,1)} %tok_h.5, ...), custom_call_target="tpu_custom_call" | custom-call | tf_op jit(solution)/shard_map/middle/pallas_call | solution.py:879
  132.5 116.2 %backward.1 = (bf16[1024,768]{1,0:T(8,128)(2,1)}, bf16[7,2,2,2,48,384]{5,4,3,2,1,0:T(8,128)(2,1)}, bf16[4,2,2,2,48,384]{5,4,3,2,1,0:T(8,128)(2,1)}, bf16[2,2,2,48,384]{4,3,2,1,0:T(8,128)(2,1)}, f32[24,768]{1,0:T(8,128)}) custom-call(s32[8,128]{1,0:T(8,128)} %bitcast.12, s32[8,128]{1,0:T(8,128)} %bitcast.14, s32[8,128]{1,0:T(8,128)} %bitcast.16, ...), custom_call_target="tpu_custom_call" | custom-call | tf_op jit(solution)/shard_map/backward/pallas_call | solution.py:1258
  248.7 8.4 %finish.1 = (bf16[1024,768]{1,0:T(8,128)(2,1)}, bf16[1024,768]{1,0:T(8,128)(2,1)}, f32[192,2304]{1,0:T(8,128)}, f32[3,2,63]{2,1,0:T(2,128)}, f32[192,768]{1,0:T(...) custom-call(bf16[7,2,2,2,48,384]{5,4,3,2,1,0:T(8,128)(2,1)} %get-tup, ...), custom_call_target="tpu_custom_call" | custom-call | tf_op jit(solution)/shard_map/finish/pallas_call | solution.py:1457

commit v4 on v3

--- a/solution.py
+++ b/solution.py
@@ -127,9 +127,8 @@
             return l.partner("core")
         if k == 1:
             return l.partner("x")
-        if k <= self.halved + self.extra:
-            return l.partner("dp", k - 2)
-        return l.partner("dp", self.halvings - 1 - (k - 1 - self.halved - self.extra))
+        j = k - 2 if k <= self.halved + self.extra else self.halvings - 1 - (k - 1 - self.halved - self.extra)
+        return l.partner("dp", j)
 
     def copy(self, k, n):
         l = self.l
@@ -206,12 +205,17 @@
         else:
             self.out(n).start()
 
-    def tick(self, t, turns, lags):
+    def tick(self, turn, r, start, period, lags):
         for k, lag in sorted(lags.items(), reverse=True):
-            n = sum(jnp.where(t - lag >= turn, 1, 0) for turn in turns) - 1
-            due = sum(jnp.where(t - lag == turn, 1, 0) for turn in turns)
-
-            @pl.when(due > 0)
+            if (start + lag - r) % period:
+                continue
+            n = turn - (start + lag - r) // period
+            if isinstance(n, int):
+                if 0 <= n < len(self.order):
+                    self.launch(n) if k == -1 else self.step(k, n)
+                continue
+
+            @pl.when((n >= 0) & (n < len(self.order)))
             def _(k=k, n=n):
                 if k == -1:
                     self.launch(n)
@@ -240,8 +244,8 @@
     return table
 
 
-def last_tick(lags, turns):
-    return max(lags.values()) + max(turns) + 1
+def last_tick(start, period, count, lags):
+    return start + period * (count - 1) + max(lags.values()) + 1
 
 
 class Weights:
@@ -644,10 +648,10 @@
     return u * half, slope
 
 
-EARLY = [("d", 0), ("d", 1), ("d", 2), ("d", 3)]
+EARLY = [("d", 0), ("d", 1), ("d", 2)]
 EARLY_STOP = 3
-EARLY_TURNS = [0, 5, 10, 15]
-EARLY_LAGS = {1: 0, 2: 6, 3: 10}
+EARLY_PERIOD = 4
+EARLY_LAGS = {1: 0, 2: 8, 3: 12}
 
 
 def middle_kernel(
@@ -695,6 +699,7 @@
     out_sem,
     layer_sem,
     part_sem,
+    spare_sem,
     load_sem,
     send_sem,
     recv_sem,
@@ -784,7 +789,13 @@
                         own[2 * h + i, j % 2, j // 2, c, r // 2, r % 2] = value[rows, 384 * c : 384 * c + 384].astype(BF)
 
         red.launch(2 * h)
-        red.launch(2 * h + 1)
+
+        @pl.when(h == 0)
+        def _():
+            red.launch(1)
+
+    spare = pltpu.make_async_copy(own.at[3], part_h.at[5], spare_sem)
+    spare.start()
 
     @pl.loop(0, blocks)
     def _(b):
@@ -792,7 +803,7 @@
         d_down = ddown[at, :]
         d_norm = jnp.zeros((256, width), F32)
         for j in range(cols):
-            red.tick(cols * b + j, EARLY_TURNS, EARLY_LAGS)
+            red.tick(b, j, 0, EARLY_PERIOD, EARLY_LAGS)
             d_act = mm(d_down, wdown[j * width : (j + 1) * width, :], NT)
             some = slice(j * width, (j + 1) * width)
             d_up = (d_act * dup[at, some].astype(F32)).astype(BF)
@@ -835,7 +846,12 @@
 
     @pl.loop(0, cols)
     def _(j):
-        red.tick(cols * blocks + j, EARLY_TURNS, EARLY_LAGS)
+        for r in range(cols):
+
+            @pl.when(j == r)
+            def _(r=r):
+                red.tick(blocks, r, 0, EARLY_PERIOD, EARLY_LAGS)
+
         col = pl.ds(pl.multiple_of(j * width, width), width)
         slot = j % 2
 
@@ -854,9 +870,8 @@
     for copy in sends(cols, 0):
         copy.start()
 
-    @pl.loop(cols * blocks + cols, last_tick(EARLY_LAGS, EARLY_TURNS))
-    def _(t):
-        red.tick(t, EARLY_TURNS, EARLY_LAGS)
+    for t in range(EARLY_PERIOD * (blocks + 1), last_tick(0, EARLY_PERIOD, len(EARLY), EARLY_LAGS)):
+        red.tick(t // EARLY_PERIOD, t % EARLY_PERIOD, 0, EARLY_PERIOD, EARLY_LAGS)
 
     for copy in sends(cols - 1, 1) + sends(cols, 0):
         copy.wait()
@@ -867,6 +882,7 @@
         for copy in outs(b):
             copy.wait()
 
+    spare.wait()
     red.finish()
 
 
@@ -883,7 +899,7 @@
             jax.ShapeDtypeStruct((count, width), F32),
             jax.ShapeDtypeStruct((count, width), BF),
             jax.ShapeDtypeStruct((count, 128), BF),
-            jax.ShapeDtypeStruct((5, 2, 2, 2, 2, 2, 48, 384), BF),
+            jax.ShapeDtypeStruct((6, 2, 2, 2, 2, 2, 48, 384), BF),
             jax.ShapeDtypeStruct((n, 2, 2, 48, 384), BF),
             jax.ShapeDtypeStruct((24, width), F32),
         ],
@@ -909,7 +925,7 @@
             tall,
             pltpu.VMEM((count, 128), BF),
             pltpu.VMEM((2, 4, 2, 2, 2, 48, 384), BF),
-            pltpu.VMEM((n, 2, 2, 2, 2, 2, 48, 384), BF),
+            pltpu.VMEM((4, 2, 2, 2, 2, 2, 48, 384), BF),
             pltpu.VMEM((n, 2, 2, 2, 2, 48, 384), BF),
             pltpu.VMEM((n, 2, 2, 2, 2, 48, 384), BF),
             pltpu.VMEM((n, 2, 2, 2, 48, 384), BF),
@@ -918,6 +934,7 @@
             pltpu.SemaphoreType.DMA((3, count // 256)),
             pltpu.SemaphoreType.DMA((count // 256,)),
             pltpu.SemaphoreType.DMA((2, 4)),
+            pltpu.SemaphoreType.DMA,
             pltpu.SemaphoreType.DMA((n,)),
             pltpu.SemaphoreType.DMA((EARLY_STOP, n)),
             pltpu.SemaphoreType.DMA((EARLY_STOP, n)),
@@ -928,12 +945,11 @@
     )(tok, cot, att, ext, vec, wout, wup, wdown)
 
 
-ORDER = [("g", 0), ("g", 1), ("g", 2), ("q", 0), ("g", 3), ("g", 4), ("q", 1)]
-TURNS = [0, 3, 6, 9, 12, 15, 18]
-LAGS = {1: 1, 2: 5, 3: 4, 4: 3, 5: 3, 6: 3, 7: 3, 8: 4}
-LATE_TURNS = [1, 4, 7, 10]
-HALF = [("h", 0), ("h", 1)]
-HALF_TURNS = [21, 24]
+ORDER = [("g", 5), ("g", 0), ("g", 1), ("g", 2), ("q", 0), ("g", 3), ("g", 4)]
+LAGS = {1: 1, 2: 5, 3: 4, 8: 4}
+LATE_START = 1
+HALF = [("h", 0), ("h", 1), ("h", 2), ("h", 3)]
+HALF_START = 12
 
 
 def backward_kernel(
@@ -1095,12 +1111,19 @@
     )
     lags = lag_table(0, red.stages, 0, 3, LAGS)
     late_lags = lag_table(EARLY_STOP, late.stages, 0, 3, {EARLY_STOP: 1})
-    half_lags = lag_table(0, half.stages, 0, 2, {1: 1})
-
-    def tick(t):
-        red.tick(t, TURNS, lags)
-        late.tick(t, LATE_TURNS, late_lags)
-        half.tick(t, HALF_TURNS, half_lags)
+    half_lags = lag_table(0, half.stages, 0, 3, {1: 1, 2: 6})
+
+    def tick(turn, r):
+        red.tick(2 * turn + r // 2, r % 2, 0, 2, lags)
+        late.tick(2 * turn + r // 2, r % 2, LATE_START, 2, late_lags)
+        half.tick(turn, r, HALF_START, 4, half_lags)
+
+    def tick_at(turn, place):
+        for r in range(4):
+
+            @pl.when(place == r)
+            def _(r=r):
+                tick(turn, r)
 
     for r in range(page.shape[0]):
         want = 31 - lax.broadcasted_iota(jnp.int32, (32, 128), 0)
@@ -1139,7 +1162,7 @@
 
         @pl.loop(0, blocks)
         def _(b):
-            tick(p * blocks + b)
+            tick_at(p, b)
             at = pl.ds(pl.multiple_of(b * 256, 256), 256)
             dks, dvs = [], []
             for e in range(2):
@@ -1197,7 +1220,7 @@
 
     @pl.loop(0, blocks)
     def _(b):
-        tick(first_tick + b)
+        tick_at(pairs, b)
         at = pl.ds(pl.multiple_of(b * 256, 256), 256)
         d_norm = mm(dqkv[0, at, :], wq[0], NT)
         for g in range(1, pairs // 2):
@@ -1223,18 +1246,26 @@
     small_copy(0).start()
     at_tick = first_tick + blocks
     for i in range(len(others)):
-        tick(at_tick + i)
+        tick((at_tick + i) // 4, (at_tick + i) % 4)
         small_copy(i).wait_recv()
         small_acc[i + 1] = small_acc[i] + small_recv[i]
         if i + 1 < len(others):
             small_copy(i + 1).start()
     small_out[...] = small_acc[len(others)]
     at_tick = at_tick + len(others)
-    last = max(last_tick(lags, TURNS), last_tick(late_lags, LATE_TURNS), last_tick(half_lags, HALF_TURNS))
-
-    @pl.loop(at_tick, last)
-    def _(t):
-        tick(t)
+    while at_tick % 4:
+        tick(at_tick // 4, at_tick % 4)
+        at_tick += 1
+    last = max(
+        last_tick(0, 2, len(ORDER), lags),
+        last_tick(LATE_START, 2, len(EARLY), late_lags),
+        last_tick(HALF_START, 4, len(HALF), half_lags),
+    )
+
+    @pl.loop(at_tick // 4, -(-last // 4))
+    def _(turn):
+        for r in range(4):
+            tick(turn, r)
 
     red.finish()
     late.finish()
@@ -1288,7 +1319,7 @@
             pltpu.VMEM((64, count), BF),
             pltpu.VMEM((64, 128), F32),
             pltpu.VMEM((width // 128, 2, 128), F32),
-            pltpu.VMEM((2, 2, 2, 2, 2, 2, 48, 384), BF),
+            pltpu.VMEM((1, 2, 2, 2, 2, 2, 48, 384), BF),
             pltpu.VMEM((q, 2, 2, 2, 2, 48, 384), BF),
             pltpu.VMEM((n, 2, 2, 2, 2, 48, 384), BF),
             pltpu.VMEM((n, 2, 2, 2, 2, 48, 384), BF),
@@ -1384,12 +1415,14 @@
         copy.start()
         pending.append(copy)
 
-    for h in range(m // 2):
-        for i in (2 * h, 2 * h + 1):
-            loads[i].wait()
+    spare = [kind for kind, _ in ORDER].index("g")
+    for h in range(2):
+        loads[2 * h].wait()
+        loads[2 * h + 1 if h == 0 else m + spare].wait()
         sides = []
         for c in range(2):
-            rows = [late[2 * h + i, c, r // 2, r % 2].astype(F32) for i in range(2) for r in range(4)]
+            both = [late.at[2 * h], late.at[2 * h + 1] if h == 0 else total.at[spare]]
+            rows = [one[c, r // 2, r % 2].astype(F32) for one in both for r in range(4)]
             sides.append(jnp.concatenate(rows, axis=0).T)
         for c in range(2):
             wdown[384 * c : 384 * c + 384, 384 * h : 384 * h + 384] = sides[c]
@@ -1398,6 +1431,8 @@
         loads[m + n + 1 + i].wait()
         leave(mid, dst)
     for i, (kind, j) in enumerate(ORDER):
+        if i == spare:
+            continue
         loads[m + i].wait()
         for c in range(2):
             for r in range(4):
@@ -1418,7 +1453,7 @@
         for r in range(4):
             value = last[i, r // 2, r % 2].astype(F32)
             for part in range(3):
-                start = 768 * part + 128 * (4 + i)
+                start = 768 * part + 128 * (2 + i)
                 wqkv[48 * r : 48 * r + 48, start : start + 128] = value[:, 128 * part : 128 * part + 128]
     leave(wqkv, wqkv_h)
 

time: 258 us -> 248 us (0.961)
  Pallas kernels: 256 us -> 247 us
    pallas_call x1, Pallas kernels: 68.4 us -> 62.2 us  [middle_call(): pl.pallas_call(functools.partial(middle_kernel, ndp), out_shape=[jax.Shap...]
    pallas_call x1, Pallas kernels: 116 us -> 113 us  [backward_call(): pl.pallas_call(functools.partial(backward_kernel, ndp), out_shape=[jax.Sh...]
where the time goes in v4:
time: 248 us; the launch traced here: 247 us
  Pallas kernels  247 us (100%)
    pallas_call x1, Pallas kernels, backward_call(): pl.pallas_call(functools.partial(backward_kernel, ndp), out_shape=[jax.Sh...  113 us
    pallas_call x1, Pallas kernels, forward_call(): pl.pallas_call(functools.partial(forward_kernel, ndp), out_shape=[jax.Sha...  63.4 us
    pallas_call x1, Pallas kernels, middle_call(): pl.pallas_call(functools.partial(middle_kernel, ndp), out_shape=[jax.Shap...  62.2 us
    pallas_call x1, Pallas kernels, finish_call(): pl.pallas_call(finish_kernel, out_shape=[jax.ShapeDtypeStruct(layer.shape...  8.41 us

profile of v4, /device:TPU:0, one launch (start us, length us, event | category | flops | bytes accessed | tf_op | source)
XLA Modules:
  0.0 247.5 jit_solution(700326782245351892)
XLA Ops:
  0.7 63.4 %forward.1 = (bf16[768,1024]{1,0:T(8,128)(2,1)}, bf16[18,1024,128]{2,1,0:T(8,128)(2,1)}, bf16[1024,768]{1,0:T(8,128)(2,1)}, bf16[1024,128]{1,0:T(8,128)(2,1)}, b...) custom-call(s32[8,128]{1,0:T(8,128)} %bitcast.11, ...), custom_call_target="tpu_custom_call" | custom-call | tf_op jit(solution)/shard_map/forward/pallas_call | solution.py:592
  64.1 62.2 %middle.1 = (bf16[1024,768]{1,0:T(8,128)(2,1)}, f32[1024,768]{1,0:T(8,128)}, bf16[1024,768]{1,0:T(8,128)(2,1)}, bf16[1024,128]{1,0:T(8,128)(2,1)}, bf16[6,2,2,2,...) custom-call(bf16[1024,768]{1,0:T(8,128)(2,1)} %tok_h.5, ...), custom_call_target="tpu_custom_call" | custom-call | tf_op jit(solution)/shard_map/middle/pallas_call | solution.py:895
  126.3 112.6 %backward.1 = (bf16[1024,768]{1,0:T(8,128)(2,1)}, bf16[7,2,2,2,48,384]{5,4,3,2,1,0:T(8,128)(2,1)}, bf16[3,2,2,2,48,384]{5,4,3,2,1,0:T(8,128)(2,1)}, bf16[4,2,2,48,384]{4,3,2,1,0:T(8,128)(2,1)}, f32[24,768]{1,0:T(8,128)}) custom-call(s32[8,128]{1,0:T(8,128)} %bitcast.12, s32[8,128]{1,0:T(8,128)} %bitcast.14, s32[8,128]{1,0:T(8,128)} %bitcast.16, ...), custom_call_target="tpu_custom_call" | custom-call | tf_op jit(solution)/shard_map/backward/pallas_call | solution.py:1289
  238.9 8.4 %finish.1 = (bf16[1024,768]{1,0:T(8,128)(2,1)}, bf16[1024,768]{1,0:T(8,128)(2,1)}, f32[192,2304]{1,0:T(8,128)}, f32[3,2,63]{2,1,0:T(2,128)}, f32[192,768]{1,0:T(...) custom-call(bf16[7,2,2,2,48,384]{5,4,3,2,1,0:T(8,128)(2,1)} %get-tup, ...), custom_call_target="tpu_custom_call" | custom-call | tf_op jit(solution)/shard_map/finish/pallas_call | solution.py:1492

commit v5 on v4

--- a/solution.py
+++ b/solution.py
@@ -901,7 +901,7 @@
             jax.ShapeDtypeStruct((count, 128), BF),
             jax.ShapeDtypeStruct((6, 2, 2, 2, 2, 2, 48, 384), BF),
             jax.ShapeDtypeStruct((n, 2, 2, 48, 384), BF),
-            jax.ShapeDtypeStruct((24, width), F32),
+            jax.ShapeDtypeStruct((16, width), F32),
         ],
         in_specs=[ANY] * 4 + [VMEM] + [ANY] * 3,
         out_specs=[ANY] * 6 + [VMEM],
@@ -1210,7 +1210,9 @@
                     own_half[at] = value[192 * f + 48 * r : 192 * f + 48 * r + 48, :]
 
     for p in range(pairs):
-        small_acc[0, 12 + 2 * p : 14 + 2 * p, 0:128] = dtab[p]
+        for axis in range(2):
+            i = 2 * p + axis
+            small_acc[0, 12 + i // 6 : 13 + i // 6, 128 * (i % 6) : 128 * (i % 6) + 128] = dtab[p, axis : axis + 1, :]
 
     def gtok_out(b):
         at = pl.ds(pl.multiple_of(b * 256, 256), 256)
@@ -1426,10 +1428,11 @@
             sides.append(jnp.concatenate(rows, axis=0).T)
         for c in range(2):
             wdown[384 * c : 384 * c + 384, 384 * h : 384 * h + 384] = sides[c]
+        if h == 0:
+            for i, (_, mid, dst) in enumerate(through):
+                loads[m + n + 1 + i].wait()
+                leave(mid, dst)
     leave(wdown, wdown_h)
-    for i, (_, mid, dst) in enumerate(through):
-        loads[m + n + 1 + i].wait()
-        leave(mid, dst)
     for i, (kind, j) in enumerate(ORDER):
         if i == spare:
             continue
@@ -1476,8 +1479,9 @@
             value = jnp.zeros((1, offsets), F32)
             for k in range(4):
                 head = rel.shape[0] * k + i
-                start = 64 * (1 - head % 2)
-                at = 12 + 2 * (head // 2) + axis
+                line = 2 * (head // 2) + axis
+                start = 128 * (line % 6) + 64 * (1 - head % 2)
+                at = 12 + line // 6
                 value = jnp.where(f == k, small[at : at + 1, start : start + offsets], value)
             rel[i, axis : axis + 1, :] = value
     for copy in pending:

time: 248 us -> 245 us (0.988)
  Pallas kernels: 247 us -> 244 us
where the time goes in v5:
time: 245 us
  Pallas kernels  244 us (100%)
    pallas_call x1, Pallas kernels, backward_call(): pl.pallas_call(functools.partial(backward_kernel, ndp), out_shape=[jax.Sh...  110 us
    pallas_call x1, Pallas kernels, forward_call(): pl.pallas_call(functools.partial(forward_kernel, ndp), out_shape=[jax.Sha...  63.4 us
    pallas_call x1, Pallas kernels, middle_call(): pl.pallas_call(functools.partial(middle_kernel, ndp), out_shape=[jax.Shap...  62.2 us
    pallas_call x1, Pallas kernels, finish_call(): pl.pallas_call(finish_kernel, out_shape=[jax.ShapeDtypeStruct(layer.shape...  7.97 us

profile of v5, /device:TPU:0, one launch (start us, length us, event | category | flops | bytes accessed | tf_op | source)
XLA Modules:
  0.0 244.8 jit_solution(11314609852201395876)
XLA Ops:
  0.7 63.4 %forward.1 = (bf16[768,1024]{1,0:T(8,128)(2,1)}, bf16[18,1024,128]{2,1,0:T(8,128)(2,1)}, bf16[1024,768]{1,0:T(8,128)(2,1)}, bf16[1024,128]{1,0:T(8,128)(2,1)}, b...) custom-call(s32[8,128]{1,0:T(8,128)} %bitcast.11, ...), custom_call_target="tpu_custom_call" | custom-call | tf_op jit(solution)/shard_map/forward/pallas_call | solution.py:592
  64.1 62.2 %middle.1 = (bf16[1024,768]{1,0:T(8,128)(2,1)}, f32[1024,768]{1,0:T(8,128)}, bf16[1024,768]{1,0:T(8,128)(2,1)}, bf16[1024,128]{1,0:T(8,128)(2,1)}, bf16[6,2,2,2,...) custom-call(bf16[1024,768]{1,0:T(8,128)(2,1)} %tok_h.5, ...), custom_call_target="tpu_custom_call" | custom-call | tf_op jit(solution)/shard_map/middle/pallas_call | solution.py:895
  126.3 110.4 %backward.1 = (bf16[1024,768]{1,0:T(8,128)(2,1)}, bf16[7,2,2,2,48,384]{5,4,3,2,1,0:T(8,128)(2,1)}, bf16[3,2,2,2,48,384]{5,4,3,2,1,0:T(8,128)(2,1)}, bf16[4,2,2,48,384]{4,3,2,1,0:T(8,128)(2,1)}, f32[16,768]{1,0:T(8,128)}) custom-call(s32[8,128]{1,0:T(8,128)} %bitcast.12, s32[8,128]{1,0:T(8,128)} %bitcast.14, s32[8,128]{1,0:T(8,128)} %bitcast.16, ...), custom_call_target="tpu_custom_call" | custom-call | tf_op jit(solution)/shard_map/backward/pallas_call | solution.py:1291
  236.7 8.0 %finish.1 = (bf16[1024,768]{1,0:T(8,128)(2,1)}, bf16[1024,768]{1,0:T(8,128)(2,1)}, f32[192,2304]{1,0:T(8,128)}, f32[3,2,63]{2,1,0:T(2,128)}, f32[192,768]{1,0:T(...) custom-call(bf16[7,2,2,2,48,384]{5,4,3,2,1,0:T(8,128)(2,1)} %get-tup, ...), custom_call_target="tpu_custom_call" | custom-call | tf_op jit(solution)/shard_map/finish/pallas_call | solution.py:1496
